TPU v7x, 32 devices: a whole 2x2x4 slice. The times are simulated.
32 devices in a mesh: dp: 8 (over z, x), ctx: 4 (over y, core).
Axes of the slice: x: 2, y: 2, z: 4, core: 2. Of those that a mesh axis runs over, the one named last changes fastest.
Arguments:
- layer_input: bfloat16 [16, 1024, 2048], P('dp', 'ctx'), may hold values from -6 to 6
- lengths: int32 [16], P('dp'), may hold values from 256 to 1024, as said below
- attn_gain: float32 [2048], replicated, may hold values from 0.5 to 1.5
- w_query: bfloat16 [2048, 1280], P('dp', 'ctx'), may hold values from -0.125 to 0.125
- w_key: bfloat16 [2048, 320], P('dp', 'ctx'), may hold values from -0.125 to 0.125
- w_value: bfloat16 [2048, 320], P('dp', 'ctx'), may hold values from -0.125 to 0.125
- query_gain: float32 [64], replicated, may hold values from 0.1 to 1.9
- key_gain: float32 [64], replicated, may hold values from 0.1 to 1.9
- w_out: bfloat16 [2048, 1280], P('dp', 'ctx'), may hold values from -3 to 3
- ffn_gain: float32 [2048], replicated, may hold values from 0.5 to 1.5
- w_gate: bfloat16 [2048, 5120], P('dp', 'ctx'), may hold values from -0.125 to 0.125
- w_up: bfloat16 [2048, 5120], P('dp', 'ctx'), may hold values from -0.125 to 0.125
- w_down: bfloat16 [2048, 5120], P('dp', 'ctx'), may hold values from -0.078125 to 0.078125
- cotangent: bfloat16 [16, 1024, 2048], P('dp', 'ctx'), may hold values from -6 to 6
Outputs:
- layer_output: bfloat16 [16, 1024, 2048], P('dp', 'ctx')
- input_grad: bfloat16 [16, 1024, 2048], P('dp', 'ctx')
- attn_gain_grad: float32 [2048], replicated
- w_query_grad: float32 [2048, 1280], P('dp', 'ctx')
- w_key_grad: float32 [2048, 320], P('dp', 'ctx')
- w_value_grad: float32 [2048, 320], P('dp', 'ctx')
- query_gain_grad: float32 [64], replicated
- key_gain_grad: float32 [64], replicated
- w_out_grad: float32 [2048, 1280], P('dp', 'ctx')
- ffn_gain_grad: float32 [2048], replicated
- w_gate_grad: float32 [2048, 5120], P('dp', 'ctx')
- w_up_grad: float32 [2048, 5120], P('dp', 'ctx')
- w_down_grad: float32 [2048, 5120], P('dp', 'ctx')
Inputs may be any that keep to these rules, and one draw needn't show every extreme that they name: `lengths`: some row has all 1024 slots valid.
All inputs are finite; a program needn't handle non-finite values.
Results may differ from a plain program's by a relative error of at most 0.02.
Values may be sent and summed in bfloat16 or wider, within the bound.
A program may use at most 384 MiB of HBM per device.

v0:
```python
import math

import jax
import jax.numpy as jnp
from jax import lax
from jax.sharding import PartitionSpec as P

D = 2048
HQ = 20
KVH = 5
HD = 64
SLOTS = 1024


EPSILON = 1e-06
ROPE_BASE = 10000.0


def norm_rows(values, gain_vec):
    scale_inv = lax.rsqrt(jnp.mean(values * values, -1, keepdims=True) + EPSILON)
    unit_rows = values * scale_inv
    return (unit_rows * gain_vec, unit_rows, scale_inv)


def norm_back(grad_unit, unit_rows, scale_inv):
    return scale_inv * (grad_unit - unit_rows * jnp.mean(grad_unit * unit_rows, -1, keepdims=True))


def rope_tables(positions, head_size):
    steps_half = jnp.arange(head_size // 2, dtype=jnp.float32)
    inverse = jnp.exp(steps_half * (-2.0 * math.log(ROPE_BASE) / head_size))
    angles = positions.astype(jnp.float32)[:, None] * inverse[None, :]
    cosine_table = jnp.concatenate([jnp.cos(angles), jnp.cos(angles)], -1)[:, None, :]
    sine_table = jnp.concatenate([jnp.sin(angles), jnp.sin(angles)], -1)[:, None, :]
    return (cosine_table, sine_table)


def rotate(values, cosine_table, sine_table):
    half_size = values.shape[-1] // 2
    turned = jnp.concatenate([-values[..., half_size:], values[..., :half_size]], -1)
    return values * cosine_table + turned * sine_table


def rotate_back(incoming, cosine_table, sine_table):
    half_size = incoming.shape[-1] // 2
    turned = incoming * sine_table
    return incoming * cosine_table + jnp.concatenate(
        [turned[..., half_size:], -turned[..., :half_size]], -1
    )


def contract_last(left_side, right_side):
    return lax.dot_general(
        left_side, right_side, (((1,), (1,)), ((), ())), preferred_element_type=jnp.float32
    )


def contract_rows(left_side, right_side):
    return lax.dot_general(
        left_side, right_side, (((0,), (0,)), ((), ())), preferred_element_type=jnp.float32
    )


def masked_scores(grouped, kv_block, allowed, kv_width, scaling):
    key_rows = kv_block[:, :kv_width].reshape(kv_block.shape[0], KVH, HD)
    raw_scores = (
        jnp.einsum("skgh,tkh->kgst", grouped, key_rows, preferred_element_type=jnp.float32)
        * scaling
    )
    return jnp.where(allowed, raw_scores, -1e30)


def per_device(
    layer_input,
    lengths,
    attn_gain,
    w_query,
    w_key,
    w_value,
    query_gain,
    key_gain,
    w_out,
    ffn_gain,
    w_gate,
    w_up,
    w_down,
    cotangent,
):
    micro_count = layer_input.shape[0]
    seq_len = layer_input.shape[1]
    group_size = HQ // KVH
    kv_width = KVH * HD
    q_width = HQ * HD
    scaling = 1.0 / math.sqrt(HD)
    positions = lax.axis_index("ctx") * seq_len + jnp.arange(seq_len, dtype=jnp.int32)
    key_slots = jnp.arange(SLOTS, dtype=jnp.int32)
    cosine_table, sine_table = rope_tables(positions, HD)
    causal = key_slots[None, :] <= positions[:, None]
    grad_attn_gain = jnp.zeros((D,), jnp.float32)
    grad_ffn_gain = jnp.zeros((D,), jnp.float32)
    grad_query_gain = jnp.zeros((HD,), jnp.float32)
    grad_key_gain = jnp.zeros((HD,), jnp.float32)
    stored = {
        "normed": [],
        "query": [],
        "key": [],
        "value": [],
        "mixed": [],
        "attn": [],
        "normed_two": [],
        "gate": [],
        "upper": [],
        "hidden": [],
        "branch": [],
    }
    out_rows = []
    input_grads = []
    columns = (
        lax.all_gather(w_query, "ctx", axis=1, tiled=True),
        lax.all_gather(w_key, "ctx", axis=1, tiled=True),
        lax.all_gather(w_value, "ctx", axis=1, tiled=True),
        lax.all_gather(w_out, "ctx", axis=1, tiled=True),
        lax.all_gather(w_gate, "ctx", axis=1, tiled=True),
        lax.all_gather(w_up, "ctx", axis=1, tiled=True),
        lax.all_gather(w_down, "ctx", axis=1, tiled=True),
    )
    gathered = (
        lax.all_gather(columns[0], "dp", axis=0, tiled=True),
        lax.all_gather(columns[1], "dp", axis=0, tiled=True),
        lax.all_gather(columns[2], "dp", axis=0, tiled=True),
        lax.all_gather(columns[3], "dp", axis=0, tiled=True),
        lax.all_gather(columns[4], "dp", axis=0, tiled=True),
        lax.all_gather(columns[5], "dp", axis=0, tiled=True),
        lax.all_gather(columns[6], "dp", axis=0, tiled=True),
    )
    for batch_index in range(micro_count):
        row_length = lengths[batch_index]
        mat_query, mat_key, mat_value, mat_out, mat_gate, mat_up, mat_down = gathered
        valid_mask = (positions < row_length).astype(jnp.float32)[:, None]
        allowed = causal & (key_slots < row_length)[None, :]
        row_input = layer_input[batch_index].astype(jnp.float32)
        normed_one, unit_one, inv_one = norm_rows(row_input, attn_gain)
        normed_bf = normed_one.astype(jnp.bfloat16)
        query_lin = jnp.dot(normed_bf, mat_query, preferred_element_type=jnp.float32)
        key_lin = jnp.dot(normed_bf, mat_key, preferred_element_type=jnp.float32)
        value_lin = jnp.dot(normed_bf, mat_value, preferred_element_type=jnp.float32)
        query_norm, query_unit, query_inv = norm_rows(
            query_lin.reshape(seq_len, HQ, HD), query_gain
        )
        key_norm, key_unit, key_inv = norm_rows(key_lin.reshape(seq_len, KVH, HD), key_gain)
        query_bf = rotate(query_norm, cosine_table, sine_table).astype(jnp.bfloat16)
        grouped = query_bf.reshape(seq_len, KVH, group_size, HD)
        key_bf = rotate(key_norm, cosine_table, sine_table).astype(jnp.bfloat16)
        value_bf = value_lin.astype(jnp.bfloat16)
        kv_local = jnp.concatenate([key_bf.reshape(seq_len, kv_width), value_bf], -1)
        kv_whole = lax.all_gather(kv_local, "ctx", axis=0, tiled=True)
        scores = masked_scores(grouped, kv_whole, allowed, kv_width, scaling)
        largest = jnp.max(scores, -1, keepdims=True)
        log_total = largest + jnp.log(jnp.sum(jnp.exp(scores - largest), -1, keepdims=True))
        probs_bf = jnp.exp(scores - log_total).astype(jnp.bfloat16)
        values_all = kv_whole[:, kv_width:].reshape(SLOTS, KVH, HD)
        mixed_bf = (
            jnp.einsum("kgst,tkh->skgh", probs_bf, values_all, preferred_element_type=jnp.float32)
            .reshape(seq_len, q_width)
            .astype(jnp.bfloat16)
        )
        middle = row_input + contract_last(mixed_bf, mat_out)
        normed_two, unit_two, inv_two = norm_rows(middle, ffn_gain)
        normed_two_bf = normed_two.astype(jnp.bfloat16)
        gate_lin = jnp.dot(normed_two_bf, mat_gate, preferred_element_type=jnp.float32)
        up_lin = jnp.dot(normed_two_bf, mat_up, preferred_element_type=jnp.float32)
        sigmoid_gate = jax.nn.sigmoid(gate_lin)
        activated = gate_lin * sigmoid_gate
        hidden_bf = (activated * up_lin).astype(jnp.bfloat16)
        branch = contract_last(hidden_bf, mat_down)
        out_rows.append((valid_mask * (middle + branch)).astype(jnp.bfloat16))
        mat_query, mat_key, mat_value, mat_out, mat_gate, mat_up, mat_down = gathered
        row_grad = cotangent[batch_index].astype(jnp.float32) * valid_mask
        branch_grad = row_grad.astype(jnp.bfloat16)
        hidden_grad = jnp.dot(branch_grad, mat_down, preferred_element_type=jnp.float32)
        gate_grad = (
            hidden_grad * up_lin * sigmoid_gate * (1.0 + gate_lin * (1.0 - sigmoid_gate))
        ).astype(jnp.bfloat16)
        up_grad = (hidden_grad * activated).astype(jnp.bfloat16)
        normed_two_grad = contract_last(gate_grad, mat_gate) + contract_last(up_grad, mat_up)
        grad_ffn_gain = grad_ffn_gain + jnp.sum(normed_two_grad * unit_two, 0)
        middle_grad = row_grad + norm_back(normed_two_grad * ffn_gain, unit_two, inv_two)
        attn_grad = middle_grad.astype(jnp.bfloat16)
        mixed_grad = (
            jnp.dot(attn_grad, mat_out, preferred_element_type=jnp.float32)
            .astype(jnp.bfloat16)
            .reshape(seq_len, KVH, group_size, HD)
        )
        kv_back = lax.all_gather(kv_local, "ctx", axis=0, tiled=True)
        scores = masked_scores(grouped, kv_back, allowed, kv_width, scaling)
        probs = jnp.exp(scores - log_total)
        keys_back = kv_back[:, :kv_width].reshape(SLOTS, KVH, HD)
        values_back = kv_back[:, kv_width:].reshape(SLOTS, KVH, HD)
        prob_grad = jnp.einsum(
            "skgh,tkh->kgst", mixed_grad, values_back, preferred_element_type=jnp.float32
        )
        score_grad = (probs * (prob_grad - jnp.sum(probs * prob_grad, -1, keepdims=True))).astype(
            jnp.bfloat16
        )
        query_rot_grad = (
            jnp.einsum(
                "kgst,tkh->skgh", score_grad, keys_back, preferred_element_type=jnp.float32
            ).reshape(seq_len, HQ, HD)
            * scaling
        )
        key_grad_all = (
            jnp.einsum("kgst,skgh->tkh", score_grad, grouped, preferred_element_type=jnp.float32)
            * scaling
        )
        value_grad_all = jnp.einsum(
            "kgst,skgh->tkh",
            probs.astype(jnp.bfloat16),
            mixed_grad,
            preferred_element_type=jnp.float32,
        )
        kv_grad_whole = jnp.concatenate(
            [key_grad_all.reshape(SLOTS, kv_width), value_grad_all.reshape(SLOTS, kv_width)], -1
        )
        kv_grad_local = lax.psum_scatter(
            kv_grad_whole.astype(jnp.bfloat16), "ctx", scatter_dimension=0, tiled=True
        ).astype(jnp.float32)
        key_rot_grad = kv_grad_local[:, :kv_width].reshape(seq_len, KVH, HD)
        value_grad = kv_grad_local[:, kv_width:].astype(jnp.bfloat16)
        query_norm_grad = rotate_back(query_rot_grad, cosine_table, sine_table)
        grad_query_gain = grad_query_gain + jnp.sum(query_norm_grad * query_unit, (0, 1))
        query_grad = (
            norm_back(query_norm_grad * query_gain, query_unit, query_inv)
            .reshape(seq_len, q_width)
            .astype(jnp.bfloat16)
        )
        key_norm_grad = rotate_back(key_rot_grad, cosine_table, sine_table)
        grad_key_gain = grad_key_gain + jnp.sum(key_norm_grad * key_unit, (0, 1))
        key_grad = (
            norm_back(key_norm_grad * key_gain, key_unit, key_inv)
            .reshape(seq_len, kv_width)
            .astype(jnp.bfloat16)
        )
        normed_grad = (
            contract_last(query_grad, mat_query)
            + contract_last(key_grad, mat_key)
            + contract_last(value_grad, mat_value)
        )
        grad_attn_gain = grad_attn_gain + jnp.sum(normed_grad * unit_one, 0)
        input_grads.append(
            (middle_grad + norm_back(normed_grad * attn_gain, unit_one, inv_one)).astype(
                jnp.bfloat16
            )
        )
        stored["normed"].append(normed_bf)
        stored["query"].append(query_grad)
        stored["key"].append(key_grad)
        stored["value"].append(value_grad)
        stored["mixed"].append(mixed_bf)
        stored["attn"].append(attn_grad)
        stored["normed_two"].append(normed_two_bf)
        stored["gate"].append(gate_grad)
        stored["upper"].append(up_grad)
        stored["hidden"].append(hidden_bf)
        stored["branch"].append(branch_grad)
    joined = {name_key: jnp.concatenate(stored[name_key], 0) for name_key in stored}
    right_parts = (
        lax.all_to_all(joined["query"], "ctx", split_axis=1, concat_axis=0, tiled=True),
        lax.all_to_all(joined["key"], "ctx", split_axis=1, concat_axis=0, tiled=True),
        lax.all_to_all(joined["value"], "ctx", split_axis=1, concat_axis=0, tiled=True),
        lax.all_to_all(joined["mixed"], "ctx", split_axis=1, concat_axis=0, tiled=True),
        lax.all_to_all(joined["gate"], "ctx", split_axis=1, concat_axis=0, tiled=True),
        lax.all_to_all(joined["upper"], "ctx", split_axis=1, concat_axis=0, tiled=True),
        lax.all_to_all(joined["hidden"], "ctx", split_axis=1, concat_axis=0, tiled=True),
    )
    left_parts = (
        lax.all_gather(joined["normed"], "ctx", axis=0, tiled=True),
        lax.all_gather(joined["attn"], "ctx", axis=0, tiled=True),
        lax.all_gather(joined["normed_two"], "ctx", axis=0, tiled=True),
        lax.all_gather(joined["branch"], "ctx", axis=0, tiled=True),
    )
    widths = [part.shape[1] for part in right_parts]
    normed_cut = left_parts[0]
    attn_cut = left_parts[1]
    normed_two_cut = left_parts[2]
    branch_cut = left_parts[3]
    block_sums = lax.psum_scatter(
        jnp.concatenate(
            [
                contract_rows(normed_cut, right_parts[0]),
                contract_rows(normed_cut, right_parts[1]),
                contract_rows(normed_cut, right_parts[2]),
                contract_rows(attn_cut, right_parts[3]),
                contract_rows(normed_two_cut, right_parts[4]),
                contract_rows(normed_two_cut, right_parts[5]),
                contract_rows(branch_cut, right_parts[6]),
            ],
            1,
        ).astype(jnp.bfloat16),
        "dp",
        scatter_dimension=0,
        tiled=True,
    ).astype(jnp.float32)
    owned = []
    offset = 0
    for width_now in widths:
        owned.append(block_sums[:, offset : offset + width_now])
        offset = offset + width_now
    gain_totals = lax.psum(
        (grad_attn_gain, grad_query_gain, grad_key_gain, grad_ffn_gain), ("dp", "ctx")
    )
    return (
        jnp.stack(out_rows, 0),
        jnp.stack(input_grads, 0),
        gain_totals[0],
        owned[0],
        owned[1],
        owned[2],
        gain_totals[1],
        gain_totals[2],
        owned[3],
        gain_totals[3],
        owned[4],
        owned[5],
        owned[6],
    )


def solution(mesh):
    in_specs = (
        P("dp", "ctx", None),
        P("dp"),
        P(),
        P("dp", "ctx"),
        P("dp", "ctx"),
        P("dp", "ctx"),
        P(),
        P(),
        P("dp", "ctx"),
        P(),
        P("dp", "ctx"),
        P("dp", "ctx"),
        P("dp", "ctx"),
        P("dp", "ctx", None),
    )
    out_specs = (
        P("dp", "ctx", None),
        P("dp", "ctx", None),
        P(),
        P("dp", "ctx"),
        P("dp", "ctx"),
        P("dp", "ctx"),
        P(),
        P(),
        P("dp", "ctx"),
        P(),
        P("dp", "ctx"),
        P("dp", "ctx"),
        P("dp", "ctx"),
    )
    return jax.shard_map(
        per_device, mesh=mesh, in_specs=in_specs, out_specs=out_specs, check_vma=False
    )
```

profile of v0, /device:TPU:0, one launch (start us, length us, event | category | flops | bytes accessed | tf_op | source)
XLA Modules:
  0.0 2606.6 jit_solution(15764828685533548878)
XLA Ops:
  27.6 31.1 %all-gather.17.cloned.1.call-done = bf16[2048,320]{0,1:T(8,128)(2,1)} async-done(((bf16[256,320]{0,1:T(8,128)(2,1)}), bf16[2048,320]{0,1:T(8,128)(2,1)}) %all-gather.17.cloned.1.call-update) | async-done | bytes 1310736 | tf_op jit(solution)/shard_map/all_gather | solution.py:129
  63.0 38.7 %all-gather.19.cloned.1.call-done = bf16[2048,320]{0,1:T(8,128)(2,1)} async-done(((bf16[256,320]{0,1:T(8,128)(2,1)}), bf16[2048,320]{0,1:T(8,128)(2,1)}) %all-gather.19.cloned.1.call-update) | async-done | bytes 1310736 | tf_op jit(solution)/shard_map/all_gather | solution.py:130
  119.1 12.3 all_gather.69
  133.6 25.2 all-gather.31.cloned.1.call-done
  158.9 26.9 %all-gather.35.cloned.1.call-done = bf16[256,5120]{1,0:T(8,128)(2,1)} async-done(((bf16[256,1280]{1,0:T(8,128)(2,1)}), bf16[256,5120]{1,0:T(8,128)(2,1)}) %all-gather.35.cloned.1.call-update) | async-done | bytes 2621456 | tf_op jit(solution)/shard_map/all_gather | solution.py:125
  208.7 18.0 all-gather.39.cloned.1.call-done
  229.1 86.9 %all-gather.23.cloned.1.call-done = bf16[2048,1280]{0,1:T(8,128)(2,1)} async-done(((bf16[256,1280]{0,1:T(8,128)(2,1)}), bf16[2048,1280]{0,1:T(8,128)(2,1)}) %all-gather.23.cloned.1.call-update) | async-done | bytes 5242896 | tf_op jit(solution)/shard_map/all_gather | solution.py:128
  341.8 61.6 %all-gather.25.cloned.1.call-done = bf16[2048,1280]{0,1:T(8,128)(2,1)} async-done(((bf16[256,1280]{0,1:T(8,128)(2,1)}), bf16[2048,1280]{0,1:T(8,128)(2,1)}) %all-gather.25.cloned.1.call-update) | async-done | bytes 5242896 | tf_op jit(solution)/shard_map/all_gather | solution.py:131
  432.4 372.4 %all-gather.29.cloned.1.call-done = bf16[2048,5120]{1,0:T(8,128)(2,1)} async-done(((bf16[256,5120]{1,0:T(8,128)(2,1)}), bf16[2048,5120]{1,0:T(8,128)(2,1)}) %all-gather.29.cloned.1.call-update) | async-done | bytes 20971536 | tf_op jit(solution)/shard_map/all_gather | solution.py:132
  817.0 391.2 %all-gather.33.cloned.1.call-done = bf16[2048,5120]{1,0:T(8,128)(2,1)} async-done(((bf16[256,5120]{1,0:T(8,128)(2,1)}), bf16[2048,5120]{1,0:T(8,128)(2,1)}) %all-gather.33.cloned.1.call-update) | async-done | bytes 20971536 | tf_op jit(solution)/shard_map/all_gather | solution.py:133
  1208.1 12.4 fusion.125
  1220.5 390.8 %all-gather.37.cloned.1.call-done = bf16[2048,5120]{1,0:T(8,128)(2,1)} async-done(((bf16[256,5120]{1,0:T(8,128)(2,1)}), bf16[2048,5120]{1,0:T(8,128)(2,1)}) %all-gather.37.cloned.1.call-update) | async-done | bytes 20971536 | tf_op jit(solution)/shard_map/all_gather | solution.py:134
  1611.3 15.4 multiply_convert_fusion.2
  1639.0 13.8 multiply_reduce_fusion.1
  1652.8 12.6 fusion.127
  1677.6 18.6 multiply_convert_fusion
  1708.5 14.2 multiply_reduce_fusion
  1742.3 14.0 fusion.3
  1756.4 14.6 fusion.5
  1782.9 14.4 fusion
  1797.2 14.5 fusion.2
  1875.8 23.8 all-to-all-done
  1942.9 92.3 %all-to-all-done.4 = bf16[512,4,1280]{2,0,1:T(8,128)(2,1)} async-done(((bf16[512,4,1280]{2,0,1:T(8,128)(2,1)}), bf16[512,4,1280]{2,0,1:T(8,128)(2,1)}, u32[]{:S(2)}, u32[]{:S(2)}) %all-to-all-start.4) | async-done | bytes 5242912 | tf_op jit(solution)/shard_map/all_to_all | solution.py:271
  2068.9 74.9 %all-to-all-done.5 = bf16[512,4,1280]{2,0,1:T(8,128)(2,1)} async-done(((bf16[512,4,1280]{2,0,1:T(8,128)(2,1)}), bf16[512,4,1280]{2,0,1:T(8,128)(2,1)}, u32[]{:S(2)}, u32[]{:S(2)}) %all-to-all-start.5) | async-done | bytes 5242912 | tf_op jit(solution)/shard_map/all_to_all | solution.py:272
  2148.9 16.9 fusion.12
  2165.8 15.2 fusion.11
  2181.1 70.0 %all-gather.47.cloned.1.call-done = bf16[2048,2048]{1,0:T(8,128)(2,1)} async-done(((bf16[512,2048]{1,0:T(8,128)(2,1)}), bf16[2048,2048]{1,0:T(8,128)(2,1)}) %all-gather.47.cloned.1.call-update) | async-done | bytes 8388624 | tf_op jit(solution)/shard_map/all_gather | solution.py:279
  2253.3 16.8 fusion.10
  2271.7 12.4 fusion.36
  2284.1 12.5 fusion.35
  2309.8 44.0 %all-reduce = (f32[2048]{0:T(1024)}, f32[64]{0:T(128)}, f32[64]{0:T(128)}, f32[2048]{0:T(1024)}) all-reduce(f32[2048]{0:T(1024)S(1)} %add.241, f32[64]{0:T(128)S(1)} %add.242, f32[64]{0:T(128)S(1)} %add.243, f32[2048]{0:T(1024)S(1)} %add.244), channel_id=1, replica_groups=mesh['dp'=8,'ctx'=4] {'dp','ctx'}, use_global_device_ids=true, to_apply=%region_26.27 | all-reduce | flops 4224 | bytes 33792 | tf_op jit(solution)/shard_map/psum | solution.py:308
  2360.0 227.7 %reduce-scatter.8.cloned.1.call-done = bf16[256,4640]{0,1:T(8,128)(2,1)} async-done(((bf16[2048,4640]{0,1:T(8,128)(2,1)}), bf16[256,4640]{0,1:T(8,128)(2,1)}) %reduce-scatter.8.cloned.1.call-update) | async-done | bytes 2375696 | tf_op jit(solution)/shard_map/reduce_scatter | solution.py:286
  (408 shorter events, 384.6 us)
Async XLA Ops:
  7.2 51.5 %all-gather.17.cloned.1.call-start = ((), (), s32[]{:S(2)}) async-start(), calls=%async_computation.10 | async-start | bytes 1474560 | tf_op jit(solution)/shard_map/all_gather | solution.py:129
  15.9 85.8 %all-gather.19.cloned.1.call-start = ((), (), s32[]{:S(2)}) async-start(), calls=%async_computation.11 | async-start | bytes 1474560 | tf_op jit(solution)/shard_map/all_gather | solution.py:130
  22.2 111.3 %all-gather.27.cloned.1.call-start = ((), (), s32[]{:S(2)}) async-start(), calls=%async_computation.15 | async-start | bytes 3276800 | tf_op jit(solution)/shard_map/all_gather | solution.py:123
  23.0 135.8 %all-gather.31.cloned.1.call-start = ((), (), s32[]{:S(2)}) async-start(), calls=%async_computation.17 | async-start | bytes 3276800 | tf_op jit(solution)/shard_map/all_gather | solution.py:124
  23.5 162.2 %all-gather.35.cloned.1.call-start = ((), (), s32[]{:S(2)}) async-start(), calls=%async_computation.19 | async-start | bytes 3276800 | tf_op jit(solution)/shard_map/all_gather | solution.py:125
  24.1 182.0 %all-gather.21.cloned.1.call-start = ((), (), s32[]{:S(2)}) async-start(), calls=%async_computation.12 | async-start | bytes 1638400 | tf_op jit(solution)/shard_map/all_gather | solution.py:156
  25.1 298.3 %copy-start.51 = (f32[256,64]{0,1:T(8,128)}, f32[256,64]{0,1:T(8,128)S(1)}, u32[]{:S(2)}) copy-start(f32[256,64]{0,1:T(8,128)S(1)} %get-tuple-element.156) | copy-start | bytes 196612
  25.7 297.7 %copy-start.63 = (f32[256,64]{0,1:T(8,128)}, f32[256,64]{0,1:T(8,128)S(1)}, u32[]{:S(2)}) copy-start(f32[256,64]{0,1:T(8,128)S(1)} %get-tuple-element.158) | copy-start | bytes 196612
  26.2 289.7 %copy-start.95 = (f32[256]{0:T(256)}, f32[256]{0:T(256)S(1)}, u32[]{:S(2)}) copy-start(f32[256]{0:T(256)S(1)} %get-tuple-element.195) | copy-start | bytes 3076
  26.2 294.1 %copy-start.97 = (f32[256]{0:T(256)}, f32[256]{0:T(256)S(1)}, u32[]{:S(2)}) copy-start(f32[256]{0:T(256)S(1)} %get-tuple-element.196) | copy-start | bytes 3076
  27.6 74.1 %copy-start.41 = (bf16[256,2048]{1,0:T(8,128)(2,1)}, bf16[256,2048]{1,0:T(8,128)(2,1)S(1)}, u32[]{:S(2)}) copy-start(bf16[256,2048]{1,0:T(8,128)(2,1)S(1)} %get-tuple-element.114) | copy-start | bytes 3145732
  104.4 122.2 %all-gather.39.cloned.1.call-start = ((), (), s32[]{:S(2)}) async-start(), calls=%async_computation.21 | async-start | bytes 1638400 | tf_op jit(solution)/shard_map/all_gather | solution.py:156
  107.4 208.5 %all-gather.23.cloned.1.call-start = ((), (), s32[]{:S(2)}) async-start(), calls=%async_computation.13 | async-start | bytes 5898240 | tf_op jit(solution)/shard_map/all_gather | solution.py:128
  119.0 284.4 %all-gather.25.cloned.1.call-start = ((), (), s32[]{:S(2)}) async-start(), calls=%async_computation.14 | async-start | bytes 5898240 | tf_op jit(solution)/shard_map/all_gather | solution.py:131
  131.5 673.3 %all-gather.29.cloned.1.call-start = ((), (), s32[]{:S(2)}) async-start(), calls=%async_computation.16 | async-start | bytes 23592960 | tf_op jit(solution)/shard_map/all_gather | solution.py:132
  133.6 1074.6 %all-gather.33.cloned.1.call-start = ((), (), s32[]{:S(2)}) async-start(), calls=%async_computation.18 | async-start | bytes 23592960 | tf_op jit(solution)/shard_map/all_gather | solution.py:133
  158.8 1452.5 %all-gather.37.cloned.1.call-start = ((), (), s32[]{:S(2)}) async-start(), calls=%async_computation.20 | async-start | bytes 23592960 | tf_op jit(solution)/shard_map/all_gather | solution.py:134
  185.8 1675.9 %reduce-scatter.4.cloned.1.call-start = ((), (), s32[]{:S(2)}) async-start(), calls=%async_computation.22 | async-start | bytes 1638400 | tf_op jit(solution)/shard_map/reduce_scatter | solution.py:224
  432.4 775.8 %copy-start.39 = (bf16[256,2048]{1,0:T(8,128)(2,1)}, bf16[256,2048]{1,0:T(8,128)(2,1)S(1)}, u32[]{:S(2)}) copy-start(bf16[256,2048]{1,0:T(8,128)(2,1)S(1)} %multiply_convert_fusion.7) | copy-start | bytes 3145732
  1776.1 87.6 %reduce-scatter.6.cloned.1.call-start = ((), (), s32[]{:S(2)}) async-start(), calls=%async_computation.23 | async-start | bytes 1638400 | tf_op jit(solution)/shard_map/reduce_scatter | solution.py:224
  1829.6 218.3 %all-gather.41.cloned.1.call-start = ((), (), s32[]{:S(2)}) async-start(), calls=%async_computation.24 | async-start | bytes 10485760 | tf_op jit(solution)/shard_map/all_gather | solution.py:276
  1832.9 228.5 %all-gather.43.cloned.1.call-start = ((), (), s32[]{:S(2)}) async-start(), calls=%async_computation.25 | async-start | bytes 10485760 | tf_op jit(solution)/shard_map/all_gather | solution.py:277
  1834.5 314.4 %all-gather.45.cloned.1.call-start = ((), (), s32[]{:S(2)}) async-start(), calls=%async_computation.26 | async-start | bytes 10485760 | tf_op jit(solution)/shard_map/all_gather | solution.py:278
  1839.2 28.0 %all-to-all-start.3 = ((bf16[512,4,320]{0,2,1:T(8,128)(2,1)}), bf16[512,4,320]{0,2,1:T(8,128)(2,1)S(1)}, u32[]{:S(2)}, u32[]{:S(2)}) async-start(bf16[512,4,320]{0,2,1:T(8,128)(2,1)} %pad_maximum_fusion.12), calls=%async_computation.5 | async-start | bytes 2621440 | tf_op jit(solution)/shard_map/all_to_all | solution.py:270
  1867.2 32.4 %all-to-all-start = ((bf16[512,4,320]{0,2,1:T(8,128)(2,1)}), bf16[512,4,320]{0,2,1:T(8,128)(2,1)S(1)}, u32[]{:S(2)}, u32[]{:S(2)}) async-start(bf16[512,4,320]{0,2,1:T(8,128)(2,1)} %pad_maximum_fusion.11), calls=%async_computation.2 | async-start | bytes 2621440 | tf_op jit(solution)/shard_map/all_to_all | solution.py:267
  1899.6 14.7 all-to-all-start.2
  1914.3 14.0 all-to-all-start.1
  1929.0 106.1 %all-to-all-start.4 = ((bf16[512,4,1280]{2,0,1:T(8,128)(2,1)}), bf16[512,4,1280]{2,0,1:T(8,128)(2,1)}, u32[]{:S(2)}, u32[]{:S(2)}) async-start(bf16[512,4,1280]{2,0,1:T(8,128)(2,1)} %bitcast.382), calls=%async_computation.6 | async-start | bytes 10485760 | tf_op jit(solution)/shard_map/all_to_all | solution.py:271
  1934.1 317.0 %all-gather.47.cloned.1.call-start = ((), (), s32[]{:S(2)}) async-start(), calls=%async_computation.27 | async-start | bytes 10485760 | tf_op jit(solution)/shard_map/all_gather | solution.py:279
  2035.1 108.7 %all-to-all-start.5 = ((bf16[512,4,1280]{2,0,1:T(8,128)(2,1)}), bf16[512,4,1280]{2,0,1:T(8,128)(2,1)}, u32[]{:S(2)}, u32[]{:S(2)}) async-start(bf16[512,4,1280]{2,0,1:T(8,128)(2,1)} %bitcast.381), calls=%async_computation.7 | async-start | bytes 10485760 | tf_op jit(solution)/shard_map/all_to_all | solution.py:272
  2143.8 109.5 %all-to-all-start.6 = ((bf16[512,4,1280]{2,0,1:T(8,128)(2,1)}), bf16[512,4,1280]{2,0,1:T(8,128)(2,1)}, u32[]{:S(2)}, u32[]{:S(2)}) async-start(bf16[512,4,1280]{2,0,1:T(8,128)(2,1)} %bitcast.380), calls=%async_computation.8 | async-start | bytes 10485760 | tf_op jit(solution)/shard_map/all_to_all | solution.py:273
  2148.9 438.9 %reduce-scatter.8.cloned.1.call-start = ((), (), s32[]{:S(2)}) async-start(), calls=%async_computation.28 | async-start | bytes 21381120 | tf_op jit(solution)/shard_map/reduce_scatter | solution.py:286
  (105 other events, 610.8 us)
Sparse Core Ops, SparseCore 0:
  16.0 42.6 all-gather.16
  60.8 40.9 all-gather.18
  103.3 30.2 all-gather.26
  135.0 23.7 all-gather.30
  160.2 25.5 all-gather.34
  187.8 18.3 all-gather.20
  208.3 18.3 all-gather.38
  228.7 87.1 all-gather.22
  318.0 85.3 all-gather.24
  404.8 399.9 all-gather.28
  806.3 401.7 all-gather.32
  1209.5 401.7 all-gather.36
  1776.2 26.5 reduce-scatter.3
  1829.7 33.8 reduce-scatter.5
  1865.1 79.0 all-gather.40
  1945.6 98.5 all-gather.42
  2045.6 101.1 all-gather.44
  2148.2 102.8 all-gather.46
  2270.2 317.4 reduce-scatter.7
where the time goes:
time: 2610 us
  waiting for transfers between devices  1960 us (75%)
  matrix products  356 us (14%)
  other arithmetic  104 us (4%)
  blocking collectives  82.8 us (3%)
  local copies, waits for them, and re-layouts  53.4 us (2%)
  starting transfers between devices  31.4 us (1%)
    all_gather x1, waiting for transfers between devices, per_device(): lax.all_gather(columns[5], 'dp', axis=0, tiled=True)  391 us
    all_gather x1, waiting for transfers between devices, per_device(): lax.all_gather(columns[6], 'dp', axis=0, tiled=True)  391 us
    all_gather x1, waiting for transfers between devices, per_device(): lax.all_gather(columns[4], 'dp', axis=0, tiled=True)  372 us
    reduce_scatter x1, waiting for transfers between devices, per_device(): lax.psum_scatter(jnp.concatenate([contract_rows(normed_cut, right_parts[0...  228 us
    dot_general x14, matrix products, contract_last(): lax.dot_general(left_side, right_side, (((1,), (1,)), ((), ())), preferre...  97.2 us
    all_to_all x1, waiting for transfers between devices, per_device(): lax.all_to_all(joined['gate'], 'ctx', split_axis=1, concat_axis=0, tiled=...  92.3 us
    all_gather x1, waiting for transfers between devices, per_device(): lax.all_gather(columns[0], 'dp', axis=0, tiled=True)  86.9 us
    all_to_all x1, waiting for transfers between devices, per_device(): lax.all_to_all(joined['upper'], 'ctx', split_axis=1, concat_axis=0, tiled...  74.9 us
  transfers between devices with their start and end apart: 26, of which 22 were waited for; matrix products, arithmetic and copies ran while one was open for 12% of the time, Pallas kernels for 0%

commit v1 on v0

v1 whole, which is shorter than its diff:
```python
import math

import jax
import jax.numpy as jnp
import numpy as np
from jax import lax
from jax.experimental import pallas as pl
from jax.experimental.pallas import tpu as pltpu
from jax.sharding import PartitionSpec as P

HQ = 20
KVH = 5
HD = 64
GROUP = HQ // KVH
QW = HQ * HD
KVW = KVH * HD
GW = GROUP * HD
LANES = 2 * HD
NEG = -1e30
EPSILON = 1e-06
ROPE_BASE = 10000.0
F32 = jnp.float32
BF16 = jnp.bfloat16
VMEM_LIMIT = 60 << 20


def nn(a, b):
    return lax.dot_general(a, b, (((1,), (0,)), ((), ())), preferred_element_type=F32)


def nt(a, b):
    return lax.dot_general(a, b, (((1,), (1,)), ((), ())), preferred_element_type=F32)


def tn(a, b):
    return lax.dot_general(a, b, (((0,), (0,)), ((), ())), preferred_element_type=F32)


def params(limit=VMEM_LIMIT):
    return pltpu.CompilerParams(vmem_limit_bytes=limit)


class Ring:
    def __init__(self, axis, size, direct, late):
        self.axis, self.size, self.direct, self.late = axis, size, direct, late
        combos = [0]
        for bit in direct:
            combos = combos + [c | bit for c in combos]
        self.combos = combos
        masks = list(combos)
        for bit in late:
            masks = masks + [m | bit for m in masks]
        self.masks = masks

    def swap(self, value, mask):
        return lax.ppermute(value, self.axis, [(i, i ^ mask) for i in range(self.size)])

    def gather(self, own):
        held = [own] + [self.swap(own, mask) for mask in self.combos[1:]]
        first = list(held)
        for bit in self.late:
            held = held + [self.swap(piece, bit) for piece in held]
        return held, first

    def scatter_late(self, blocks):
        for bit in reversed(self.late):
            half = len(blocks) // 2
            got = [self.swap(b.astype(BF16), bit) for b in blocks[half:]]
            blocks = [b + g.astype(F32) for b, g in zip(blocks[:half], got)]
        return blocks

    def scatter_direct(self, blocks):
        got = [self.swap(b.astype(BF16), m) for b, m in zip(blocks[1:], self.combos[1:])]
        total = blocks[0]
        for g in got:
            total = total + g.astype(F32)
        return total

    def scatter(self, blocks):
        return self.scatter_direct(self.scatter_late(blocks))


def split_bits(devices, axis_size):
    return [1 << i for i in range(axis_size.bit_length() - 1)]


def rings(mesh):
    grid = mesh.devices
    dp, ctx = mesh.shape["dp"], mesh.shape["ctx"]

    def place(d):
        return tuple(d.coords)

    far, near = [], []
    for bit in split_bits(grid, dp):
        a, b = place(grid[0, 0]), place(grid[bit, 0])
        (far if a[2] != b[2] else near).append(bit)
    outer, core = [], []
    for bit in split_bits(grid, ctx):
        a, b = place(grid[0, 0]), place(grid[0, bit])
        (core if a == b else outer).append(bit)
    return Ring("dp", dp, far, near), Ring("ctx", ctx, outer, core)


def permute_columns(value, index):
    rows, width = value.shape
    count = index.shape[0]
    block = width // count

    def body(index_ref, in_ref, out_ref):
        out_ref[...] = in_ref[...]

    return pl.pallas_call(
        body,
        out_shape=jax.ShapeDtypeStruct(value.shape, value.dtype),
        grid_spec=pltpu.PrefetchScalarGridSpec(
            num_scalar_prefetch=1,
            grid=(count,),
            in_specs=[pl.BlockSpec((rows, block), lambda i, ix: (0, ix[i]))],
            out_specs=pl.BlockSpec((rows, block), lambda i, ix: (0, i)),
        ),
        compiler_params=params(),
        name="permute_columns",
    )(index, value)


def head_stats(x, low):
    square = x * x
    first = jnp.sum(jnp.where(low, square, 0.0), -1, keepdims=True)
    second = jnp.sum(jnp.where(low, 0.0, square), -1, keepdims=True)
    return lax.rsqrt(jnp.where(low, first, second) * (1.0 / HD) + EPSILON)


def head_mean(x, low):
    first = jnp.sum(jnp.where(low, x, 0.0), -1, keepdims=True)
    second = jnp.sum(jnp.where(low, 0.0, x), -1, keepdims=True)
    return jnp.where(low, first, second) * (1.0 / HD)


def lane_masks(rows):
    lane = lax.broadcasted_iota(jnp.int32, (rows, LANES), 1)
    return lane < HD, lax.rem(lane, HD) < HD // 2


def qk_forward(lin, qgain, kgain, cosine, sine, rows, slots):
    total = QW + 2 * KVW

    def body(lin_ref, qgain_ref, kgain_ref, cos_ref, sin_ref, q_ref, kv_ref):
        low, front = lane_masks(slots)
        cos, sin = cos_ref[...], sin_ref[...]

        def turn(x, gain):
            n = x * head_stats(x, low) * gain
            turned = jnp.where(
                front, -pltpu.roll(n, LANES - HD // 2, 1), pltpu.roll(n, HD // 2, 1)
            )
            return n * cos + turned * sin

        for c in range(QW // LANES):
            x = lin_ref[:, c * LANES : (c + 1) * LANES]
            y = turn(x, qgain_ref[...]) * (1.0 / math.sqrt(HD))
            q_ref[:, c * LANES : (c + 1) * LANES] = y.astype(BF16)
        for g in range(KVH):
            x = lin_ref[:, QW + g * LANES : QW + (g + 1) * LANES]
            y = jnp.where(low, turn(x, kgain_ref[...]), x)
            kv_ref[:, g * LANES : (g + 1) * LANES] = y.astype(BF16)

    n = rows * slots
    whole = lambda r: (0, 0)
    return pl.pallas_call(
        body,
        out_shape=(
            jax.ShapeDtypeStruct((n, QW), BF16),
            jax.ShapeDtypeStruct((n, 2 * KVW), BF16),
        ),
        grid=(rows,),
        in_specs=[
            pl.BlockSpec((slots, total), lambda r: (r, 0)),
            pl.BlockSpec((1, LANES), whole),
            pl.BlockSpec((1, LANES), whole),
            pl.BlockSpec((slots, LANES), whole),
            pl.BlockSpec((slots, LANES), whole),
        ],
        out_specs=(
            pl.BlockSpec((slots, QW), lambda r: (r, 0)),
            pl.BlockSpec((slots, 2 * KVW), lambda r: (r, 0)),
        ),
        compiler_params=params(),
        name="qk_forward",
    )(lin, qgain, kgain, cosine, sine)


def qk_backward(dq, dkv, lin, qgain, kgain, cosine, sine, rows, slots):
    total = QW + 2 * KVW

    def body(
        dq_ref, dkv_ref, lin_ref, qgain_ref, kgain_ref, cos_ref, sin_ref, out_ref, gq_ref, gk_ref
    ):
        low, front = lane_masks(slots)
        cos, sin = cos_ref[...], sin_ref[...]

        @pl.when(pl.program_id(0) == 0)
        def _():
            gq_ref[...] = jnp.zeros_like(gq_ref)
            gk_ref[...] = jnp.zeros_like(gk_ref)

        def back(e, x, gain):
            t = e * sin
            e = e * cos + jnp.where(
                front, pltpu.roll(t, LANES - HD // 2, 1), -pltpu.roll(t, HD // 2, 1)
            )
            inv = head_stats(x, low)
            unit = x * inv
            part = e * unit
            u = e * gain
            return inv * (u - unit * head_mean(u * unit, low)), part

        gq = jnp.zeros((1, LANES), F32)
        for c in range(QW // LANES):
            at = slice(c * LANES, (c + 1) * LANES)
            y, part = back(dq_ref[:, at], lin_ref[:, at], qgain_ref[...])
            out_ref[:, at] = y.astype(BF16)
            gq = gq + jnp.sum(part, 0, keepdims=True)
        gk = jnp.zeros((1, LANES), F32)
        for g in range(KVH):
            at = slice(QW + g * LANES, QW + (g + 1) * LANES)
            e = dkv_ref[:, g * LANES : (g + 1) * LANES]
            y, part = back(e, lin_ref[:, at], kgain_ref[...])
            out_ref[:, at] = jnp.where(low, y, e).astype(BF16)
            gk = gk + jnp.sum(jnp.where(low, part, 0.0), 0, keepdims=True)
        gq_ref[...] += gq
        gk_ref[...] += gk

    n = rows * slots
    whole = lambda r: (0, 0)
    return pl.pallas_call(
        body,
        out_shape=(
            jax.ShapeDtypeStruct((n, total), BF16),
            jax.ShapeDtypeStruct((1, LANES), F32),
            jax.ShapeDtypeStruct((1, LANES), F32),
        ),
        grid=(rows,),
        in_specs=[
            pl.BlockSpec((slots, QW), lambda r: (r, 0)),
            pl.BlockSpec((slots, 2 * KVW), lambda r: (r, 0)),
            pl.BlockSpec((slots, total), lambda r: (r, 0)),
            pl.BlockSpec((1, LANES), whole),
            pl.BlockSpec((1, LANES), whole),
            pl.BlockSpec((slots, LANES), whole),
            pl.BlockSpec((slots, LANES), whole),
        ],
        out_specs=(
            pl.BlockSpec((slots, total), lambda r: (r, 0)),
            pl.BlockSpec((1, LANES), whole),
            pl.BlockSpec((1, LANES), whole),
        ),
        compiler_params=params(),
        name="qk_backward",
    )(dq, dkv, lin, qgain, kgain, cosine, sine)


def fill_bias(bias_ref, info_ref, row, masks, slots):
    place, length = info_ref[0], info_ref[1 + row]
    query = place * slots + lax.broadcasted_iota(jnp.int32, (slots, slots), 1)
    for i, mask in enumerate(masks):
        key = (place ^ mask) * slots + lax.broadcasted_iota(jnp.int32, (slots, slots), 0)
        allowed = (key <= query) & (key < length)
        bias_ref[i * slots : (i + 1) * slots, :] = jnp.where(allowed, 0.0, NEG)


def attend(info, q, kv_pieces, masks, rows, slots):
    count = len(masks)
    keys = count * slots

    def body(info_ref, q_ref, *refs):
        kv_refs, (o_ref, lse_ref, bias_ref) = refs[:count], refs[count:]
        row = pl.program_id(0)
        live = info_ref[0] * slots < info_ref[1 + row]

        @pl.when(live & (pl.program_id(1) == 0))
        def _():
            fill_bias(bias_ref, info_ref, row, masks, slots)

        @pl.when(jnp.logical_not(live))
        def _():
            o_ref[...] = jnp.zeros_like(o_ref)
            lse_ref[...] = jnp.zeros_like(lse_ref)

        @pl.when(live)
        def _():
            kv = jnp.concatenate([r[...] for r in kv_refs], 0)
            k, v = kv[:, :HD], kv[:, HD:]
            for h in range(GROUP):
                qh = q_ref[:, h * HD : (h + 1) * HD]
                s = nt(k, qh) + bias_ref[...]
                m = jnp.max(s, 0, keepdims=True)
                e = jnp.exp(s - m)
                l = jnp.sum(e, 0, keepdims=True)
                p = (e * (1.0 / l)).astype(BF16)
                o = tn(v, p)
                o_ref[:, h * HD : (h + 1) * HD] = o.T.astype(BF16)
                lse_ref[0, 0, h : h + 1, :] = m + jnp.log(l)

    n = rows * slots
    return pl.pallas_call(
        body,
        out_shape=(
            jax.ShapeDtypeStruct((n, QW), BF16),
            jax.ShapeDtypeStruct((rows, KVH, GROUP, slots), F32),
        ),
        grid_spec=pltpu.PrefetchScalarGridSpec(
            num_scalar_prefetch=1,
            grid=(rows, KVH),
            in_specs=[pl.BlockSpec((slots, GW), lambda r, g, s: (r, g))]
            + [pl.BlockSpec((slots, LANES), lambda r, g, s: (r, g))] * count,
            out_specs=(
                pl.BlockSpec((slots, GW), lambda r, g, s: (r, g)),
                pl.BlockSpec((1, 1, GROUP, slots), lambda r, g, s: (r, g, 0, 0)),
            ),
            scratch_shapes=[pltpu.VMEM((keys, slots), F32)],
        ),
        compiler_params=params(),
        cost_estimate=pl.CostEstimate(
            flops=16 * n * keys * QW, bytes_accessed=8 * n * QW, transcendentals=n * keys * HQ
        ),
        name="attend",
    )(info, q, *kv_pieces)


def attend_back(info, q, kv_pieces, do, lse, masks, rows, slots):
    count = len(masks)
    keys = count * slots

    def body(info_ref, q_ref, do_ref, lse_ref, *refs):
        kv_refs, dq_ref = refs[:count], refs[count]
        dkv_refs, bias_ref = refs[count + 1 : -1], refs[-1]
        row = pl.program_id(0)
        live = info_ref[0] * slots < info_ref[1 + row]

        @pl.when(live & (pl.program_id(1) == 0))
        def _():
            fill_bias(bias_ref, info_ref, row, masks, slots)

        @pl.when(jnp.logical_not(live))
        def _():
            dq_ref[...] = jnp.zeros_like(dq_ref)
            for r in dkv_refs:
                r[...] = jnp.zeros_like(r)

        @pl.when(live)
        def _():
            kv = jnp.concatenate([r[...] for r in kv_refs], 0)
            k, v = kv[:, :HD], kv[:, HD:]
            dk = jnp.zeros((keys, HD), F32)
            dv = jnp.zeros((keys, HD), F32)
            for h in range(GROUP):
                at = slice(h * HD, (h + 1) * HD)
                qh, doh = q_ref[:, at], do_ref[:, at]
                p = jnp.exp(nt(k, qh) + bias_ref[...] - lse_ref[0, 0, h : h + 1, :])
                dp = nt(v, doh)
                delta = jnp.sum(p * dp, 0, keepdims=True)
                ds = (p * (dp - delta)).astype(BF16)
                dv = dv + nn(p.astype(BF16), doh)
                dk = dk + nn(ds, qh)
                dq_ref[:, at] = tn(k, ds).T * (1.0 / math.sqrt(HD))
            both = jnp.concatenate([dk, dv], 1).astype(BF16)
            for i, r in enumerate(dkv_refs):
                r[...] = both[i * slots : (i + 1) * slots, :]

    n = rows * slots
    kv_spec = pl.BlockSpec((slots, LANES), lambda r, g, s: (r, g))
    q_spec = pl.BlockSpec((slots, GW), lambda r, g, s: (r, g))
    return pl.pallas_call(
        body,
        out_shape=(
            jax.ShapeDtypeStruct((n, QW), F32),
            *([jax.ShapeDtypeStruct((n, 2 * KVW), BF16)] * count),
        ),
        grid_spec=pltpu.PrefetchScalarGridSpec(
            num_scalar_prefetch=1,
            grid=(rows, KVH),
            in_specs=[
                q_spec,
                q_spec,
                pl.BlockSpec((1, 1, GROUP, slots), lambda r, g, s: (r, g, 0, 0)),
            ]
            + [kv_spec] * count,
            out_specs=(q_spec, *([kv_spec] * count)),
            scratch_shapes=[pltpu.VMEM((keys, slots), F32)],
        ),
        compiler_params=params(),
        cost_estimate=pl.CostEstimate(
            flops=40 * n * keys * QW, bytes_accessed=16 * n * QW, transcendentals=n * keys * HQ
        ),
        name="attend_back",
    )(info, q, do, lse, *kv_pieces)


def feed_forward(w_pieces, n2, bg, sums, acts, total, offset, last):
    parts, (tokens, depth), units = len(n2), n2[0].shape, w_pieces[0].shape[1]
    count, block = len(w_pieces), depth // len(w_pieces)
    tile = min(256, tokens)
    per = tokens // tile
    steps = parts * per
    shift = offset // tile
    tu = 256 if units % 256 == 0 else units
    td = 256
    sum_type = BF16 if last else F32
    has_sums, has_acts = sums is not None, acts is not None

    def body(*refs):
        w_refs, refs = refs[:count], refs[count:]
        n2_refs, refs = refs[:parts], refs[parts:]
        bg_refs, refs = refs[:parts], refs[parts:]
        sum_refs = ()
        if has_sums:
            sum_refs, refs = refs[:2], refs[2:]
        if has_acts:
            refs = refs[3:]
        branch_ref, grad_ref, h_ref, gg_ref, ug_ref = refs[:5]
        wg, wu, wd, sem = refs[5:]
        step = pl.program_id(0)

        @pl.when(step == 0)
        def _():
            copies = []
            for i, w in enumerate(w_refs):
                for j, dst in enumerate((wg, wu, wd)):
                    copies.append(
                        pltpu.make_async_copy(
                            w.at[j * block : (j + 1) * block, :],
                            dst.at[i * block : (i + 1) * block, :],
                            sem.at[3 * i + j],
                        )
                    )
            for c in copies:
                c.start()
            for c in copies:
                c.wait()

        x, b = n2_refs[0][...], bg_refs[0][...]
        for p in range(1, parts):
            here = step >= p * per
            x = jnp.where(here, n2_refs[p][...], x)
            b = jnp.where(here, bg_refs[p][...], b)
        for j in range(units // tu):
            at = slice(j * tu, (j + 1) * tu)
            gate, up = nn(x, wg[:, at]), nn(x, wu[:, at])
            dh = nn(b, wd[:, at])
            sig = 1.0 / (1.0 + jnp.exp(-gate))
            act = gate * sig
            h_ref[:, at] = (act * up).astype(BF16)
            gg_ref[:, at] = (dh * up * sig * (1.0 + gate * (1.0 - sig))).astype(BF16)
            ug_ref[:, at] = (dh * act).astype(BF16)
        h, gg, ug = h_ref[...], gg_ref[...], ug_ref[...]
        for j in range(depth // td):
            at = slice(j * td, (j + 1) * td)
            branch = nt(h, wd[at, :])
            grad = nt(gg, wg[at, :]) + nt(ug, wu[at, :])
            if has_sums:
                branch = branch + sum_refs[0][:, at]
                grad = grad + sum_refs[1][:, at]
            branch_ref[:, at] = branch.astype(sum_type)
            grad_ref[:, at] = grad.astype(sum_type)

    def token_map(p):
        return lambda i: (jnp.clip(i - p * per, 0, per - 1), 0)

    tok = [pl.BlockSpec((tile, depth), token_map(p)) for p in range(parts)]
    any_spec = pl.BlockSpec(memory_space=pl.ANY)
    sum_spec = pl.BlockSpec((tile, depth), lambda i: (i, 0))
    act_spec = pl.BlockSpec((tile, units), lambda i: (i + shift, 0))
    operands = [*w_pieces, *n2, *bg]
    in_specs = [any_spec] * count + tok + tok
    aliases = {}
    if has_sums:
        operands += sums
        in_specs += [sum_spec] * 2
    if has_acts:
        for j in range(3):
            aliases[len(operands) + j] = 2 + j
        operands += acts
        in_specs += [any_spec] * 3
    n = parts * tokens
    flops = 12 * n * depth * units
    out = pl.pallas_call(
        body,
        out_shape=(
            *([jax.ShapeDtypeStruct((n, depth), sum_type)] * 2),
            *([jax.ShapeDtypeStruct((total, units), BF16)] * 3),
        ),
        grid=(steps,),
        in_specs=in_specs,
        out_specs=(sum_spec, sum_spec, act_spec, act_spec, act_spec),
        scratch_shapes=[pltpu.VMEM((depth, units), BF16)] * 3
        + [pltpu.SemaphoreType.DMA((3 * count,))],
        input_output_aliases=aliases,
        compiler_params=params(),
        cost_estimate=pl.CostEstimate(
            flops=flops, bytes_accessed=16 * n * depth, transcendentals=n * units
        ),
        name="feed_forward",
    )(*operands)
    return list(out[:2]), list(out[2:])


def rope_tables(positions):
    steps_half = jnp.arange(HD // 2, dtype=F32)
    inverse = jnp.exp(steps_half * (-2.0 * math.log(ROPE_BASE) / HD))
    angles = positions.astype(F32)[:, None] * inverse[None, :]
    return jnp.tile(jnp.cos(angles), (1, 4)), jnp.tile(jnp.sin(angles), (1, 4))


def norm_rows(values, gain_vec):
    scale_inv = lax.rsqrt(jnp.mean(values * values, -1, keepdims=True) + EPSILON)
    unit_rows = values * scale_inv
    return unit_rows * gain_vec, unit_rows, scale_inv


def norm_back(grad_unit, unit_rows, scale_inv):
    return scale_inv * (grad_unit - unit_rows * jnp.mean(grad_unit * unit_rows, -1, keepdims=True))


def after(value, *others):
    return lax.optimization_barrier((value, *others))[0]


def make_layer(dp_ring, ctx_ring):
    nd, nc = dp_ring.size, ctx_ring.size
    dp_masks, ctx_masks = dp_ring.masks, ctx_ring.masks

    def column_blocks(stack):
        place = lax.axis_index("ctx")
        by_mask = jnp.stack([stack[ctx_masks.index(m)] for m in range(nc)], 0)
        ordered = jnp.take(by_mask, place ^ jnp.arange(nc), axis=0)
        return jnp.transpose(ordered, (1, 0, 2)).reshape(ordered.shape[1], -1)

    def relative_columns(value):
        place = lax.axis_index("ctx")
        width = value.shape[1] // nc
        return [
            lax.dynamic_slice_in_dim(value, (place ^ m) * width, width, 1) for m in ctx_masks
        ]

    def interleave(k, v):
        rows = k.shape[0]
        both = jnp.stack([k.reshape(rows, KVH, HD), v.reshape(rows, KVH, HD)], 2)
        return both.reshape(rows, 2 * KVW)

    def per_device(
        layer_input,
        lengths,
        attn_gain,
        w_query,
        w_key,
        w_value,
        query_gain,
        key_gain,
        w_out,
        ffn_gain,
        w_gate,
        w_up,
        w_down,
        cotangent,
    ):
        rows, slots, depth = layer_input.shape
        n = rows * slots
        block = depth // nd
        qc, kc, units = w_query.shape[1], w_key.shape[1], w_gate.shape[1]
        group, place = lax.axis_index("dp"), lax.axis_index("ctx")
        to_relative = group ^ jnp.array(dp_masks, jnp.int32)
        where_mask = np.argsort(np.array(dp_masks))
        to_absolute = jnp.array(where_mask, jnp.int32)[group ^ jnp.arange(nd)]
        positions = place * slots + jnp.arange(slots, dtype=jnp.int32)
        cosine, sine = rope_tables(positions)
        info = jnp.concatenate([place[None].astype(jnp.int32), lengths])
        valid = (positions[None, :] < lengths[:, None]).astype(F32).reshape(n, 1)
        qgain2 = jnp.tile(query_gain, 2)[None, :]
        kgain2 = jnp.tile(key_gain, 2)[None, :]

        qkv_held, first = dp_ring.gather(jnp.concatenate([w_query, w_key, w_value], 1))
        out_held, first_out = dp_ring.gather(after(w_out, *first[1:]))
        sizes = [768, 512] if units == 1280 else [units]
        chunks, start, behind = [], 0, first_out
        for size in sizes:
            at = slice(start, start + size)
            local = jnp.concatenate([w_gate[:, at], w_up[:, at], w_down[:, at]], 0)
            held, behind = dp_ring.gather(after(local, *behind[1:]))
            chunks.append(held)
            start += size

        x_bf = permute_columns(layer_input.reshape(n, depth), to_relative)
        bg = permute_columns(
            (cotangent.reshape(n, depth).astype(F32) * valid).astype(BF16), to_relative
        )
        gain_one = jnp.take(attn_gain.reshape(nd, block), to_relative, axis=0).reshape(depth)
        gain_two = jnp.take(ffn_gain.reshape(nd, block), to_relative, axis=0).reshape(depth)
        bg_all, _ = ctx_ring.gather(bg)

        x = x_bf.astype(F32)
        normed_one, unit_one, inv_one = norm_rows(x, gain_one)
        normed_bf = normed_one.astype(BF16)

        qkv_cols, _ = ctx_ring.gather(jnp.concatenate(qkv_held, 0))
        mat_q = column_blocks([c[:, :qc] for c in qkv_cols])
        mat_k = column_blocks([c[:, qc : qc + kc] for c in qkv_cols])
        mat_v = column_blocks([c[:, qc + kc :] for c in qkv_cols])
        mat_qkv = jnp.concatenate([mat_q, interleave(mat_k, mat_v)], 1)
        out_cols, _ = ctx_ring.gather(jnp.concatenate(out_held, 0))
        mat_out = column_blocks(out_cols)

        lin = nn(normed_bf, mat_qkv)
        q, kv = qk_forward(lin, qgain2, kgain2, cosine, sine, rows, slots)
        kv_all, _ = ctx_ring.gather(kv)
        mixed, lse = attend(info, q, kv_all, ctx_masks, rows, slots)
        middle = x + nt(mixed, mat_out)
        normed_two, unit_two, inv_two = norm_rows(middle, gain_two)
        n2_all, _ = ctx_ring.gather(normed_two.astype(BF16))

        half = nc // 2
        near = [i for i in range(nc) if not ctx_masks[i] & (nc >> 1)]
        far = [i for i in range(nc) if ctx_masks[i] & (nc >> 1)]
        pick = lambda pieces, which: [pieces[i] for i in which]
        sums = {"near": None, "far": None}
        acts_of = []
        for c, held in enumerate(chunks):
            last = c == len(chunks) - 1
            order = ("near", "far") if c == 0 else ("far", "near")
            acts = None
            for side in order:
                which, offset = (near, 0) if side == "near" else (far, half * n)
                sums[side], acts = feed_forward(
                    held,
                    pick(n2_all, which),
                    pick(bg_all, which),
                    sums[side],
                    acts,
                    nc * n,
                    offset,
                    last,
                )
            acts_of.append(acts)

        def pieces_of(k):
            out = [None] * nc
            for side, which in (("near", near), ("far", far)):
                for slot, i in enumerate(which):
                    out[i] = sums[side][k][slot * n : (slot + 1) * n].astype(F32)
            return out

        n2_cat = jnp.concatenate(pick(n2_all, near + far), 0)
        bg_cat = jnp.concatenate(pick(bg_all, near + far), 0)

        def scatter_rows(left, right):
            width = depth // (1 << len(dp_ring.late))
            parts = [
                tn(left[:, i * width : (i + 1) * width], right)
                for i in range(1 << len(dp_ring.late))
            ]
            parts = dp_ring.scatter_late(parts)[0]
            return dp_ring.scatter_direct(
                [parts[i * block : (i + 1) * block] for i in range(len(dp_ring.combos))]
            )

        gate_parts, up_parts, down_parts = [], [], []
        for h, gg, ug in acts_of:
            gate_parts.append(scatter_rows(n2_cat, gg))
            up_parts.append(scatter_rows(n2_cat, ug))
            down_parts.append(scatter_rows(bg_cat, h))

        grad_two = ctx_ring.scatter(pieces_of(1))
        branch = ctx_ring.scatter(pieces_of(0))
        out_rows = permute_columns((valid * (middle + branch)).astype(BF16), to_absolute)
        ffn_gain_part = jnp.sum(grad_two * unit_two, 0)
        middle_grad = bg.astype(F32) + norm_back(grad_two * gain_two, unit_two, inv_two)
        attn_grad = middle_grad.astype(BF16)
        mixed_grad = nn(attn_grad, mat_out).astype(BF16)

        dq, *dkv = attend_back(info, q, kv_all, mixed_grad, lse, ctx_masks, rows, slots)
        dkv_own = ctx_ring.scatter([d.astype(F32) for d in dkv])
        dlin, gq, gk = qk_backward(dq, dkv_own, lin, qgain2, kgain2, cosine, sine, rows, slots)
        normed_grad = nt(dlin, mat_qkv)
        attn_gain_part = jnp.sum(normed_grad * unit_one, 0)
        input_grad = (middle_grad + norm_back(normed_grad * gain_one, unit_one, inv_one)).astype(
            BF16
        )
        input_grad = permute_columns(input_grad, to_absolute)

        def scatter_both(blocks):
            own = ctx_ring.scatter(blocks)
            width = depth // (1 << len(dp_ring.late))
            parts = [own[i * width : (i + 1) * width] for i in range(1 << len(dp_ring.late))]
            parts = dp_ring.scatter_late(parts)[0]
            return dp_ring.scatter_direct(
                [parts[i * block : (i + 1) * block] for i in range(len(dp_ring.combos))]
            )

        w_out_grad = scatter_both([tn(attn_grad, m) for m in relative_columns(mixed)])
        dkv_heads = dlin[:, QW:].reshape(n, KVH, 2, HD)
        dk, dv = dkv_heads[:, :, 0].reshape(n, KVW), dkv_heads[:, :, 1].reshape(n, KVW)
        cuts = zip(
            relative_columns(dlin[:, :QW]), relative_columns(dk), relative_columns(dv)
        )
        w_qkv_grad = scatter_both(
            [tn(normed_bf, jnp.concatenate(cut, 1)) for cut in cuts]
        )

        def absolute(part):
            return jnp.take(part.reshape(nd, block), to_absolute, axis=0).reshape(depth)

        gains = jnp.concatenate(
            [absolute(attn_gain_part), absolute(ffn_gain_part), gq[0], gk[0]]
        )
        gains = lax.psum(gains, ("dp", "ctx"))
        gq = gains[2 * depth : 2 * depth + LANES]
        gk = gains[2 * depth + LANES :]
        return (
            out_rows.reshape(rows, slots, depth),
            input_grad.reshape(rows, slots, depth),
            gains[:depth],
            w_qkv_grad[:, :qc],
            w_qkv_grad[:, qc : qc + kc],
            w_qkv_grad[:, qc + kc :],
            gq[:HD] + gq[HD:],
            gk[:HD] + gk[HD:],
            w_out_grad,
            gains[depth : 2 * depth],
            jnp.concatenate(gate_parts, 1),
            jnp.concatenate(up_parts, 1),
            jnp.concatenate(down_parts, 1),
        )

    return per_device


def solution(mesh):
    wide = P("dp", "ctx")
    rows = P("dp", "ctx", None)
    in_specs = (
        rows, P("dp"), P(), wide, wide, wide, P(), P(), wide, P(), wide, wide, wide, rows,
    )
    out_specs = (
        rows, rows, P(), wide, wide, wide, P(), P(), wide, P(), wide, wide, wide,
    )
    return jax.shard_map(
        make_layer(*rings(mesh)),
        mesh=mesh,
        in_specs=in_specs,
        out_specs=out_specs,
        check_vma=False,
    )
```

time: 2610 us -> 1250 us (0.48)
  waiting for transfers between devices: 1960 us -> 531 us
  matrix products: 356 us -> 104 us
  Pallas kernels: 0 us -> 235 us
  starting transfers between devices: 31.4 us -> 110 us
  local copies, waits for them, and re-layouts: 53.4 us -> 89 us
    all_gather x16 -> x0, waiting for transfers between devices: 1530 us -> none  [the longest x1 391 us: per_device(): lax.all_gather(columns[5], 'dp', axis=0, tiled=True)]
    ppermute x0 -> x90, waiting for transfers between devices: none -> 531 us  [swap(): lax.ppermute(value, self.axis, [(i, i ^ mask) for i in range(self.size)])]
    dot_general x47 -> x24, matrix products: 356 us -> 104 us  [the longest x20 79.6 us: tn(): lax.dot_general(a, b, (((0,), (0,)), ((), ())), preferred_element_type=F32)]
    pallas_call x0 -> x12, Pallas kernels: none -> 235 us  [the longest x4 109 us: feed_forward(): pl.pallas_call(body, out_shape=(*[jax.ShapeDtypeStruct((n, depth), sum_ty...]
    reduce_scatter x3 -> x0, waiting for transfers between devices: 228 us -> none  [the longest x1 228 us: per_device(): lax.psum_scatter(jnp.concatenate([contract_rows(normed_cut, right_parts[0...]
    all_to_all x7 -> x0, waiting for transfers between devices: 206 us -> none  [the longest x1 92.3 us: per_device(): lax.all_to_all(joined['gate'], 'ctx', split_axis=1, concat_axis=0, tiled=...]
    ppermute x0 -> x90, starting transfers between devices: none -> 110 us  [swap(): lax.ppermute(value, self.axis, [(i, i ^ mask) for i in range(self.size)])]
    psum x1, blocking collectives: 44 us -> 90 us  [per_device(): gains = lax.psum(gains, ('dp', 'ctx'))]
  transfers between devices with their start and end apart: 26 -> 90, of which waited for: 22 -> 29; matrix products, arithmetic and copies ran while one was open for 12% -> 20% of each run, Pallas kernels for 0% -> 15%
where the time goes in v1:
time: 1250 us; the launch traced here: 1240 us
  waiting for transfers between devices  531 us (42%)
  Pallas kernels  235 us (19%)
  starting transfers between devices  110 us (9%)
  matrix products  104 us (8%)
  blocking collectives  90 us (7%)
  local copies, waits for them, and re-layouts  89 us (7%)
  other arithmetic  81.9 us (7%)
    ppermute x90, waiting for transfers between devices, swap(): lax.ppermute(value, self.axis, [(i, i ^ mask) for i in range(self.size)])  531 us
    ppermute x90, starting transfers between devices, swap(): lax.ppermute(value, self.axis, [(i, i ^ mask) for i in range(self.size)])  110 us
    pallas_call x4, Pallas kernels, feed_forward(): pl.pallas_call(body, out_shape=(*[jax.ShapeDtypeStruct((n, depth), sum_ty...  109 us
    psum x1, blocking collectives, per_device(): gains = lax.psum(gains, ('dp', 'ctx'))  90 us
    dot_general x20, matrix products, tn(): lax.dot_general(a, b, (((0,), (0,)), ((), ())), preferred_element_type=F32)  79.6 us
    pallas_call x1, Pallas kernels, attend_back(): pl.pallas_call(body, out_shape=(jax.ShapeDtypeStruct((n, QW), F32), *[jax...  40.9 us
    pallas_call x1, Pallas kernels, attend(): pl.pallas_call(body, out_shape=(jax.ShapeDtypeStruct((n, QW), BF16), jax....  38.4 us
    unnamed x193, local copies, waits for them, and re-layouts  38.2 us
  transfers between devices with their start and end apart: 90, of which 29 were waited for; matrix products, arithmetic and copies ran while one was open for 20% of the time, Pallas kernels for 15%

profile of v1, /device:TPU:0, one launch (start us, length us, event | category | flops | bytes accessed | tf_op | source)
XLA Modules:
  0.0 1242.9 jit_solution(5650992100106729436)
XLA Ops:
  76.6 64.3 %collective-permute-done.21 = bf16[2048,320]{0,1:T(8,128)(2,1)S(1)} collective-permute-done((bf16[2048,320]{0,1:T(8,128)(2,1)S(1)}, bf16[2048,320]{0,1:T(8,128)(2,1)S(1)}, u32[]{:S(2)}, u32[]{:S(2)}) %collective-permute-start.21) | collective-permute-done | bytes 1310752 | tf_op jit(solution)/shard_map/ppermute | solution.py:56
  175.9 9.1 broadcast_select_fusion
  185.0 9.8 fusion.5.lin_ref
  194.8 8.8 qk_forward.1
  208.7 12.3 collective-permute-done.10.refs_1_
  221.8 63.8 %collective-permute-done.24.refs_2_ = bf16[768,768]{1,0:T(8,128)(2,1)S(1)} collective-permute-done((bf16[768,768]{1,0:T(8,128)(2,1)}, bf16[768,768]{1,0:T(8,128)(2,1)S(1)}, u32[]{:S(2)}, u32[]{:S(2)}) %collective-permute-start.24) | collective-permute-done | bytes 1179680 | tf_op jit(solution)/shard_map/ppermute | solution.py:56
  287.1 24.8 %collective-permute-start.26 = (bf16[768,512]{1,0:T(8,128)(2,1)S(1)}, bf16[768,512]{1,0:T(8,128)(2,1)}, u32[]{:S(2)}, u32[]{:S(2)}) collective-permute-start(bf16[768,512]{1,0:T(8,128)(2,1)S(1)} %pad_maximum_fusion.14.refs_0_), channel_id=1, source_target_pairs={{0,8},{4,12},{8,0},{12,4},{16,24},{20,28},{24,16},{28,20},{1,9},{5... | collective-permute-start | bytes 2359304 | tf_op jit(solution)/shard_map/ppermute | solution.py:56
  313.5 38.4 %attend.1 = (bf16[512,1280]{1,0:T(8,128)(2,1)}, f32[2,5,4,256]{3,2,1,0:T(4,128)}) custom-call(s32[3]{0:T(128)} %pad_add_fusion.info_ref, bf16[512,1280]{1,0:T(8,128)(2,1)} %get-tuple-element.51.q_ref, bf16[512,640]{1,0:T(8,128)(2,1)} %get-tuple-element.52.refs_0_, bf16[512,640]{1,0:T(8,128)(2,1)} %copy-done.62, bf16[512,640]{1,0:T(8,128)(2,1)} %copy-done.63, ...), custom_call_target="tpu_custom_call" | custom-call | flops 10737418240 | bytes 5242880 | tf_op jit(solution)/shard_map/attend/pallas_call | solution.py:306
  362.9 50.4 %collective-permute-done.27.refs_2_ = bf16[768,512]{1,0:T(8,128)(2,1)} collective-permute-done((bf16[768,512]{1,0:T(8,128)(2,1)S(1)}, bf16[768,512]{1,0:T(8,128)(2,1)}, u32[]{:S(2)}, u32[]{:S(2)}) %collective-permute-start.27) | collective-permute-done | bytes 786464 | tf_op jit(solution)/shard_map/ppermute | solution.py:56
  424.7 17.7 %collective-permute-done.36.refs_5_ = bf16[768,768]{1,0:T(8,128)(2,1)} collective-permute-done((bf16[768,768]{1,0:T(8,128)(2,1)}, bf16[768,768]{1,0:T(8,128)(2,1)}, u32[]{:S(2)}, u32[]{:S(2)}) %collective-permute-start.36) | collective-permute-done | bytes 1179680 | tf_op jit(solution)/shard_map/ppermute | solution.py:56
  443.7 24.1 %collective-permute-done.37.refs_6_ = bf16[768,768]{1,0:T(8,128)(2,1)} collective-permute-done((bf16[768,768]{1,0:T(8,128)(2,1)}, bf16[768,768]{1,0:T(8,128)(2,1)}, u32[]{:S(2)}, u32[]{:S(2)}) %collective-permute-start.37) | collective-permute-done | bytes 1179680 | tf_op jit(solution)/shard_map/ppermute | solution.py:56
  468.9 24.1 %collective-permute-done.38.refs_7_ = bf16[768,768]{1,0:T(8,128)(2,1)} collective-permute-done((bf16[768,768]{1,0:T(8,128)(2,1)}, bf16[768,768]{1,0:T(8,128)(2,1)}, u32[]{:S(2)}, u32[]{:S(2)}) %collective-permute-start.38) | collective-permute-done | bytes 1179680 | tf_op jit(solution)/shard_map/ppermute | solution.py:56
  495.0 31.1 %feed_forward.4 = (f32[1024,2048]{1,0:T(8,128)}, f32[1024,2048]{1,0:T(8,128)}, bf16[2048,768]{1,0:T(8,128)(2,1)}, bf16[2048,768]{1,0:T(8,128)(2,1)}, bf16[2048,768]{1,0:T(8,128)(2,1)}) custom-call(bf16[768,768]{1,0:T(8,128)(2,1)} %pad_maximum_fusion.13.refs_0_, bf16[768,768]{1,0:T(8,128)(2,1)} %collective-permute-done.23.refs_1_, ...), custom_call_target="tpu_custom_call" | custom-call | flops 19327352832 | bytes 33554432 | tf_op jit(solution)/shard_map/feed_forward/pallas_call | solution.py:487
  526.1 31.3 %feed_forward.5 = (f32[1024,2048]{1,0:T(8,128)}, f32[1024,2048]{1,0:T(8,128)}, bf16[2048,768]{1,0:T(8,128)(2,1)}, bf16[2048,768]{1,0:T(8,128)(2,1)}, bf16[2048,768]{1,0:T(8,128)(2,1)}) custom-call(bf16[768,768]{1,0:T(8,128)(2,1)} %pad_maximum_fusion.13.refs_0_, ...), custom_call_target="tpu_custom_call", output_to_operand_aliasing={{2}: (12, {}), {3}: (13, {}), {4}: (14, {})} | custom-call | flops 19327352832 | bytes 33554432 | tf_op jit(solution)/shard_map/feed_forward/pallas_call | solution.py:487
  560.1 23.3 %feed_forward.6 = (bf16[1024,2048]{1,0:T(8,128)(2,1)}, bf16[1024,2048]{1,0:T(8,128)(2,1)}, bf16[2048,512]{1,0:T(8,128)(2,1)}, bf16[2048,512]{1,0:T(8,128)(2,1)}, bf16[2048,512]{1,0:T(8,128)(2,1)}) custom-call(bf16[768,512]{1,0:T(8,128)(2,1)} %copy-done.25, bf16[768,512]{1,0:T(8,128)(2,1)} %collective-permute-done.26.refs_1_, ...), custom_call_target="tpu_custom_call" | custom-call | flops 12884901888 | bytes 33554432 | tf_op jit(solution)/shard_map/feed_forward/pallas_call | solution.py:487
  583.4 23.3 %feed_forward.7 = (bf16[1024,2048]{1,0:T(8,128)(2,1)}, bf16[1024,2048]{1,0:T(8,128)(2,1)}, bf16[2048,512]{1,0:T(8,128)(2,1)}, bf16[2048,512]{1,0:T(8,128)(2,1)}, bf16[2048,512]{1,0:T(8,128)(2,1)}) custom-call(bf16[768,512]{1,0:T(8,128)(2,1)} %copy-done.25, ...), custom_call_target="tpu_custom_call", output_to_operand_aliasing={{2}: (14, {}), {3}: (15, {}), {4}: (16, {})} | custom-call | flops 12884901888 | bytes 33554432 | tf_op jit(solution)/shard_map/feed_forward/pallas_call | solution.py:487
  652.9 48.5 %collective-permute-done.78 = bf16[1024,512]{0,1:T(8,128)(2,1)S(1)} collective-permute-done((bf16[1024,512]{0,1:T(8,128)(2,1)}, bf16[1024,512]{0,1:T(8,128)(2,1)S(1)}, u32[]{:S(2)}, u32[]{:S(2)}) %collective-permute-start.78) | collective-permute-done | bytes 1048608 | tf_op jit(solution)/shard_map/ppermute | solution.py:56
  705.4 50.2 %collective-permute-done.86 = bf16[1024,512]{0,1:T(8,128)(2,1)S(1)} collective-permute-done((bf16[1024,512]{0,1:T(8,128)(2,1)S(1)}, bf16[1024,512]{0,1:T(8,128)(2,1)S(1)}, u32[]{:S(2)}, u32[]{:S(2)}) %collective-permute-start.86) | collective-permute-done | bytes 1048608 | tf_op jit(solution)/shard_map/ppermute | solution.py:56
  774.5 17.3 %collective-permute-done.80 = bf16[256,512]{0,1:T(8,128)(2,1)S(1)} collective-permute-done((bf16[256,512]{0,1:T(8,128)(2,1)S(1)}, bf16[256,512]{0,1:T(8,128)(2,1)S(1)}, u32[]{:S(2)}, u32[]{:S(2)}) %collective-permute-start.80) | collective-permute-done | bytes 262176 | tf_op jit(solution)/shard_map/ppermute | solution.py:56
  795.7 12.2 collective-permute-done.88
  809.4 7.5 fusion.148
  834.7 20.5 %collective-permute-done.82 = bf16[1024,768]{0,1:T(8,128)(2,1)} collective-permute-done((bf16[1024,768]{0,1:T(8,128)(2,1)}, bf16[1024,768]{0,1:T(8,128)(2,1)}, u32[]{:S(2)}, u32[]{:S(2)}) %collective-permute-start.82) | collective-permute-done | bytes 1572896 | tf_op jit(solution)/shard_map/ppermute | solution.py:56
  863.8 11.1 collective-permute-done.68
  877.1 8.8 collective-permute-done.67
  896.1 28.6 %collective-permute-done.45 = bf16[512,2048]{1,0:T(8,128)(2,1)} collective-permute-done((bf16[512,2048]{1,0:T(8,128)(2,1)S(1)}, bf16[512,2048]{1,0:T(8,128)(2,1)}, u32[]{:S(2)}, u32[]{:S(2)}) %collective-permute-start.45) | collective-permute-done | bytes 2097184 | tf_op jit(solution)/shard_map/ppermute | solution.py:56
  924.7 8.6 fusion.135
  937.3 40.9 %attend_back.1 = (f32[512,1280]{1,0:T(8,128)}, bf16[512,640]{1,0:T(8,128)(2,1)}, bf16[512,640]{1,0:T(8,128)(2,1)}, bf16[512,640]{1,0:T(8,128)(2,1)}, bf16[512,640]{1,0:T(8,128)(2,1)}) custom-call(s32[3]{0:T(128)} %pad_add_fusion.info_ref, bf16[512,1280]{1,0:T(8,128)(2,1)} %get-tuple-element.51.q_ref, bf16[512,1280]{1,0:T(8,128)(2,1)} %convolution_convert_fusion.do_ref, ...), custom_call_target="tpu_custom_call" | custom-call | flops 26843545600 | bytes 10485760 | tf_op jit(solution)/shard_map/attend_back/pallas_call | solution.py:374
  1014.3 12.3 qk_backward.1
  1084.7 90.0 %psum.7 = f32[4352]{0:T(1024)} all-reduce(f32[4352]{0:T(1024)} %pad_maximum_fusion.15), channel_id=1, replica_groups=mesh['dp'=8,'ctx'=4] {'dp','ctx'}, use_global_device_ids=true, to_apply=%region_6.10 | all-reduce | flops 4352 | bytes 34816 | tf_op jit(solution)/shard_map/psum | solution.py:715
  1187.3 10.9 collective-permute-done.62
  1203.0 14.4 %collective-permute-done.55 = bf16[1024,480]{0,1:T(8,128)(2,1)S(1)} collective-permute-done((bf16[1024,480]{0,1:T(8,128)(2,1)S(1)}, bf16[1024,480]{0,1:T(8,128)(2,1)S(1)}, u32[]{:S(2)}, u32[]{:S(2)}) %collective-permute-start.55) | collective-permute-done | bytes 983072 | tf_op jit(solution)/shard_map/ppermute | solution.py:56
  1228.7 12.5 %collective-permute-done.57 = bf16[256,480]{0,1:T(8,128)(2,1)S(1)} collective-permute-done((bf16[256,480]{0,1:T(8,128)(2,1)S(1)}, bf16[256,480]{0,1:T(8,128)(2,1)S(1)}, u32[]{:S(2)}, u32[]{:S(2)}) %collective-permute-start.57) | collective-permute-done | bytes 245792 | tf_op jit(solution)/shard_map/ppermute | solution.py:56
  (507 shorter events, 390.0 us)
Async XLA Ops:
  24.1 262.6 %collective-permute-start.41 = (bf16[512,2048]{1,0:T(8,128)(2,1)}, bf16[512,2048]{1,0:T(8,128)(2,1)}, u32[]{:S(2)}, u32[]{:S(2)}) collective-permute-start(bf16[512,2048]{1,0:T(8,128)(2,1)} %permute_columns.5.refs_10_), channel_id=1, source_target_pairs={{0,2},{1,3},{2,0},{3,1},{4,6},{5,7},{6,4},{7,5},{8,10},{9,11},{10,... | collective-permute-start | bytes 6291464 | tf_op jit(solution)/shard_map/ppermute | solution.py:56
  63.8 77.1 %collective-permute-start.8 = (bf16[2048,480]{0,1:T(8,128)(2,1)S(1)}, bf16[2048,480]{0,1:T(8,128)(2,1)}, u32[]{:S(2)}, u32[]{:S(2)}) collective-permute-start(bf16[2048,480]{0,1:T(8,128)(2,1)S(1)} %constant_dynamic-update-slice_fusion.3), channel_id=1, source_target_pairs={{0,2},{1,3},{2,0},{3,1},{4,6},{5,7},{6,4},{7,5},{8,10},{9,11},{10,... | collective-permute-start | bytes 5898248 | tf_op jit(solution)/shard_map/ppermute | solution.py:56
  70.6 72.8 %collective-permute-start.7 = (bf16[2048,480]{0,1:T(8,128)(2,1)S(1)}, bf16[2048,480]{0,1:T(8,128)(2,1)S(1)}, u32[]{:S(2)}, u32[]{:S(2)}) collective-permute-start(bf16[2048,480]{0,1:T(8,128)(2,1)S(1)} %constant_dynamic-update-slice_fusion.3), channel_id=1, source_target_pairs={{0,1},{1,0},{2,3},{3,2},{4,5},{5,4},{6,7},{7,6},{8,9},{9,8},{10,11... | collective-permute-start | bytes 5898248 | tf_op jit(solution)/shard_map/ppermute | solution.py:56
  75.0 133.8 %collective-permute-start.23 = (bf16[768,768]{1,0:T(8,128)(2,1)}, bf16[768,768]{1,0:T(8,128)(2,1)}, u32[]{:S(2)}, u32[]{:S(2)}) collective-permute-start(bf16[768,768]{1,0:T(8,128)(2,1)} %pad_maximum_fusion.13.refs_0_), channel_id=1, source_target_pairs={{0,8},{4,12},{8,0},{12,4},{16,24},{20,28},{24,16},{28,20},{1,9},{5... | collective-permute-start | bytes 3538952 | tf_op jit(solution)/shard_map/ppermute | solution.py:56
  205.2 80.5 %collective-permute-start.24 = (bf16[768,768]{1,0:T(8,128)(2,1)}, bf16[768,768]{1,0:T(8,128)(2,1)S(1)}, u32[]{:S(2)}, u32[]{:S(2)}) collective-permute-start(bf16[768,768]{1,0:T(8,128)(2,1)} %pad_maximum_fusion.13.refs_0_), channel_id=1, source_target_pairs={{0,16},{4,20},{8,24},{12,28},{16,0},{20,4},{24,8},{28,12},{1,17},{... | collective-permute-start | bytes 3538952 | tf_op jit(solution)/shard_map/ppermute | solution.py:56
  206.8 78.9 %collective-permute-start.25 = (bf16[768,768]{1,0:T(8,128)(2,1)}, bf16[768,768]{1,0:T(8,128)(2,1)S(1)}, u32[]{:S(2)}, u32[]{:S(2)}) collective-permute-start(bf16[768,768]{1,0:T(8,128)(2,1)} %pad_maximum_fusion.13.refs_0_), channel_id=1, source_target_pairs={{0,24},{4,28},{8,16},{12,20},{16,8},{20,12},{24,0},{28,4},{1,25},{... | collective-permute-start | bytes 3538952 | tf_op jit(solution)/shard_map/ppermute | solution.py:56
  208.7 103.1 %collective-permute-start.11 = (bf16[512,640]{1,0:T(8,128)(2,1)}, bf16[512,640]{1,0:T(8,128)(2,1)S(1)}, u32[]{:S(2)}, u32[]{:S(2)}) collective-permute-start(bf16[512,640]{1,0:T(8,128)(2,1)} %get-tuple-element.52.refs_0_), channel_id=1, source_target_pairs={{0,1},{1,0},{2,3},{3,2},{4,5},{5,4},{6,7},{7,6},{8,9},{9,8},{10,11... | collective-permute-start | bytes 1966088 | tf_op jit(solution)/shard_map/ppermute | solution.py:56
  221.0 90.9 %collective-permute-start.12 = (bf16[512,640]{1,0:T(8,128)(2,1)S(1)}, bf16[512,640]{1,0:T(8,128)(2,1)S(1)}, u32[]{:S(2)}, u32[]{:S(2)}) collective-permute-start(bf16[512,640]{1,0:T(8,128)(2,1)S(1)} %collective-permute-done.10.refs_1_), channel_id=1, source_target_pairs={{0,1},{1,0},{2,3},{3,2},{4,5},{5,4},{6,7},{7,6},{8,9},{9,8},{10,11... | collective-permute-start | bytes 1966088 | tf_op jit(solution)/shard_map/ppermute | solution.py:56
  285.7 74.8 %collective-permute-start.34 = (bf16[512,2048]{1,0:T(8,128)(2,1)}, bf16[512,2048]{1,0:T(8,128)(2,1)}, u32[]{:S(2)}, u32[]{:S(2)}) collective-permute-start(bf16[512,2048]{1,0:T(8,128)(2,1)} %permute_columns.5.refs_10_), channel_id=1, source_target_pairs={{0,1},{1,0},{2,3},{3,2},{4,5},{5,4},{6,7},{7,6},{8,9},{9,8},{10,11... | collective-permute-start | bytes 6291464 | tf_op jit(solution)/shard_map/ppermute | solution.py:56
  285.7 74.1 %collective-permute-start.35 = (bf16[768,768]{1,0:T(8,128)(2,1)}, bf16[768,768]{1,0:T(8,128)(2,1)}, u32[]{:S(2)}, u32[]{:S(2)}) collective-permute-start(bf16[768,768]{1,0:T(8,128)(2,1)} %pad_maximum_fusion.13.refs_0_), channel_id=1, source_target_pairs={{0,4},{4,0},{8,12},{12,8},{16,20},{20,16},{24,28},{28,24},{1,5},{5... | collective-permute-start | bytes 3538952 | tf_op jit(solution)/shard_map/ppermute | solution.py:56
  287.1 75.1 %collective-permute-start.26 = (bf16[768,512]{1,0:T(8,128)(2,1)S(1)}, bf16[768,512]{1,0:T(8,128)(2,1)}, u32[]{:S(2)}, u32[]{:S(2)}) collective-permute-start(bf16[768,512]{1,0:T(8,128)(2,1)S(1)} %pad_maximum_fusion.14.refs_0_), channel_id=1, source_target_pairs={{0,8},{4,12},{8,0},{12,4},{16,24},{20,28},{24,16},{28,20},{1,9},{5... | collective-permute-start | bytes 2359304 | tf_op jit(solution)/shard_map/ppermute | solution.py:56
  311.8 103.5 %collective-permute-start.42 = (bf16[512,2048]{1,0:T(8,128)(2,1)}, bf16[512,2048]{1,0:T(8,128)(2,1)}, u32[]{:S(2)}, u32[]{:S(2)}) collective-permute-start(bf16[512,2048]{1,0:T(8,128)(2,1)} %collective-permute-done.41.refs_10_), channel_id=1, source_target_pairs={{0,1},{1,0},{2,3},{3,2},{4,5},{5,4},{6,7},{7,6},{8,9},{9,8},{10,11... | collective-permute-start | bytes 6291464 | tf_op jit(solution)/shard_map/ppermute | solution.py:56
  362.2 132.0 %collective-permute-start.33 = (bf16[512,2048]{1,0:T(8,128)(2,1)S(1)}, bf16[512,2048]{1,0:T(8,128)(2,1)}, u32[]{:S(2)}, u32[]{:S(2)}) collective-permute-start(bf16[512,2048]{1,0:T(8,128)(2,1)S(1)} %multiply_convert_fusion.1.refs_8_), channel_id=1, source_target_pairs={{0,1},{1,0},{2,3},{3,2},{4,5},{5,4},{6,7},{7,6},{8,9},{9,8},{10,11... | collective-permute-start | bytes 6291464 | tf_op jit(solution)/shard_map/ppermute | solution.py:56
  415.3 77.7 %collective-permute-start.38 = (bf16[768,768]{1,0:T(8,128)(2,1)}, bf16[768,768]{1,0:T(8,128)(2,1)}, u32[]{:S(2)}, u32[]{:S(2)}) collective-permute-start(bf16[768,768]{1,0:T(8,128)(2,1)} %copy-done.59), channel_id=1, source_target_pairs={{0,4},{4,0},{8,12},{12,8},{16,20},{20,16},{24,28},{28,24},{1,5},{5... | collective-permute-start | bytes 3538952 | tf_op jit(solution)/shard_map/ppermute | solution.py:56
  417.7 108.4 %collective-permute-start.40 = (bf16[512,2048]{1,0:T(8,128)(2,1)}, bf16[512,2048]{1,0:T(8,128)(2,1)}, u32[]{:S(2)}, u32[]{:S(2)}) collective-permute-start(bf16[512,2048]{1,0:T(8,128)(2,1)} %collective-permute-done.39.refs_8_), channel_id=1, source_target_pairs={{0,1},{1,0},{2,3},{3,2},{4,5},{5,4},{6,7},{7,6},{8,9},{9,8},{10,11... | collective-permute-start | bytes 6291464 | tf_op jit(solution)/shard_map/ppermute | solution.py:56
  442.4 115.0 %collective-permute-start.29 = (bf16[768,512]{1,0:T(8,128)(2,1)S(1)}, bf16[768,512]{1,0:T(8,128)(2,1)}, u32[]{:S(2)}, u32[]{:S(2)}) collective-permute-start(bf16[768,512]{1,0:T(8,128)(2,1)S(1)} %pad_maximum_fusion.14.refs_0_), channel_id=1, source_target_pairs={{0,4},{4,0},{8,12},{12,8},{16,20},{20,16},{24,28},{28,24},{1,5},{5... | collective-permute-start | bytes 2359304 | tf_op jit(solution)/shard_map/ppermute | solution.py:56
  467.7 89.7 %collective-permute-start.30 = (bf16[768,512]{1,0:T(8,128)(2,1)}, bf16[768,512]{1,0:T(8,128)(2,1)}, u32[]{:S(2)}, u32[]{:S(2)}) collective-permute-start(bf16[768,512]{1,0:T(8,128)(2,1)} %collective-permute-done.26.refs_1_), channel_id=1, source_target_pairs={{0,4},{4,0},{8,12},{12,8},{16,20},{20,16},{24,28},{28,24},{1,5},{5... | collective-permute-start | bytes 2359304 | tf_op jit(solution)/shard_map/ppermute | solution.py:56
  623.9 185.4 %collective-permute-start.66 = (bf16[1024,768]{0,1:T(8,128)(2,1)S(1)}, bf16[1024,768]{0,1:T(8,128)(2,1)}, u32[]{:S(2)}, u32[]{:S(2)}) collective-permute-start(bf16[1024,768]{0,1:T(8,128)(2,1)S(1)} %fusion.47), channel_id=1, source_target_pairs={{0,4},{4,0},{8,12},{12,8},{16,20},{20,16},{24,28},{28,24},{1,5},{5... | collective-permute-start | bytes 4718600 | tf_op jit(solution)/shard_map/ppermute | solution.py:56
  628.3 73.1 %collective-permute-start.78 = (bf16[1024,512]{0,1:T(8,128)(2,1)}, bf16[1024,512]{0,1:T(8,128)(2,1)S(1)}, u32[]{:S(2)}, u32[]{:S(2)}) collective-permute-start(bf16[1024,512]{0,1:T(8,128)(2,1)} %fusion.65), channel_id=1, source_target_pairs={{0,4},{4,0},{8,12},{12,8},{16,20},{20,16},{24,28},{28,24},{1,5},{5... | collective-permute-start | bytes 3145736 | tf_op jit(solution)/shard_map/ppermute | solution.py:56
  634.1 182.8 %collective-permute-start.74 = (bf16[1024,768]{0,1:T(8,128)(2,1)}, bf16[1024,768]{0,1:T(8,128)(2,1)S(1)}, u32[]{:S(2)}, u32[]{:S(2)}) collective-permute-start(bf16[1024,768]{0,1:T(8,128)(2,1)} %fusion.50), channel_id=1, source_target_pairs={{0,4},{4,0},{8,12},{12,8},{16,20},{20,16},{24,28},{28,24},{1,5},{5... | collective-permute-start | bytes 4718600 | tf_op jit(solution)/shard_map/ppermute | solution.py:56
  647.1 108.5 %collective-permute-start.86 = (bf16[1024,512]{0,1:T(8,128)(2,1)S(1)}, bf16[1024,512]{0,1:T(8,128)(2,1)S(1)}, u32[]{:S(2)}, u32[]{:S(2)}) collective-permute-start(bf16[1024,512]{0,1:T(8,128)(2,1)S(1)} %fusion.68), channel_id=1, source_target_pairs={{0,4},{4,0},{8,12},{12,8},{16,20},{20,16},{24,28},{28,24},{1,5},{5... | collective-permute-start | bytes 3145736 | tf_op jit(solution)/shard_map/ppermute | solution.py:56
  650.9 110.1 %collective-permute-start.73 = (bf16[256,512]{0,1:T(8,128)(2,1)S(1)}, bf16[256,512]{0,1:T(8,128)(2,1)S(1)}, u32[]{:S(2)}, u32[]{:S(2)}) collective-permute-start(bf16[256,512]{0,1:T(8,128)(2,1)S(1)} %get-tuple-element.153), channel_id=1, source_target_pairs={{0,24},{4,28},{8,16},{12,20},{16,8},{20,12},{24,0},{28,4},{1,25},{... | collective-permute-start | bytes 786440 | tf_op jit(solution)/shard_map/ppermute | solution.py:56
  807.9 81.8 %collective-permute-start.46 = (bf16[512,2048]{1,0:T(8,128)(2,1)}, bf16[512,2048]{1,0:T(8,128)(2,1)S(1)}, u32[]{:S(2)}, u32[]{:S(2)}) collective-permute-start(bf16[512,2048]{1,0:T(8,128)(2,1)} %slice.300), channel_id=1, source_target_pairs={{0,1},{1,0},{2,3},{3,2},{4,5},{5,4},{6,7},{7,6},{8,9},{9,8},{10,11... | collective-permute-start | bytes 6291464 | tf_op jit(solution)/shard_map/ppermute | solution.py:56
  809.4 85.1 %collective-permute-start.43 = (bf16[512,2048]{1,0:T(8,128)(2,1)}, bf16[512,2048]{1,0:T(8,128)(2,1)}, u32[]{:S(2)}, u32[]{:S(2)}) collective-permute-start(bf16[512,2048]{1,0:T(8,128)(2,1)} %slice.296), channel_id=1, source_target_pairs={{0,1},{1,0},{2,3},{3,2},{4,5},{5,4},{6,7},{7,6},{8,9},{9,8},{10,11... | collective-permute-start | bytes 6291464 | tf_op jit(solution)/shard_map/ppermute | solution.py:56
  886.0 92.2 %collective-permute-start.77 = (bf16[256,768]{0,1:T(8,128)(2,1)}, bf16[256,768]{0,1:T(8,128)(2,1)S(1)}, u32[]{:S(2)}, u32[]{:S(2)}) collective-permute-start(bf16[256,768]{0,1:T(8,128)(2,1)} %get-tuple-element.137), channel_id=1, source_target_pairs={{0,24},{4,28},{8,16},{12,20},{16,8},{20,12},{24,0},{28,4},{1,25},{... | collective-permute-start | bytes 1179656 | tf_op jit(solution)/shard_map/ppermute | solution.py:56
  889.7 90.8 %collective-permute-start.76 = (bf16[256,768]{0,1:T(8,128)(2,1)}, bf16[256,768]{0,1:T(8,128)(2,1)S(1)}, u32[]{:S(2)}, u32[]{:S(2)}) collective-permute-start(bf16[256,768]{0,1:T(8,128)(2,1)} %get-tuple-element.138), channel_id=1, source_target_pairs={{0,16},{4,20},{8,24},{12,28},{16,0},{20,4},{24,8},{28,12},{1,17},{... | collective-permute-start | bytes 1179656 | tf_op jit(solution)/shard_map/ppermute | solution.py:56
  890.0 92.6 %collective-permute-start.75 = (bf16[256,768]{0,1:T(8,128)(2,1)}, bf16[256,768]{0,1:T(8,128)(2,1)}, u32[]{:S(2)}, u32[]{:S(2)}) collective-permute-start(bf16[256,768]{0,1:T(8,128)(2,1)} %get-tuple-element.136), channel_id=1, source_target_pairs={{0,8},{4,12},{8,0},{12,4},{16,24},{20,28},{24,16},{28,20},{1,9},{5... | collective-permute-start | bytes 1179656 | tf_op jit(solution)/shard_map/ppermute | solution.py:56
  894.5 89.6 %collective-permute-start.85 = (bf16[256,768]{0,1:T(8,128)(2,1)}, bf16[256,768]{0,1:T(8,128)(2,1)}, u32[]{:S(2)}, u32[]{:S(2)}) collective-permute-start(bf16[256,768]{0,1:T(8,128)(2,1)} %get-tuple-element.134), channel_id=1, source_target_pairs={{0,24},{4,28},{8,16},{12,20},{16,8},{20,12},{24,0},{28,4},{1,25},{... | collective-permute-start | bytes 1179656 | tf_op jit(solution)/shard_map/ppermute | solution.py:56
  1044.0 133.5 %collective-permute-start.59 = (bf16[2048,320]{0,1:T(8,128)(2,1)}, bf16[2048,320]{0,1:T(8,128)(2,1)S(1)}, u32[]{:S(2)}, u32[]{:S(2)}) collective-permute-start(bf16[2048,320]{0,1:T(8,128)(2,1)} %convolution_convert_fusion.4), channel_id=1, source_target_pairs={{0,1},{1,0},{2,3},{3,2},{4,5},{5,4},{6,7},{7,6},{8,9},{9,8},{10,11... | collective-permute-start | bytes 3932168 | tf_op jit(solution)/shard_map/ppermute | solution.py:56
  1055.5 127.1 %collective-permute-start.52 = (bf16[2048,480]{0,1:T(8,128)(2,1)}, bf16[2048,480]{0,1:T(8,128)(2,1)}, u32[]{:S(2)}, u32[]{:S(2)}) collective-permute-start(bf16[2048,480]{0,1:T(8,128)(2,1)} %convolution_convert_fusion.2), channel_id=1, source_target_pairs={{0,1},{1,0},{2,3},{3,2},{4,5},{5,4},{6,7},{7,6},{8,9},{9,8},{10,11... | collective-permute-start | bytes 5898248 | tf_op jit(solution)/shard_map/ppermute | solution.py:56
  1069.0 113.5 %collective-permute-start.54 = (bf16[2048,480]{0,1:T(8,128)(2,1)}, bf16[2048,480]{0,1:T(8,128)(2,1)}, u32[]{:S(2)}, u32[]{:S(2)}) collective-permute-start(bf16[2048,480]{0,1:T(8,128)(2,1)} %add_convert_fusion.2), channel_id=1, source_target_pairs={{0,2},{1,3},{2,0},{3,1},{4,6},{5,7},{6,4},{7,5},{8,10},{9,11},{10,... | collective-permute-start | bytes 5898248 | tf_op jit(solution)/shard_map/ppermute | solution.py:56
  1069.6 107.9 %collective-permute-start.61 = (bf16[2048,320]{0,1:T(8,128)(2,1)}, bf16[2048,320]{0,1:T(8,128)(2,1)}, u32[]{:S(2)}, u32[]{:S(2)}) collective-permute-start(bf16[2048,320]{0,1:T(8,128)(2,1)} %fusion.40), channel_id=1, source_target_pairs={{0,2},{1,3},{2,0},{3,1},{4,6},{5,7},{6,4},{7,5},{8,10},{9,11},{10,... | collective-permute-start | bytes 3932168 | tf_op jit(solution)/shard_map/ppermute | solution.py:56
  (145 other events, 3121.8 us)

commit v2 on v1

v2 whole, which is shorter than its diff:
```python
import math

import jax
import jax.numpy as jnp
import numpy as np
from jax import lax
from jax.experimental import pallas as pl
from jax.experimental.pallas import tpu as pltpu
from jax.sharding import Mesh, PartitionSpec as P

HQ = 20
KVH = 5
HD = 64
GROUP = HQ // KVH
QW = HQ * HD
KVW = KVH * HD
GW = GROUP * HD
LANES = 2 * HD
NEG = -1e30
EPSILON = 1e-06
ROPE_BASE = 10000.0
F32 = jnp.float32
BF16 = jnp.bfloat16
VMEM_LIMIT = 60 << 20


def nn(a, b):
    return lax.dot_general(a, b, (((1,), (0,)), ((), ())), preferred_element_type=F32)


def nt(a, b):
    return lax.dot_general(a, b, (((1,), (1,)), ((), ())), preferred_element_type=F32)


def tn(a, b):
    return lax.dot_general(a, b, (((0,), (0,)), ((), ())), preferred_element_type=F32)


def cost(**_):
    return pl.CostEstimate(flops=1, bytes_accessed=1, transcendentals=0)


def params(limit=VMEM_LIMIT):
    return pltpu.CompilerParams(vmem_limit_bytes=limit)


def after(value, *others):
    return lax.optimization_barrier((value, *others))[0] if others else value


def swap(value, axis, size, mask):
    return lax.ppermute(value, axis, [(i, i ^ mask) for i in range(size)])


class Place:
    def __init__(self, mesh):
        grid = mesh.devices
        self.nd, self.nc = mesh.shape["dp"], mesh.shape["ctx"]
        first = tuple(grid[0, 0].coords)
        bits = [1 << i for i in range(self.nd.bit_length() - 1)]
        far = [b for b in bits if tuple(grid[b, 0].coords)[2] != first[2]]
        self.nf = 1 << len(far)
        self.nn = self.nd // self.nf
        self.far_low = 1 in far
        bits = [1 << i for i in range(self.nc.bit_length() - 1)]
        self.core = [b for b in bits if tuple(grid[0, b].coords) == first]
        self.outer = [b for b in bits if b not in self.core]
        shape = (self.nn, self.nf) if self.far_low else (self.nf, self.nn)
        self.dp = ("near", "far") if self.far_low else ("far", "near")
        self.mesh = Mesh(grid.reshape(*shape, self.nc), (*self.dp, "ctx"))
        combos = [0]
        for bit in self.outer:
            combos = combos + [c | bit for c in combos]
        self.combos = combos
        masks = list(combos)
        for bit in self.core:
            masks = [m for pair in masks for m in (pair, pair | bit)]
        self.masks = masks

    def block(self, far, near):
        return near * self.nf + far if self.far_low else far * self.nn + near

    def cross(self, own, *first):
        held = {m: swap(own, "ctx", self.nc, m) if m else own for m in self.combos}
        for bit in self.core:
            held[bit] = swap(after(own, *first), "ctx", self.nc, bit)
        return held

    def gather(self, held, *hold):
        if not isinstance(held, dict):
            held = self.cross(held)
        held = dict(held)
        for bit in self.core:
            for m in self.combos[1:]:
                held[m | bit] = swap(after(held[m], *hold), "ctx", self.nc, bit)
        return [held[m] for m in self.masks]

    def arrived(self, held):
        return [v for m, v in held.items() if m]

    def exchange(self, blocks):
        return [blocks[0]] + [
            swap(b, "ctx", self.nc, m) for b, m in zip(blocks[1:], self.masks[1:])
        ]

    def scatter_core(self, blocks, kind=BF16):
        came = []
        for bit in self.core:
            kept = {}
            for m in blocks:
                if not m & bit:
                    got = swap(blocks[m | bit].astype(BF16), "ctx", self.nc, bit)
                    came.append(got)
                    kept[m] = combine([blocks[m], got], BF16 if m else kind)[0]
            blocks = kept
        return blocks, came

    def total(self, value):
        for axis, size in (("ctx", self.nc), ("near", self.nn), ("far", self.nf)):
            value = sum([swap(value, axis, size, m) for m in range(1, size)], value)
        return value

    def send_outer(self, blocks):
        return [swap(b, "ctx", self.nc, m) for m, b in blocks.items() if m]


def combine(parts, kind, pieces=1):
    shape = parts[0].shape
    tile = 256 if pieces == 1 and shape[0] % 256 == 0 else shape[0]
    block = (tile, *shape[1:])
    out = (shape[0] // pieces, *shape[1:])
    step = tile // pieces

    def body(*refs):
        part_refs, out_refs = refs[: len(parts)], refs[len(parts) :]
        for i, o in enumerate(out_refs):
            at = slice(i * step, (i + 1) * step)
            value = part_refs[0][at].astype(F32)
            for r in part_refs[1:]:
                value = value + r[at].astype(F32)
            o[...] = value.astype(kind)

    index = lambda i: (i,) + (0,) * (len(shape) - 1)
    return pl.pallas_call(
        body,
        out_shape=[jax.ShapeDtypeStruct(out, kind)] * pieces,
        grid=(shape[0] // tile,),
        in_specs=[pl.BlockSpec(block, index)] * len(parts),
        out_specs=[pl.BlockSpec((step, *shape[1:]), index)] * pieces,
        compiler_params=params(),
        cost_estimate=cost(),
        name="combine",
    )(*parts)


def finish_rows(middles, parts, valid):
    rows, (slots, depth) = len(middles), middles[0].shape

    def body(valid_ref, *refs):
        mid_refs, part_refs, out_ref = refs[:rows], refs[rows:-1], refs[-1]
        step = pl.program_id(0)
        y = mid_refs[0][...]
        for r in range(1, rows):
            y = jnp.where(step >= r, mid_refs[r][...], y)
        for p in part_refs:
            y = y + p[...].astype(F32)
        out_ref[...] = (y * valid_ref[...]).astype(BF16)

    whole = lambda i: (0, 0)
    by_row = lambda i: (i, 0)
    return pl.pallas_call(
        body,
        out_shape=jax.ShapeDtypeStruct((rows * slots, depth), BF16),
        grid=(rows,),
        in_specs=[pl.BlockSpec((slots, 1), by_row)]
        + [pl.BlockSpec((slots, depth), whole)] * rows
        + [pl.BlockSpec((slots, depth), by_row)] * len(parts),
        out_specs=pl.BlockSpec((slots, depth), by_row),
        compiler_params=params(),
        cost_estimate=cost(),
        name="finish_rows",
    )(valid, *middles, *parts)


def finish_grads(own, start, width, previous):
    many, units, block = own.shape

    def body(own_ref, *refs):
        for k in range(many):
            refs[-many + k][...] = own_ref[k].astype(F32).T

    extra = [] if previous is None else list(previous)
    return pl.pallas_call(
        body,
        out_shape=[jax.ShapeDtypeStruct((block, width), F32)] * many,
        grid=(1,),
        in_specs=[pl.BlockSpec((many, units, block), lambda i: (0, 0, 0))]
        + [pl.BlockSpec(memory_space=pl.ANY)] * len(extra),
        out_specs=[pl.BlockSpec((block, units), lambda i: (0, start // units))] * many,
        input_output_aliases={1 + k: k for k in range(len(extra))},
        compiler_params=params(),
        cost_estimate=cost(),
        name="finish_grads",
    )(own, *extra)


def head_stats(x, low):
    return lax.rsqrt(head_mean(x * x, low) + EPSILON)


def head_mean(x, low):
    first = jnp.sum(jnp.where(low, x, 0.0), -1, keepdims=True)
    second = jnp.sum(jnp.where(low, 0.0, x), -1, keepdims=True)
    return jnp.where(low, first, second) * (1.0 / HD)


def lane_masks(rows):
    lane = lax.broadcasted_iota(jnp.int32, (rows, LANES), 1)
    return lane < HD, lax.rem(lane, HD) < HD // 2


def spans(start, stop, width):
    out = []
    while start < stop:
        j = start // width
        end = min(stop, (j + 1) * width)
        out.append((j, start - j * width, end - j * width))
        start = end
    return out


def joined(parts):
    return parts[0] if len(parts) == 1 else jnp.concatenate(parts, 1)


def slot_copies(info_ref, place, w_refs, slots_ref, sem):
    copies = []
    for k, m in enumerate(place.masks):
        block = w_refs[k].shape[2]
        for i in range(place.nd):
            copies.append(
                pltpu.make_async_copy(
                    w_refs[k].at[i],
                    slots_ref.at[info_ref[0] ^ m, :, i * block : (i + 1) * block],
                    sem.at[len(copies)],
                )
            )
    return copies


def load_slots(*args):
    copies = slot_copies(*args)
    for c in copies:
        c.start()
    for c in copies:
        c.wait()


def project(info, place, x, gain, w_cols, qc, kc, qgain, kgain, cosine, sine, rows, slots):
    nc, depth, wc = place.nc, x.shape[1], w_cols[0].shape[-2]
    n = rows * slots

    def body(info_ref, x_ref, gain_ref, qgain_ref, kgain_ref, cos_ref, sin_ref, *refs):
        w_refs, (normed_ref, lin_ref, q_ref, kv_ref, w_ref, sem) = refs[:nc], refs[nc:]

        @pl.when(pl.program_id(0) == 0)
        def _():
            load_slots(info_ref, place, w_refs, w_ref, sem)

        xf = x_ref[...].astype(F32)
        inv = lax.rsqrt(jnp.mean(xf * xf, -1, keepdims=True) + EPSILON)
        normed_ref[...] = (xf * inv * gain_ref[...]).astype(BF16)
        for j in range(nc):
            lin_ref[j] = nt(normed_ref[...], w_ref[j])
        low, front = lane_masks(slots)
        cos, sin = cos_ref[...], sin_ref[...]

        def columns(base, width, start, stop):
            return [lin_ref[j, :, base + a : base + b] for j, a, b in spans(start, stop, width)]

        def turn(v, gain):
            v = v * head_stats(v, low) * gain
            turned = jnp.where(
                front, -pltpu.roll(v, LANES - HD // 2, 1), pltpu.roll(v, HD // 2, 1)
            )
            return v * cos + turned * sin

        for c in range(QW // LANES):
            at = slice(c * LANES, (c + 1) * LANES)
            y = turn(joined(columns(0, qc, at.start, at.stop)), qgain_ref[...])
            q_ref[:, at] = (y * (1.0 / math.sqrt(HD))).astype(BF16)
        for g in range(KVH):
            v = joined(
                columns(qc, kc, g * HD, (g + 1) * HD) + columns(qc + kc, kc, g * HD, (g + 1) * HD)
            )
            y = jnp.where(low, turn(v, kgain_ref[...]), v)
            kv_ref[:, g * LANES : (g + 1) * LANES] = y.astype(BF16)

    whole = lambda r, s: (0, 0)
    by_row = lambda r, s: (r, 0)
    return pl.pallas_call(
        body,
        out_shape=(
            jax.ShapeDtypeStruct((n, depth), BF16),
            jax.ShapeDtypeStruct((nc, n, wc), F32),
            jax.ShapeDtypeStruct((n, QW), BF16),
            jax.ShapeDtypeStruct((n, 2 * KVW), BF16),
        ),
        grid_spec=pltpu.PrefetchScalarGridSpec(
            num_scalar_prefetch=1,
            grid=(rows,),
            in_specs=[
                pl.BlockSpec((slots, depth), by_row),
                pl.BlockSpec((1, depth), whole),
                pl.BlockSpec((1, LANES), whole),
                pl.BlockSpec((1, LANES), whole),
                pl.BlockSpec((slots, LANES), whole),
                pl.BlockSpec((slots, LANES), whole),
            ]
            + [pl.BlockSpec(memory_space=pl.ANY)] * nc,
            out_specs=(
                pl.BlockSpec((slots, depth), by_row),
                pl.BlockSpec((nc, slots, wc), lambda r, s: (0, r, 0)),
                pl.BlockSpec((slots, QW), by_row),
                pl.BlockSpec((slots, 2 * KVW), by_row),
            ),
            scratch_shapes=[
                pltpu.VMEM((nc, wc, depth), BF16),
                pltpu.SemaphoreType.DMA((nc * place.nd,)),
            ],
        ),
        compiler_params=params(),
        cost_estimate=cost(
            flops=2 * n * depth * nc * wc, bytes_accessed=2 * nc * depth * wc, transcendentals=n
        ),
        name="project",
    )(info, x, gain, qgain, kgain, cosine, sine, *w_cols)


def project_back(
    info, place, dq, dkv_parts, lin, x, middle_grad, gain, w_cols, qc, kc, qgain, kgain, cosine, sine, row, slots
):
    nc, depth, wc = place.nc, x.shape[1], w_cols[0].shape[-2]

    def body(
        info_ref, dq_ref, lin_ref, x_ref, mid_ref, gain_ref, qgain_ref, kgain_ref, cos_ref, sin_ref, *refs
    ):
        dkv_refs, refs = refs[: len(dkv_parts)], refs[len(dkv_parts) :]
        w_refs, refs = refs[:nc], refs[nc:]
        out_ref, ga_ref, gq_ref, gk_ref = refs[:4]
        dlin_refs, (w_ref, dqs, dks, dvs, dlin_ref, sem) = refs[4 : 4 + nc], refs[4 + nc :]
        copies = slot_copies(info_ref, place, w_refs, w_ref, sem)
        for c in copies:
            c.start()
        low, front = lane_masks(slots)
        cos, sin = cos_ref[...], sin_ref[...]

        def columns(base, width, start, stop):
            return [lin_ref[j, :, base + a : base + b] for j, a, b in spans(start, stop, width)]

        def back(e, v, gain):
            t = e * sin
            e = e * cos + jnp.where(
                front, pltpu.roll(t, LANES - HD // 2, 1), -pltpu.roll(t, HD // 2, 1)
            )
            inv = head_stats(v, low)
            unit = v * inv
            part = e * unit
            u = e * gain
            return inv * (u - unit * head_mean(u * unit, low)), part

        gq = jnp.zeros((1, LANES), F32)
        for c in range(QW // LANES):
            at = slice(c * LANES, (c + 1) * LANES)
            v = joined(columns(0, qc, at.start, at.stop))
            y, part = back(dq_ref[:, at], v, qgain_ref[...])
            dqs[:, at] = y
            gq = gq + jnp.sum(part, 0, keepdims=True)
        gk = jnp.zeros((1, LANES), F32)
        for g in range(KVH):
            e = dkv_refs[0][:, g * LANES : (g + 1) * LANES].astype(F32)
            for ref in dkv_refs[1:]:
                e = e + ref[:, g * LANES : (g + 1) * LANES].astype(F32)
            v = joined(
                columns(qc, kc, g * HD, (g + 1) * HD) + columns(qc + kc, kc, g * HD, (g + 1) * HD)
            )
            y, part = back(e, v, kgain_ref[...])
            dks[:, g * HD : (g + 1) * HD] = y[:, :HD]
            dvs[:, g * HD : (g + 1) * HD] = e[:, HD:]
            gk = gk + jnp.sum(jnp.where(low, part, 0.0), 0, keepdims=True)
        gq_ref[...] = gq
        gk_ref[...] = gk
        for c in copies:
            c.wait()
        grad = None
        for j in range(nc):
            dlin = jnp.concatenate(
                [
                    dqs[:, j * qc : (j + 1) * qc],
                    dks[:, j * kc : (j + 1) * kc],
                    dvs[:, j * kc : (j + 1) * kc],
                ],
                1,
            )
            dlin_ref[j] = dlin.T.astype(BF16)
            part = nn(dlin.astype(BF16), w_ref[j])
            grad = part if grad is None else grad + part
        for k, m in enumerate(place.masks):
            dlin_refs[k][...] = dlin_ref[info_ref[0] ^ m]
        xf = x_ref[...].astype(F32)
        inv = lax.rsqrt(jnp.mean(xf * xf, -1, keepdims=True) + EPSILON)
        unit = xf * inv
        ga_ref[...] = jnp.sum(grad * unit, 0, keepdims=True)
        u = grad * gain_ref[...]
        back_x = inv * (u - unit * jnp.mean(u * unit, -1, keepdims=True))
        out_ref[...] = (mid_ref[...] + back_x).astype(BF16)

    whole = lambda i, s: (0, 0)
    by_row = lambda i, s: (row, 0)
    return pl.pallas_call(
        body,
        out_shape=(
            jax.ShapeDtypeStruct((slots, depth), BF16),
            jax.ShapeDtypeStruct((1, depth), F32),
            jax.ShapeDtypeStruct((1, LANES), F32),
            jax.ShapeDtypeStruct((1, LANES), F32),
            *([jax.ShapeDtypeStruct((wc, slots), BF16)] * nc),
        ),
        grid_spec=pltpu.PrefetchScalarGridSpec(
            num_scalar_prefetch=1,
            grid=(1,),
            in_specs=[
                pl.BlockSpec((slots, QW), whole),
                pl.BlockSpec((nc, slots, wc), lambda i, s: (0, row, 0)),
                pl.BlockSpec((slots, depth), by_row),
                pl.BlockSpec((slots, depth), by_row),
                pl.BlockSpec((1, depth), whole),
                pl.BlockSpec((1, LANES), whole),
                pl.BlockSpec((1, LANES), whole),
                pl.BlockSpec((slots, LANES), whole),
                pl.BlockSpec((slots, LANES), whole),
            ]
            + [pl.BlockSpec((slots, 2 * KVW), whole)] * len(dkv_parts)
            + [pl.BlockSpec(memory_space=pl.ANY)] * nc,
            out_specs=(
                pl.BlockSpec((slots, depth), whole),
                pl.BlockSpec((1, depth), whole),
                pl.BlockSpec((1, LANES), whole),
                pl.BlockSpec((1, LANES), whole),
                *([pl.BlockSpec((wc, slots), whole)] * nc),
            ),
            scratch_shapes=[
                pltpu.VMEM((nc, wc, depth), BF16),
                pltpu.VMEM((slots, QW), F32),
                pltpu.VMEM((slots, KVW), F32),
                pltpu.VMEM((slots, KVW), F32),
                pltpu.VMEM((nc, wc, slots), BF16),
                pltpu.SemaphoreType.DMA((nc * place.nd,)),
            ],
        ),
        compiler_params=params(),
        cost_estimate=cost(
            flops=2 * slots * depth * nc * wc,
            bytes_accessed=2 * nc * depth * wc,
            transcendentals=slots,
        ),
        name="project_back",
    )(info, dq, lin, x, middle_grad, gain, qgain, kgain, cosine, sine, *dkv_parts, *w_cols)


def fill_bias(bias_ref, info_ref, row, masks, slots):
    place, length = info_ref[0], info_ref[1 + row]
    query = place * slots + lax.broadcasted_iota(jnp.int32, (slots, slots), 1)
    for i, mask in enumerate(masks):
        key = (place ^ mask) * slots + lax.broadcasted_iota(jnp.int32, (slots, slots), 0)
        allowed = (key <= query) & (key < length)
        bias_ref[i * slots : (i + 1) * slots, :] = jnp.where(allowed, 0.0, NEG)


def attend(info, q, kv_pieces, masks, row, slots):
    count = len(masks)
    keys = count * slots

    def body(info_ref, q_ref, *refs):
        kv_refs, (o_ref, ot_ref, lse_ref, bias_ref) = refs[:count], refs[count:]
        live = info_ref[0] * slots < info_ref[1 + row]

        @pl.when(live & (pl.program_id(0) == 0))
        def _():
            fill_bias(bias_ref, info_ref, row, masks, slots)

        @pl.when(jnp.logical_not(live))
        def _():
            o_ref[...] = jnp.zeros_like(o_ref)
            ot_ref[...] = jnp.zeros_like(ot_ref)
            lse_ref[...] = jnp.zeros_like(lse_ref)

        @pl.when(live)
        def _():
            kv = jnp.concatenate([r[...] for r in kv_refs], 0)
            k, v = kv[:, :HD], kv[:, HD:]
            for h in range(GROUP):
                qh = q_ref[:, h * HD : (h + 1) * HD]
                s = nt(k, qh) + bias_ref[...]
                m = jnp.max(s, 0, keepdims=True)
                e = jnp.exp(s - m)
                l = jnp.sum(e, 0, keepdims=True)
                p = (e * (1.0 / l)).astype(BF16)
                o = tn(v, p)
                o_ref[:, h * HD : (h + 1) * HD] = o.T.astype(BF16)
                ot_ref[h * HD : (h + 1) * HD, :] = o.astype(BF16)
                lse_ref[0, h : h + 1, :] = m + jnp.log(l)

    n = slots
    return pl.pallas_call(
        body,
        out_shape=(
            jax.ShapeDtypeStruct((n, QW), BF16),
            jax.ShapeDtypeStruct((QW, n), BF16),
            jax.ShapeDtypeStruct((KVH, GROUP, slots), F32),
        ),
        grid_spec=pltpu.PrefetchScalarGridSpec(
            num_scalar_prefetch=1,
            grid=(KVH,),
            in_specs=[pl.BlockSpec((slots, GW), lambda g, s: (row, g))]
            + [pl.BlockSpec((slots, LANES), lambda g, s: (row, g))] * count,
            out_specs=(
                pl.BlockSpec((slots, GW), lambda g, s: (0, g)),
                pl.BlockSpec((GW, slots), lambda g, s: (g, 0)),
                pl.BlockSpec((1, GROUP, slots), lambda g, s: (g, 0, 0)),
            ),
            scratch_shapes=[pltpu.VMEM((keys, slots), F32)],
        ),
        compiler_params=params(),
        cost_estimate=cost(
            flops=16 * n * keys * QW, bytes_accessed=8 * n * QW, transcendentals=n * keys * HQ
        ),
        name="attend",
    )(info, q, *kv_pieces)


def attend_back(info, q, kv_pieces, do, lse, masks, row, slots):
    count = len(masks)
    keys = count * slots

    def body(info_ref, q_ref, do_ref, lse_ref, *refs):
        kv_refs, dq_ref = refs[:count], refs[count]
        dkv_refs, bias_ref = refs[count + 1 : -1], refs[-1]
        live = info_ref[0] * slots < info_ref[1 + row]

        @pl.when(live & (pl.program_id(0) == 0))
        def _():
            fill_bias(bias_ref, info_ref, row, masks, slots)

        @pl.when(jnp.logical_not(live))
        def _():
            dq_ref[...] = jnp.zeros_like(dq_ref)
            for r in dkv_refs:
                r[...] = jnp.zeros_like(r)

        @pl.when(live)
        def _():
            kv = jnp.concatenate([r[...] for r in kv_refs], 0)
            k, v = kv[:, :HD], kv[:, HD:]
            dk = jnp.zeros((keys, HD), F32)
            dv = jnp.zeros((keys, HD), F32)
            for h in range(GROUP):
                at = slice(h * HD, (h + 1) * HD)
                qh, doh = q_ref[:, at], do_ref[:, at]
                p = jnp.exp(nt(k, qh) + bias_ref[...] - lse_ref[0, h : h + 1, :])
                dp = nt(v, doh)
                delta = jnp.sum(p * dp, 0, keepdims=True)
                ds = (p * (dp - delta)).astype(BF16)
                dv = dv + nn(p.astype(BF16), doh)
                dk = dk + nn(ds, qh)
                dq_ref[:, at] = tn(k, ds).T * (1.0 / math.sqrt(HD))
            both = jnp.concatenate([dk, dv], 1).astype(BF16)
            for i, r in enumerate(dkv_refs):
                r[...] = both[i * slots : (i + 1) * slots, :]

    n = slots
    kv_spec = pl.BlockSpec((slots, LANES), lambda g, s: (row, g))
    q_spec = pl.BlockSpec((slots, GW), lambda g, s: (row, g))
    out_kv = pl.BlockSpec((slots, LANES), lambda g, s: (0, g))
    out_q = pl.BlockSpec((slots, GW), lambda g, s: (0, g))
    return pl.pallas_call(
        body,
        out_shape=(
            jax.ShapeDtypeStruct((n, QW), F32),
            *([jax.ShapeDtypeStruct((n, 2 * KVW), BF16)] * count),
        ),
        grid_spec=pltpu.PrefetchScalarGridSpec(
            num_scalar_prefetch=1,
            grid=(KVH,),
            in_specs=[
                q_spec,
                q_spec,
                pl.BlockSpec((1, GROUP, slots), lambda g, s: (g, 0, 0)),
            ]
            + [kv_spec] * count,
            out_specs=(out_q, *([out_kv] * count)),
            scratch_shapes=[pltpu.VMEM((keys, slots), F32)],
        ),
        compiler_params=params(),
        cost_estimate=cost(
            flops=40 * n * keys * QW, bytes_accessed=16 * n * QW, transcendentals=n * keys * HQ
        ),
        name="attend_back",
    )(info, q, do, lse, *kv_pieces)


def out_project(info, place, mixed, x, gain, w_cols, row):
    nc, depth, oc = place.nc, x.shape[1], w_cols[0].shape[-2]
    slots = mixed.shape[0]
    td = 256

    def body(info_ref, mixed_ref, x_ref, gain_ref, *refs):
        w_refs, (mid_ref, n2_ref, w_ref, sem) = refs[:nc], refs[nc:]
        load_slots(info_ref, place, w_refs, w_ref, sem)
        parts = [mixed_ref[:, j * oc : (j + 1) * oc] for j in range(nc)]
        square = jnp.zeros((slots, 1), F32)
        for d in range(depth // td):
            at = slice(d * td, (d + 1) * td)
            y = x_ref[:, at].astype(F32)
            for j in range(nc):
                y = y + nn(parts[j], w_ref[j, :, at])
            mid_ref[:, at] = y
            square = square + jnp.sum(y * y, -1, keepdims=True)
        inv = lax.rsqrt(square * (1.0 / depth) + EPSILON)
        n2_ref[...] = (mid_ref[...] * inv * gain_ref[...]).astype(BF16)

    whole = lambda i, s: (0, 0)
    return pl.pallas_call(
        body,
        out_shape=(
            jax.ShapeDtypeStruct((slots, depth), F32),
            jax.ShapeDtypeStruct((slots, depth), BF16),
        ),
        grid_spec=pltpu.PrefetchScalarGridSpec(
            num_scalar_prefetch=1,
            grid=(1,),
            in_specs=[
                pl.BlockSpec((slots, nc * oc), whole),
                pl.BlockSpec((slots, depth), lambda i, s: (row, 0)),
                pl.BlockSpec((1, depth), whole),
            ]
            + [pl.BlockSpec(memory_space=pl.ANY)] * nc,
            out_specs=(pl.BlockSpec((slots, depth), whole), pl.BlockSpec((slots, depth), whole)),
            scratch_shapes=[
                pltpu.VMEM((nc, oc, depth), BF16),
                pltpu.SemaphoreType.DMA((nc * place.nd,)),
            ],
        ),
        compiler_params=params(),
        cost_estimate=cost(
            flops=2 * slots * depth * nc * oc, bytes_accessed=4 * nc * depth * oc, transcendentals=0
        ),
        name="out_project",
    )(info, mixed, x, gain, *w_cols)


def middle_back(info, place, parts, middles, bg, gain, w_cols, rows, slots):
    nc, depth, oc, count = place.nc, bg.shape[1], w_cols[0].shape[-2], len(parts)
    n = rows * slots

    def body(info_ref, *refs):
        part_refs, refs = refs[:count], refs[count:]
        mid_refs, refs = refs[:rows], refs[rows:]
        bg_ref, gain_ref, refs = refs[0], refs[1], refs[2:]
        w_refs, (mg_ref, ag_ref, xg_ref, gf_ref, w_ref, sem) = refs[:nc], refs[nc:]
        step = pl.program_id(0)

        @pl.when(step == 0)
        def _():
            load_slots(info_ref, place, w_refs, w_ref, sem)
            gf_ref[...] = jnp.zeros_like(gf_ref)

        grad = part_refs[0][...].astype(F32)
        for p in part_refs[1:]:
            grad = grad + p[...].astype(F32)
        mid = mid_refs[0][...]
        for r in range(1, rows):
            mid = jnp.where(step >= r, mid_refs[r][...], mid)
        inv = lax.rsqrt(jnp.mean(mid * mid, -1, keepdims=True) + EPSILON)
        unit = mid * inv
        gf_ref[...] += jnp.sum(grad * unit, 0, keepdims=True)
        u = grad * gain_ref[...]
        y = bg_ref[...].astype(F32) + inv * (u - unit * jnp.mean(u * unit, -1, keepdims=True))
        mg_ref[...] = y
        ag_ref[...] = y.astype(BF16)
        xg_ref[...] = jnp.concatenate(
            [nt(ag_ref[...], w_ref[j]) for j in range(nc)], 1
        ).astype(BF16)

    whole = lambda i, s: (0, 0)
    by_row = lambda i, s: (i, 0)
    token = pl.BlockSpec((slots, depth), by_row)
    return pl.pallas_call(
        body,
        out_shape=(
            jax.ShapeDtypeStruct((n, depth), F32),
            jax.ShapeDtypeStruct((n, depth), BF16),
            jax.ShapeDtypeStruct((n, nc * oc), BF16),
            jax.ShapeDtypeStruct((1, depth), F32),
        ),
        grid_spec=pltpu.PrefetchScalarGridSpec(
            num_scalar_prefetch=1,
            grid=(rows,),
            in_specs=[token] * count
            + [pl.BlockSpec((slots, depth), whole)] * rows
            + [token, pl.BlockSpec((1, depth), whole)]
            + [pl.BlockSpec(memory_space=pl.ANY)] * nc,
            out_specs=(
                token,
                token,
                pl.BlockSpec((slots, nc * oc), by_row),
                pl.BlockSpec((1, depth), whole),
            ),
            scratch_shapes=[
                pltpu.VMEM((nc, oc, depth), BF16),
                pltpu.SemaphoreType.DMA((nc * place.nd,)),
            ],
        ),
        compiler_params=params(),
        cost_estimate=cost(
            flops=2 * n * depth * nc * oc, bytes_accessed=20 * n * depth, transcendentals=0
        ),
        name="middle_back",
    )(info, *parts, *middles, bg, gain, *w_cols)


def feed_forward(info, place, weights, n2, bg, sums, acts, total, first, last):
    owners, (tokens, depth), units = len(n2), bg[0].shape, weights.shape[1]
    cuts = len(n2[0])
    part = tokens // cuts
    block = depth // place.nd
    tu = 256 if units % 256 == 0 else units
    td = 256
    sum_type = BF16 if last else F32
    has_sums, has_acts = sums is not None, acts is not None

    def body(info_ref, w_ref, *refs):
        n2_refs, refs = refs[: owners * cuts], refs[owners * cuts :]
        bg_refs, refs = refs[:owners], refs[owners:]
        sum_refs = ()
        if has_sums:
            sum_refs, refs = refs[: 2 * owners], refs[2 * owners :]
        if has_acts:
            refs = refs[3:]
        out_refs, refs = refs[: 2 * owners], refs[2 * owners :]
        ht_ref, ggt_ref, ugt_ref, wg, wu, wd, acts_buf, tok_buf, out_buf = refs[:9]
        w_sem, tok_sem, out_sem = refs[9:12]
        in_buf, in_sem = refs[12:] if has_sums else (None, None)
        step = pl.program_id(0)
        slot = lax.rem(step, 2)

        def token_copies(p, to):
            found = [
                pltpu.make_async_copy(
                    n2_refs[p * cuts + i],
                    tok_buf.at[to, 0, i * part : (i + 1) * part, :],
                    tok_sem.at[to, i],
                )
                for i in range(cuts)
            ]
            return found + [
                pltpu.make_async_copy(bg_refs[p], tok_buf.at[to, 1], tok_sem.at[to, cuts])
            ]

        def sum_copies(p):
            return [
                pltpu.make_async_copy(sum_refs[2 * p + k], in_buf.at[k], in_sem.at[k])
                for k in range(2)
            ]

        def out_copies(p):
            return [
                pltpu.make_async_copy(out_buf.at[k], out_refs[2 * p + k], out_sem.at[k])
                for k in range(2)
            ]

        @pl.when(step == 0)
        def _():
            for c in token_copies(0, 0):
                c.start()
            copies = []
            for i in range(place.nd):
                for j, dst in enumerate((wg, wu, wd)):
                    start = (3 * i + j) * block
                    copies.append(
                        pltpu.make_async_copy(
                            w_ref.at[start : start + block, :],
                            dst.at[i * block : (i + 1) * block, :],
                            w_sem.at[len(copies)],
                        )
                    )
            for c in copies:
                c.start()
            for c in copies:
                c.wait()

        for p in range(owners):

            @pl.when(step == p)
            def _():
                if p + 1 < owners:
                    for c in token_copies(p + 1, (p + 1) % 2):
                        c.start()
                if has_sums:
                    for c in sum_copies(p):
                        c.start()

        for c in token_copies(0, slot):
            c.wait()
        x, b = tok_buf[slot, 0], tok_buf[slot, 1]
        for j in range(units // tu):
            at = slice(j * tu, (j + 1) * tu)
            gate, up = nn(x, wg[:, at]), nn(x, wu[:, at])
            dh = nn(b, wd[:, at])
            sig = 1.0 / (1.0 + jnp.exp(-gate))
            act = gate * sig
            h = act * up
            gg = dh * up * sig * (1.0 + gate * (1.0 - sig))
            ug = dh * act
            for k, (value, ref) in enumerate(((h, ht_ref), (gg, ggt_ref), (ug, ugt_ref))):
                acts_buf[k, :, at] = value.astype(BF16)
                ref[at, :] = value.T.astype(BF16)

        @pl.when(step > 0)
        def _():
            for c in out_copies(0):
                c.wait()

        if has_sums:
            for c in sum_copies(0):
                c.wait()
        h, gg, ug = acts_buf[0], acts_buf[1], acts_buf[2]
        for j in range(depth // td):
            at = slice(j * td, (j + 1) * td)
            values = [nt(h, wd[at, :]), nt(gg, wg[at, :]) + nt(ug, wu[at, :])]
            for k in range(2):
                value = values[k]
                if has_sums:
                    value = value + in_buf[k, :, at]
                out_buf[k, :, at] = value.astype(sum_type)
        for p in range(owners):

            @pl.when(step == p)
            def _():
                for c in out_copies(p):
                    c.start()

        @pl.when(step == owners - 1)
        def _():
            for c in out_copies(0):
                c.wait()

    any_spec = pl.BlockSpec(memory_space=pl.ANY)
    act_spec = pl.BlockSpec((units, tokens), lambda i, s: (0, i + first))
    operands = [weights, *[v for group in n2 for v in group], *bg]
    aliases = {}
    if has_sums:
        operands += [v for pair in sums for v in pair]
    if has_acts:
        for j in range(3):
            aliases[1 + len(operands) + j] = 2 * owners + j
        operands += acts
    n = owners * tokens
    scratch = [pltpu.VMEM((depth, units), BF16)] * 3 + [
        pltpu.VMEM((3, tokens, units), BF16),
        pltpu.VMEM((2, 2, tokens, depth), BF16),
        pltpu.VMEM((2, tokens, depth), sum_type),
        pltpu.SemaphoreType.DMA((3 * place.nd,)),
        pltpu.SemaphoreType.DMA((2, cuts + 1)),
        pltpu.SemaphoreType.DMA((2,)),
    ]
    if has_sums:
        scratch += [pltpu.VMEM((2, tokens, depth), F32), pltpu.SemaphoreType.DMA((2,))]
    out = pl.pallas_call(
        body,
        out_shape=(
            *([jax.ShapeDtypeStruct((tokens, depth), sum_type)] * (2 * owners)),
            *([jax.ShapeDtypeStruct((units, total), BF16)] * 3),
        ),
        grid_spec=pltpu.PrefetchScalarGridSpec(
            num_scalar_prefetch=1,
            grid=(owners,),
            in_specs=[any_spec] * len(operands),
            out_specs=(*([any_spec] * (2 * owners)), act_spec, act_spec, act_spec),
            scratch_shapes=scratch,
        ),
        input_output_aliases=aliases,
        compiler_params=params(),
        cost_estimate=cost(
            flops=12 * n * depth * units, bytes_accessed=16 * n * depth, transcendentals=n * units
        ),
        name="feed_forward",
    )(info, *operands)
    return [list(out[2 * o : 2 * o + 2]) for o in range(owners)], list(out[2 * owners :])


def weight_grads(order, block, sets, width, added=None, apart=False):
    lefts = [v for left, _ in sets for v in left]
    rights = [v for _, right in sets for group in right for v in group]
    many, blocks = sum(len(right) for _, right in sets), order.shape[0]

    def body(order_ref, *refs):
        left_refs, refs = refs[: len(lefts)], refs[len(lefts) :]
        right_refs, refs = refs[: len(rights)], refs[len(rights) :]
        extra_ref, out_refs = (None, refs) if added is None else (refs[0], refs[1:])
        i = k = at = 0
        for left, right in sets:
            tall = joined_rows([r[...] for r in left_refs[i : i + len(left)]])
            i += len(left)
            wides = []
            for group in right:
                wides.append(joined([r[...] for r in right_refs[at : at + len(group)]]))
                at += len(group)
            values = nn(joined_rows(wides), tall)
            for m in range(len(right)):
                value = values[m * width : (m + 1) * width]
                if added is not None:
                    value = value + extra_ref[0, k].astype(F32)
                if apart:
                    for f in range(blocks):

                        @pl.when(pl.program_id(0) == f)
                        def _():
                            out_refs[f][k] = value.astype(BF16)
                else:
                    out_refs[0][0, k] = value.astype(BF16)
                k += 1

    part = pl.BlockSpec((1, many, width, block), lambda i, ix: (i, 0, 0, 0))
    extra = [] if added is None else [added]
    if apart:
        shapes = [jax.ShapeDtypeStruct((many, width, block), BF16)] * blocks
        specs = [pl.BlockSpec((many, width, block), lambda i, ix: (0, 0, 0))] * blocks
    else:
        shapes = jax.ShapeDtypeStruct((blocks, many, width, block), BF16)
        specs = part
    return pl.pallas_call(
        body,
        out_shape=shapes,
        grid_spec=pltpu.PrefetchScalarGridSpec(
            num_scalar_prefetch=1,
            grid=(blocks,),
            in_specs=[pl.BlockSpec((v.shape[0], block), lambda i, ix: (0, ix[i])) for v in lefts]
            + [pl.BlockSpec((width, v.shape[1]), lambda i, ix: (0, 0)) for v in rights]
            + [part] * len(extra),
            out_specs=specs,
        ),
        compiler_params=params(),
        cost_estimate=cost(),
        name="weight_grads",
    )(order, *lefts, *rights, *extra)


def out_weight_grads(order, place, block, left, rights):
    nc, blocks = place.nc, order.shape[0] - 1
    width = rights[0].shape[0]
    part = width // nc

    def body(order_ref, left_ref, *refs):
        right_refs, refs = refs[: len(rights)], refs[len(rights) :]
        out_refs, value_ref = refs[:nc], refs[nc]
        value_ref[...] = nn(joined([r[...] for r in right_refs]), left_ref[...])
        for k, m in enumerate(place.masks):
            start = pl.multiple_of((order_ref[blocks] ^ m) * part, part & -part)
            out_refs[k][0] = value_ref[pl.ds(start, part), :].astype(BF16)

    return pl.pallas_call(
        body,
        out_shape=[jax.ShapeDtypeStruct((blocks, part, block), BF16)] * nc,
        grid_spec=pltpu.PrefetchScalarGridSpec(
            num_scalar_prefetch=1,
            grid=(blocks,),
            in_specs=[pl.BlockSpec((left.shape[0], block), lambda i, ix: (0, ix[i]))]
            + [pl.BlockSpec(v.shape, lambda i, ix: (0, 0)) for v in rights],
            out_specs=[pl.BlockSpec((1, part, block), lambda i, ix: (i, 0, 0))] * nc,
            scratch_shapes=[pltpu.VMEM((width, block), F32)],
        ),
        compiler_params=params(),
        cost_estimate=cost(),
        name="out_weight_grads",
    )(order, left, *rights)


def joined_rows(parts):
    return parts[0] if len(parts) == 1 else jnp.concatenate(parts, 0)


def rope_tables(positions):
    steps_half = jnp.arange(HD // 2, dtype=F32)
    inverse = jnp.exp(steps_half * (-2.0 * math.log(ROPE_BASE) / HD))
    angles = positions.astype(F32)[:, None] * inverse[None, :]
    return jnp.tile(jnp.cos(angles), (1, 4)), jnp.tile(jnp.sin(angles), (1, 4))


def make_layer(place):
    nd, nc, nf, nn_, masks = place.nd, place.nc, place.nf, place.nn, place.masks
    half = nc // 2

    def per_device(
        layer_input,
        lengths,
        attn_gain,
        w_query,
        w_key,
        w_value,
        query_gain,
        key_gain,
        w_out,
        ffn_gain,
        w_gate,
        w_up,
        w_down,
        cotangent,
    ):
        rows, slots, depth = layer_input.shape
        n = rows * slots
        block = depth // nd
        qc, kc, oc, units = w_query.shape[1], w_key.shape[1], w_out.shape[1], w_gate.shape[1]
        per = rows if slots % LANES == 0 else 1
        far, near = lax.axis_index("far"), lax.axis_index("near")
        spot = lax.axis_index("ctx")
        fars = jnp.arange(nf, dtype=jnp.int32)
        to_near = [place.block(fars, near ^ i) for i in range(nn_)]
        to_near_far = [place.block(far ^ fars, near ^ i) for i in range(nn_)]
        everywhere = jnp.arange(nd, dtype=jnp.int32)
        every = jnp.concatenate([*to_near, spot[None].astype(jnp.int32)], 0)
        positions = spot * slots + jnp.arange(slots, dtype=jnp.int32)
        cosine, sine = rope_tables(positions)
        info = jnp.concatenate([spot[None].astype(jnp.int32), lengths])
        valid = (positions[None, :] < lengths[:, None]).astype(F32).reshape(n, 1)
        qgain2 = jnp.tile(query_gain, 2)[None, :]
        kgain2 = jnp.tile(key_gain, 2)[None, :]
        gain_one, gain_two = attn_gain[None, :], ffn_gain[None, :]
        x = layer_input.reshape(n, depth)

        def gather_dp(value, tiled):
            return lax.all_gather(value, place.dp, axis=0, tiled=tiled)

        bg = (cotangent.reshape(n, depth).astype(F32) * valid).astype(BF16)
        qkv_dp = gather_dp(jnp.concatenate([w_query.T, w_key.T, w_value.T], 0), False)
        qkv_cross = place.cross(
            qkv_dp, bg, info, valid, cosine, sine, qgain2, kgain2, *to_near, every
        )
        qkv_cols = place.gather(qkv_cross)
        out_dp = gather_dp(after(w_out.T, qkv_dp), False)
        out_cross = place.cross(after(out_dp, *place.arrived(qkv_cross)))
        sizes = [512, 512, 256] if units == 1280 else [units]
        starts = [sum(sizes[:c]) for c in range(len(sizes))]
        chunks = []
        for start, size in zip(starts, sizes):
            at = slice(start, start + size)
            local = jnp.concatenate([w_gate[:, at], w_up[:, at], w_down[:, at]], 0)
            chunks.append(gather_dp(after(local, qkv_dp), True))

        normed, lin, q, kv = project(
            info, place, x, gain_one, qkv_cols, qc, kc, qgain2, kgain2, cosine, sine, rows, slots
        )
        out_cols = place.gather(out_cross, q)
        kv_cross = place.cross(kv)
        kv_all = place.gather(kv_cross)
        bg_cross = place.cross(after(bg, *place.arrived(kv_cross)))
        bg_all = place.gather(bg_cross)
        mixed_t, lse, middles, n2_cross = [], [], [], []
        before, due = place.arrived(out_cross), []
        for r in range(rows):
            m, mt, l = attend(info, after(q, *before), kv_all, masks, r, slots)
            if r == rows - 1:
                due = due + place.arrived(bg_cross)
            mid, n2 = out_project(info, place, after(m, *due), x, gain_two, out_cols, r)
            mixed_t.append(mt)
            lse.append(l)
            middles.append(mid)
            before, due = [mid], []
            if per == rows:
                n2_cross.append(place.cross(n2))
                due = place.arrived(n2_cross[-1])
            else:
                n2_cross.append(n2)
        if per != rows:
            n2_cross = [place.cross(jnp.concatenate(n2_cross, 0))]

        sides = {"near": slice(0, half), "far": slice(half, nc)}
        sums = {"near": None, "far": None}
        ffn_grads, last_out = [], []
        n2_near = [[c[m] for c in n2_cross] for m in masks[:half] if m in n2_cross[0]]
        n2_all = None

        def whole(sets, size):
            part = weight_grads(after(everywhere, *last_out), block, sets, size)
            own = lax.psum_scatter(
                part.reshape(nd * 3 * size, block), place.dp, scatter_dimension=0, tiled=True
            )
            ffn_grads.append(own.reshape(3, size, block))
            return part

        def send(sets, size):
            got = None
            for i in range(1, nn_):
                mine = weight_grads(after(to_near[i], *last_out), block, sets, size)
                part = swap(mine, "near", nn_, i)
                got = part if got is None else got + part
            return mine, (sets, size, got)

        def keep(entry):
            sets, size, got = entry
            part = weight_grads(after(to_near[0], *last_out), block, sets, size, got)
            own = lax.psum_scatter(
                part.reshape(nf * 3 * size, block), "far", scatter_dimension=0, tiled=True
            )
            ffn_grads.append(own.reshape(3, size, block))
            return part

        def scatter_core_of(k, *hold):
            pieces = [after(s[k], *hold) for s in (*sums["near"], *sums["far"])]
            return place.scatter_core(dict(zip(masks, pieces)))

        waiting = []
        for c, weights in enumerate(chunks):
            acts = None
            for side in ("far", "near") if c == len(chunks) - 1 and c else ("near", "far"):
                at = sides[side]
                if n2_all is None and len(n2_near) < half:
                    n2_all = [place.gather(v) for v in n2_cross]
                    n2_all = [[v[i] for v in n2_all] for i in range(nc)]
                sums[side], acts = feed_forward(
                    after(info, *last_out), place, weights, (n2_all or n2_near)[at], bg_all[at],
                    sums[side], acts, nc * n, at.start, c == len(chunks) - 1,
                )
                last_out = [acts[0]]
                if n2_all is None:
                    n2_all = [place.gather(v, acts[0]) for v in n2_cross]
                    n2_all = [[v[i] for v in n2_all] for i in range(nc)]
            h, gg, ug = [[a] for a in acts]
            n2_flat = [v for group in n2_all for v in group]
            sets = [(n2_flat, [gg, ug]), (bg_all, [h])]
            if c == 0:
                normed_cross = place.cross(after(normed, acts[0]))
            if c == 1:
                last_out = last_out + place.arrived(normed_cross)
            if c == len(chunks) - 1:
                grads, _ = scatter_core_of(1)
                grad_parts = [grads[0]] + place.send_outer(grads)
                last_out = last_out + [grads[m] for m in place.combos[1:]]
            if c == 0 or nn_ == 1:
                last_out = [whole(sets, sizes[c])]
            else:
                mine, entry = send(sets, sizes[c])
                waiting.append(entry)
                last_out = [mine]
        normed_got = place.gather(normed_cross, *last_out)

        branches, _ = scatter_core_of(0, *last_out)
        branch_far = [branches[m] for m in place.combos[1:]]
        last_out = last_out + branch_far
        middle_grad, attn_grad, mixed_grad, gf = middle_back(
            after(info, *last_out), place, grad_parts, middles, bg, gain_two, out_cols, rows, slots
        )
        branch_got = place.send_outer({m: after(b, middle_grad) for m, b in branches.items()})
        w_out_all = out_weight_grads(after(every, mixed_grad), place, block, attn_grad, mixed_t)
        w_out_core, _ = place.scatter_core(dict(zip(masks, w_out_all)))
        dqs, cores = [], []
        last_out = [mixed_grad, w_out_all[0]]
        for r in range(rows):
            dq, *dkv = attend_back(
                after(info, *last_out), q, kv_all, mixed_grad, lse[r], masks, r, slots
            )
            dqs.append(dq)
            last_out = [dq]
            if waiting:
                last_out = [keep(waiting.pop(0))]
            if r == 0:
                last_out = last_out + [w_out_core[m] for m in place.combos[1:]]
                w_out_got = place.send_outer({m: after(b, dq) for m, b in w_out_core.items()})
                last_out = last_out + ffn_grads[:1]
            cores.append(place.scatter_core(dict(zip(masks, dkv)), F32))
        dkvs = [[core[0], *place.send_outer(core)] for core, _ in cores]

        out_rows = finish_rows(
            middles, [branches[0], *branch_got], valid
        )
        last_out = last_out + [core[m] for core, _ in cores for m in place.combos[1:]]
        last_out = last_out + ffn_grads[1:2] + branch_got

        input_grads, dlin_got, ga, gq, gk = [], [], [], [], []
        for r in range(rows):
            ig, ga_r, gq_r, gk_r, *dlin = project_back(
                after(info, *last_out), place, dqs[r], dkvs[r], lin, x, middle_grad, gain_one, qkv_cols,
                qc, kc, qgain2, kgain2, cosine, sine, r, slots,
            )
            last_out = [ig, out_rows, *w_out_got]
            input_grads.append(ig)
            dlin_got.append(place.exchange(dlin))
            ga.append(ga_r[0])
            gq.append(gq_r[0])
            gk.append(gk_r[0])
        halves = combine(
            [w_out_core[0], *[after(g, input_grads[0]) for g in w_out_got]], BF16, nn_
        )
        halves = [halves[0]] + [
            swap(h, "near", nn_, i) for i, h in enumerate(halves[1:], 1)
        ]
        w_out_half = combine([halves[0], *[after(h, input_grads[-1]) for h in halves[1:]]], BF16)[0]
        w_out_grad = lax.psum_scatter(
            w_out_half.reshape(nf * oc, block), "far", scatter_dimension=0, tiled=True
        )

        def summed(parts):
            total = parts[0].astype(F32)
            for p in parts[1:]:
                total = total + p.astype(F32)
            return total[0]

        right = [dlin_got[r][i] for i in range(nc) for r in range(rows)]
        if per != rows:
            right = [jnp.concatenate(right, 1)]
        got = None
        for i in reversed(range(nn_)):
            part = weight_grads(
                to_near_far[i], block, [(normed_got, [right])], qc + 2 * kc,
                got if i == 0 else None, i == 0,
            )
            if i:
                part = swap(part, "near", nn_, i)
                got = part if got is None else got + part
        w_qkv_grad = summed([part[0]] + [swap(part[m], "far", nf, m) for m in range(1, nf)])
        gains = place.total(after(jnp.concatenate([sum(ga), gf[0], sum(gq), sum(gk)]), part[0]))
        gq = gains[2 * depth : 2 * depth + LANES]
        gk = gains[2 * depth + LANES :]

        grads = None
        for own, start in zip(ffn_grads, starts):
            grads = finish_grads(own, start, units, grads)
        return (
            out_rows.reshape(rows, slots, depth),
            jnp.stack(input_grads, 0),
            gains[:depth],
            w_qkv_grad[:qc].T,
            w_qkv_grad[qc : qc + kc].T,
            w_qkv_grad[qc + kc :].T,
            gq[:HD] + gq[HD:],
            gk[:HD] + gk[HD:],
            w_out_grad.astype(F32).T,
            gains[depth : 2 * depth],
            grads[0],
            grads[1],
            grads[2],
        )

    return per_device


def solution(mesh):
    place = Place(mesh)
    wide = P(place.dp, "ctx")
    rows = P(place.dp, "ctx", None)
    in_specs = (
        rows, P(place.dp), P(), wide, wide, wide, P(), P(), wide, P(), wide, wide, wide, rows,
    )
    out_specs = (
        rows, rows, P(), wide, wide, wide, P(), P(), wide, P(), wide, wide, wide,
    )
    return jax.shard_map(
        make_layer(place),
        mesh=place.mesh,
        in_specs=in_specs,
        out_specs=out_specs,
        check_vma=False,
    )
```

time: 1250 us -> 822 us (0.66)
  waiting for transfers between devices: 531 us -> 267 us
  Pallas kernels: 235 us -> 459 us
  matrix products: 104 us -> 0 us
  blocking collectives: 90 us -> 0 us
  local copies, waits for them, and re-layouts: 89 us -> 17.9 us
  starting transfers between devices: 110 us -> 39 us
  other arithmetic: 81.9 us -> 12.4 us
  between operations: 2.18 us -> 14.9 us
    ppermute x90 -> x56, waiting for transfers between devices: 531 us -> 215 us  [swap(): return lax.ppermute(value, axis, [(i, i ^ mask) for i in range(size)])]
    pallas_call x10 -> x36, Pallas kernels: 156 us -> 375 us  [the longest x6 148 us: feed_forward(): pl.pallas_call(body, out_shape=(*[jax.ShapeDtypeStruct((tokens, depth), s...]
    dot_general x24 -> x0, matrix products: 104 us -> none  [the longest x20 79.6 us: tn(): lax.dot_general(a, b, (((0,), (0,)), ((), ())), preferred_element_type=F32)]
    psum x1 -> x0, blocking collectives: 90 us -> none  [per_device(): gains = lax.psum(gains, ('dp', 'ctx'))]
    ppermute x90 -> x56, starting transfers between devices: 110 us -> 38.6 us  [swap(): return lax.ppermute(value, axis, [(i, i ^ mask) for i in range(size)])]
    all_gather x0 -> x5, waiting for transfers between devices: none -> 52 us  [gather_dp(): return lax.all_gather(value, place.dp, axis=0, tiled=tiled)]
    unnamed x193 -> x94, local copies, waits for them, and re-layouts: 38.2 us -> 10.5 us
    convert_element_type x7 -> x1, other arithmetic: 19.2 us -> 2.11 us  [per_device(): bg = (cotangent.reshape(n, depth).astype(F32) * valid).astype(BF16)]
  transfers between devices with their start and end apart: 90 -> 65, of which waited for: 29 -> 24; matrix products, arithmetic and copies ran while one was open for 20% -> 2% of each run, Pallas kernels for 15% -> 56%
where the time goes in v2:
time: 822 us; the launch traced here: 810 us
  Pallas kernels  459 us (56%)
  waiting for transfers between devices  267 us (32%)
  starting transfers between devices  39 us (5%)
  local copies, waits for them, and re-layouts  17.9 us (2%)
  between operations  14.9 us (2%)
  other arithmetic  12.4 us (2%)
    ppermute x56, waiting for transfers between devices, swap(): return lax.ppermute(value, axis, [(i, i ^ mask) for i in range(size)])  215 us
    pallas_call x6, Pallas kernels, feed_forward(): pl.pallas_call(body, out_shape=(*[jax.ShapeDtypeStruct((tokens, depth), s...  148 us
    pallas_call x7, Pallas kernels, weight_grads(): pl.pallas_call(body, out_shape=shapes, grid_spec=pltpu.PrefetchScalarGrid...  81.9 us
    all_gather x5, waiting for transfers between devices, gather_dp(): return lax.all_gather(value, place.dp, axis=0, tiled=tiled)  52 us
    pallas_call x2, Pallas kernels, attend_back(): pl.pallas_call(body, out_shape=(jax.ShapeDtypeStruct((n, QW), F32), *[jax...  43.1 us
    pallas_call x2, Pallas kernels, attend(): pl.pallas_call(body, out_shape=(jax.ShapeDtypeStruct((n, QW), BF16), jax....  41.3 us
    ppermute x56, starting transfers between devices, swap(): return lax.ppermute(value, axis, [(i, i ^ mask) for i in range(size)])  38.6 us
    pallas_call x2, Pallas kernels, project_back(): pl.pallas_call(body, out_shape=(jax.ShapeDtypeStruct((slots, depth), BF16...  36.2 us
  transfers between devices with their start and end apart: 65, of which 24 were waited for; matrix products, arithmetic and copies ran while one was open for 2% of the time, Pallas kernels for 56%

profile of v2, /device:TPU:0, one launch (start us, length us, event | category | flops | bytes accessed | tf_op | source)
XLA Modules:
  0.0 810.5 jit_solution(3390342761575164470)
XLA Ops:
  9.1 52.0 %all-gather.14.cloned.1.call-done = bf16[3840,256]{1,0:T(8,128)(2,1)} async-done(((bf16[480,256]{1,0:T(8,128)(2,1)}), bf16[3840,256]{1,0:T(8,128)(2,1)}) %all-gather.14.cloned.1.call-update) | async-done | bytes 1966096 | tf_op jit(solution)/shard_map/all_gather | solution.py:1042
  70.9 37.9 %collective-permute-done.1.refs_2_.refs_4_ = bf16[8,480,256]{2,1,0:T(8,128)(2,1)} collective-permute-done((bf16[8,480,256]{2,1,0:T(8,128)(2,1)}, bf16[8,480,256]{2,1,0:T(8,128)(2,1)}, u32[]{:S(2)}, u32[]{:S(2)}) %collective-permute-start.1) | collective-permute-done | bytes 1966112 | tf_op jit(solution)/shard_map/ppermute | solution.py:52
  113.1 18.9 %project.1 = (bf16[512,2048]{1,0:T(8,128)(2,1)}, f32[4,512,480]{2,1,0:T(8,128)}, bf16[512,1280]{1,0:T(8,128)(2,1)}, bf16[512,640]{1,0:T(8,128)(2,1)}) custom-call(s32[3]{0:T(128)} %pad_add_fusion.info_ref, bf16[512,2048]{1,0:T(8,128)(2,1)} %bitcast.53, f32[1,2048]{1,0:T(1,128)} %bitcast.80, f32[1,128]{1,0:T(1,128)} %broadcast_in_dim_tile.6.qgain_ref, ...), custom_call_target="tpu_custom_call" | custom-call | flops 1 | bytes 1 | tf_op jit(solution)/shard_map/project/pallas_call | solution.py:301
  140.8 13.5 %collective-permute-done.6.refs_2_ = bf16[512,640]{1,0:T(8,128)(2,1)S(1)} collective-permute-done((bf16[512,640]{1,0:T(8,128)(2,1)}, bf16[512,640]{1,0:T(8,128)(2,1)S(1)}, u32[]{:S(2)}, u32[]{:S(2)}) %collective-permute-start.6) | collective-permute-done | bytes 655392 | tf_op jit(solution)/shard_map/ppermute | solution.py:52
  161.1 20.4 %attend.2 = (bf16[256,1280]{1,0:T(8,128)(2,1)}, bf16[1280,256]{1,0:T(8,128)(2,1)}, f32[5,4,256]{2,1,0:T(4,128)}) custom-call(s32[3]{0:T(128)} %pad_add_fusion.info_ref, bf16[512,1280]{1,0:T(8,128)(2,1)} %get-tuple-element.167.q_ref, bf16[512,640]{1,0:T(8,128)(2,1)} %get-tuple-element.163.refs_0_, bf16[512,640]{1,0:T(8,128)(2,1)} %copy-done.8, ...), custom_call_target="tpu_custom_call" | custom-call | flops 1 | bytes 1 | tf_op jit(solution)/shard_map/attend/pallas_call | solution.py:515
  181.4 9.2 %out_project.2 = (f32[256,2048]{1,0:T(8,128)}, bf16[256,2048]{1,0:T(8,128)(2,1)}) custom-call(s32[3]{0:T(128)} %pad_add_fusion.info_ref, bf16[256,1280]{1,0:T(8,128)(2,1)} %get-tuple-element.164.mixed_ref, bf16[512,2048]{1,0:T(8,128)(2,1)} %bitcast.54, f32[1,2048]{1,0:T(1,128)} %bitcast.77, bf16[8,320,256]{2,1,0:T(8,128)(2,1)} %bitcast.61, ...), custom_call_target="tpu_custom_call" | custom-call | flops 1 | bytes 1 | tf_op jit(solution)/shard_map/out_project/pallas_call | solution.py:633
  190.9 20.9 %attend.3 = (bf16[256,1280]{1,0:T(8,128)(2,1)}, bf16[1280,256]{1,0:T(8,128)(2,1)}, f32[5,4,256]{2,1,0:T(4,128)}) custom-call(s32[3]{0:T(128)} %pad_add_fusion.info_ref, bf16[512,1280]{1,0:T(8,128)(2,1)} %get-tuple-element.167.q_ref, bf16[512,640]{1,0:T(8,128)(2,1)} %get-tuple-element.163.refs_0_, bf16[512,640]{1,0:T(8,128)(2,1)} %copy-done.8, ...), custom_call_target="tpu_custom_call" | custom-call | flops 1 | bytes 1 | tf_op jit(solution)/shard_map/attend/pallas_call | solution.py:515
  211.8 12.5 %collective-permute-done.9.refs_0_.refs_4_ = bf16[256,2048]{1,0:T(8,128)(2,1)} collective-permute-done((bf16[256,2048]{1,0:T(8,128)(2,1)}, bf16[256,2048]{1,0:T(8,128)(2,1)}, u32[]{:S(2)}, u32[]{:S(2)}) %collective-permute-start.9) | collective-permute-done | bytes 1048608 | tf_op jit(solution)/shard_map/ppermute | solution.py:52
  224.2 9.2 %out_project.3 = (f32[256,2048]{1,0:T(8,128)}, bf16[256,2048]{1,0:T(8,128)(2,1)}) custom-call(s32[3]{0:T(128)} %pad_add_fusion.info_ref, bf16[256,1280]{1,0:T(8,128)(2,1)} %get-tuple-element.171.mixed_ref, bf16[512,2048]{1,0:T(8,128)(2,1)} %bitcast.55, f32[1,2048]{1,0:T(1,128)} %bitcast.78, bf16[8,320,256]{2,1,0:T(8,128)(2,1)} %bitcast.62, ...), custom_call_target="tpu_custom_call" | custom-call | flops 1 | bytes 1 | tf_op jit(solution)/shard_map/out_project/pallas_call | solution.py:633
  237.4 24.7 %feed_forward.6 = (f32[512,2048]{1,0:T(8,128)}, f32[512,2048]{1,0:T(8,128)}, f32[512,2048]{1,0:T(8,128)}, f32[512,2048]{1,0:T(8,128)}, bf16[512,2048]{1,0:T(8,12...) custom-call(s32[3]{0:T(128)} %pad_add_fusion.info_ref, ...), custom_call_target="tpu_custom_call" | custom-call | flops 1 | bytes 1 | tf_op jit(solution)/shard_map/feed_forward/pallas_call | solution.py:879
  266.6 24.9 %feed_forward.7 = (f32[512,2048]{1,0:T(8,128)}, f32[512,2048]{1,0:T(8,128)}, f32[512,2048]{1,0:T(8,128)}, f32[512,2048]{1,0:T(8,128)}, bf16[512,2048]{1,0:T(8,12...) custom-call(s32[3]{0:T(128)} %pad_add_fusion.info_ref, ...), custom_call_target="tpu_custom_call", output_to_operand_aliasing={{4}: (8, {}), {5}: (9, {}), {6}: (10, {})} | custom-call | flops 1 | bytes 1 | tf_op jit(solution)/shard_map/feed_forward/pallas_call | solution.py:879
  292.1 21.4 %weight_grads.7 = bf16[8,3,512,256]{3,2,1,0:T(8,128)(2,1)} custom-call(s32[8]{0:T(128)} %iota.25.order_ref, bf16[256,2048]{1,0:T(8,128)(2,1)} %get-tuple-element.169.refs_0_, bf16[256,2048]{1,0:T(8,128)(2,1)} %get-tuple-element.174.refs_1_, bf16[256,2048]{1,0:T(8,128)(2,1)} %copy-done.2, bf16[256,2048]{1,0:T(8,128)(2,1)} %copy-done.3, ...), custom_call_target="tpu_custom_call" | custom-call | flops 1 | bytes 1 | tf_op jit(solution)/shard_map/weight_grads/pallas_call | solution.py:942
  316.5 28.0 %feed_forward.8 = (f32[512,2048]{1,0:T(8,128)}, f32[512,2048]{1,0:T(8,128)}, f32[512,2048]{1,0:T(8,128)}, f32[512,2048]{1,0:T(8,128)}, bf16[512,2048]{1,0:T(8,12...) custom-call(s32[3]{0:T(128)} %pad_add_fusion.info_ref, ...), custom_call_target="tpu_custom_call" | custom-call | flops 1 | bytes 1 | tf_op jit(solution)/shard_map/feed_forward/pallas_call | solution.py:879
  344.5 28.0 %feed_forward.9 = (f32[512,2048]{1,0:T(8,128)}, f32[512,2048]{1,0:T(8,128)}, f32[512,2048]{1,0:T(8,128)}, f32[512,2048]{1,0:T(8,128)}, bf16[512,2048]{1,0:T(8,12...) custom-call(s32[3]{0:T(128)} %pad_add_fusion.info_ref, ...), custom_call_target="tpu_custom_call", output_to_operand_aliasing={{4}: (12, {}), {5}: (13, {}), {6}: (14, {})} | custom-call | flops 1 | bytes 1 | tf_op jit(solution)/shard_map/feed_forward/pallas_call | solution.py:879
  372.5 13.8 %weight_grads.8 = bf16[4,3,512,256]{3,2,1,0:T(8,128)(2,1)} custom-call(s32[4]{0:T(128)} %copy-done.34, bf16[256,2048]{1,0:T(8,128)(2,1)} %get-tuple-element.169.refs_0_, bf16[256,2048]{1,0:T(8,128)(2,1)} %get-tuple-element.174.refs_1_, bf16[256,2048]{1,0:T(8,128)(2,1)} %copy-done.2, bf16[256,2048]{1,0:T(8,128)(2,1)} %copy-done.3, ...), custom_call_target="tpu_custom_call" | custom-call | flops 1 | bytes 1 | tf_op jit(solution)/shard_map/weight_grads/pallas_call | solution.py:942
  386.3 21.2 %feed_forward.10 = (bf16[512,2048]{1,0:T(8,128)(2,1)}, bf16[512,2048]{1,0:T(8,128)(2,1)}, bf16[512,2048]{1,0:T(8,128)(2,1)}, bf16[512,2048]{1,0:T(8,128)(2,1)}, ...) custom-call(s32[3]{0:T(128)} %pad_add_fusion.info_ref, ...), custom_call_target="tpu_custom_call" | custom-call | flops 1 | bytes 1 | tf_op jit(solution)/shard_map/feed_forward/pallas_call | solution.py:879
  409.4 21.4 %feed_forward.11 = (bf16[512,2048]{1,0:T(8,128)(2,1)}, bf16[512,2048]{1,0:T(8,128)(2,1)}, bf16[512,2048]{1,0:T(8,128)(2,1)}, bf16[512,2048]{1,0:T(8,128)(2,1)}, ...) custom-call(s32[3]{0:T(128)} %pad_add_fusion.info_ref, ...), custom_call_target="tpu_custom_call", output_to_operand_aliasing={{4}: (12, {}), {5}: (13, {}), {6}: (14, {})} | custom-call | flops 1 | bytes 1 | tf_op jit(solution)/shard_map/feed_forward/pallas_call | solution.py:879
  434.3 9.2 %weight_grads.9 = bf16[4,3,256,256]{3,2,1,0:T(8,128)(2,1)} custom-call(s32[4]{0:T(128)} %copy-done.34, bf16[256,2048]{1,0:T(8,128)(2,1)} %get-tuple-element.169.refs_0_, bf16[256,2048]{1,0:T(8,128)(2,1)} %get-tuple-element.174.refs_1_, bf16[256,2048]{1,0:T(8,128)(2,1)} %copy-done.2, bf16[256,2048]{1,0:T(8,128)(2,1)} %copy-done.3, ...), custom_call_target="tpu_custom_call" | custom-call | flops 1 | bytes 1 | tf_op jit(solution)/shard_map/weight_grads/pallas_call | solution.py:942
  451.6 40.4 %collective-permute-done.24.refs_1_ = bf16[512,2048]{1,0:T(8,128)(2,1)} collective-permute-done((bf16[512,2048]{1,0:T(8,128)(2,1)}, bf16[512,2048]{1,0:T(8,128)(2,1)}, u32[]{:S(2)}, u32[]{:S(2)}) %collective-permute-start.24) | collective-permute-done | bytes 2097184 | tf_op jit(solution)/shard_map/ppermute | solution.py:52
  492.1 15.3 %middle_back.1 = (f32[512,2048]{1,0:T(8,128)}, bf16[512,2048]{1,0:T(8,128)(2,1)}, bf16[512,1280]{1,0:T(8,128)(2,1)}, f32[1,2048]{1,0:T(1,128)}) custom-call(s32[3]{0:T(128)} %pad_add_fusion.info_ref, bf16[512,2048]{1,0:T(8,128)(2,1)} %combine.15.refs_0_, bf16[512,2048]{1,0:T(8,128)(2,1)} %collective-permute-done.24.refs_1_, ...), custom_call_target="tpu_custom_call" | custom-call | flops 1 | bytes 1 | tf_op jit(solution)/shard_map/middle_back/pallas_call | solution.py:698
  507.3 9.2 %out_weight_grads.1 = (bf16[8,320,256]{2,1,0:T(8,128)(2,1)}, bf16[8,320,256]{2,1,0:T(8,128)(2,1)}, bf16[8,320,256]{2,1,0:T(8,128)(2,1)}, bf16[8,320,256]{2,1,0:T(8,128)(2,1)}) custom-call(s32[9]{0:T(128)} %pad_add_fusion.1.order_ref, bf16[512,2048]{1,0:T(8,128)(2,1)} %get-tuple-element.240.left_ref, bf16[1280,256]{1,0:T(8,128)(2,1)} %get-tuple-element.241.refs_0_, ...), custom_call_target="tpu_custom_call" | custom-call | flops 1 | bytes 1 | tf_op jit(solution)/shard_map/out_weight_grads/pallas_call | solution.py:972
  516.5 21.5 %attend_back.2 = (f32[256,1280]{1,0:T(8,128)}, bf16[256,640]{1,0:T(8,128)(2,1)}, bf16[256,640]{1,0:T(8,128)(2,1)}, bf16[256,640]{1,0:T(8,128)(2,1)}, bf16[256,640]{1,0:T(8,128)(2,1)}) custom-call(s32[3]{0:T(128)} %pad_add_fusion.info_ref, bf16[512,1280]{1,0:T(8,128)(2,1)} %get-tuple-element.167.q_ref, bf16[512,1280]{1,0:T(8,128)(2,1)} %get-tuple-element.238.do_ref, ...), custom_call_target="tpu_custom_call" | custom-call | flops 1 | bytes 1 | tf_op jit(solution)/shard_map/attend_back/pallas_call | solution.py:586
  538.1 13.5 %weight_grads.10 = bf16[4,3,512,256]{3,2,1,0:T(8,128)(2,1)} custom-call(s32[4]{0:T(128)} %copy-done.35, bf16[256,2048]{1,0:T(8,128)(2,1)} %get-tuple-element.169.refs_0_, bf16[256,2048]{1,0:T(8,128)(2,1)} %get-tuple-element.174.refs_1_, bf16[256,2048]{1,0:T(8,128)(2,1)} %copy-done.2, bf16[256,2048]{1,0:T(8,128)(2,1)} %copy-done.3, ...), custom_call_target="tpu_custom_call" | custom-call | flops 1 | bytes 1 | tf_op jit(solution)/shard_map/weight_grads/pallas_call | solution.py:942
  560.9 27.8 %collective-permute-done.28.refs_15_ = bf16[4,3,256,256]{3,2,1,0:T(8,128)(2,1)} collective-permute-done((bf16[4,3,256,256]{3,2,1,0:T(8,128)(2,1)S(1)}, bf16[4,3,256,256]{3,2,1,0:T(8,128)(2,1)}, u32[]{:S(2)}, u32[]{:S(2)}) %collective-permute-start.28) | collective-permute-done | bytes 1572896 | tf_op jit(solution)/shard_map/ppermute | solution.py:52
  588.7 21.6 %attend_back.3 = (f32[256,1280]{1,0:T(8,128)}, bf16[256,640]{1,0:T(8,128)(2,1)}, bf16[256,640]{1,0:T(8,128)(2,1)}, bf16[256,640]{1,0:T(8,128)(2,1)}, bf16[256,640]{1,0:T(8,128)(2,1)}) custom-call(s32[3]{0:T(128)} %pad_add_fusion.info_ref, bf16[512,1280]{1,0:T(8,128)(2,1)} %get-tuple-element.167.q_ref, bf16[512,1280]{1,0:T(8,128)(2,1)} %get-tuple-element.238.do_ref, ...), custom_call_target="tpu_custom_call" | custom-call | flops 1 | bytes 1 | tf_op jit(solution)/shard_map/attend_back/pallas_call | solution.py:586
  620.4 9.6 %weight_grads.11 = bf16[4,3,256,256]{3,2,1,0:T(8,128)(2,1)} custom-call(s32[4]{0:T(128)} %copy-done.35, bf16[256,2048]{1,0:T(8,128)(2,1)} %get-tuple-element.169.refs_0_, bf16[256,2048]{1,0:T(8,128)(2,1)} %get-tuple-element.174.refs_1_, bf16[256,2048]{1,0:T(8,128)(2,1)} %copy-done.2, bf16[256,2048]{1,0:T(8,128)(2,1)} %copy-done.3, ...), custom_call_target="tpu_custom_call" | custom-call | flops 1 | bytes 1 | tf_op jit(solution)/shard_map/weight_grads/pallas_call | solution.py:942
  636.9 18.0 %project_back.2 = (bf16[256,2048]{1,0:T(8,128)(2,1)}, f32[1,2048]{1,0:T(1,128)}, f32[1,128]{1,0:T(1,128)}, f32[1,128]{1,0:T(1,128)}, bf16[480,256]{1,0:T(8,128)(...) custom-call(s32[3]{0:T(128)} %pad_add_fusion.info_ref, ...), custom_call_target="tpu_custom_call" | custom-call | flops 1 | bytes 1 | tf_op jit(solution)/shard_map/project_back/pallas_call | solution.py:420
  675.4 18.2 %project_back.3 = (bf16[256,2048]{1,0:T(8,128)(2,1)}, f32[1,2048]{1,0:T(1,128)}, f32[1,128]{1,0:T(1,128)}, f32[1,128]{1,0:T(1,128)}, bf16[480,256]{1,0:T(8,128)(...) custom-call(s32[3]{0:T(128)} %pad_add_fusion.info_ref, ...), custom_call_target="tpu_custom_call" | custom-call | flops 1 | bytes 1 | tf_op jit(solution)/shard_map/project_back/pallas_call | solution.py:420
  720.8 7.1 weight_grads.12
  730.1 22.1 %collective-permute-done.43.refs_12_ = bf16[4,1,480,256]{3,2,1,0:T(8,128)(2,1)S(1)} collective-permute-done((bf16[4,1,480,256]{3,2,1,0:T(8,128)(2,1)}, bf16[4,1,480,256]{3,2,1,0:T(8,128)(2,1)S(1)}, u32[]{:S(2)}, u32[]{:S(2)}) %collective-permute-start.43) | collective-permute-done | bytes 983072 | tf_op jit(solution)/shard_map/ppermute | solution.py:52
  753.2 7.4 weight_grads.13
  789.0 9.5 %collective-permute-done.52 = bf16[1,480,256]{2,1,0:T(8,128)(2,1)S(1)} collective-permute-done((bf16[1,480,256]{2,1,0:T(8,128)(2,1)S(1)}, bf16[1,480,256]{2,1,0:T(8,128)(2,1)S(1)}, u32[]{:S(2)}, u32[]{:S(2)}) %collective-permute-start.52) | collective-permute-done | bytes 245792 | tf_op jit(solution)/shard_map/ppermute | solution.py:52
  (288 shorter events, 167.6 us)
Async XLA Ops:
  7.2 53.8 %all-gather.14.cloned.1.call-start = ((), (), s32[]{:S(2)}) async-start(), calls=%async_computation.11 | async-start | bytes 2211840 | tf_op jit(solution)/shard_map/all_gather | solution.py:1042
  9.0 99.8 %all-gather.16.cloned.1.call-start = ((), (), s32[]{:S(2)}) async-start(), calls=%async_computation.12 | async-start | bytes 1474560 | tf_op jit(solution)/shard_map/all_gather | solution.py:1042
  61.1 175.3 %all-gather.8.cloned.1.call-start = ((), (), s32[]{:S(2)}) async-start(), calls=%async_computation.4 | async-start | bytes 7077888 | tf_op jit(solution)/shard_map/all_gather | solution.py:1042
  63.6 252.9 %all-gather.10.cloned.1.call-start = ((), (), s32[]{:S(2)}) async-start(), calls=%async_computation.5 | async-start | bytes 7077888 | tf_op jit(solution)/shard_map/all_gather | solution.py:1042
  64.2 322.1 %all-gather.12.cloned.1.call-start = ((), (), s32[]{:S(2)}) async-start(), calls=%async_computation.6 | async-start | bytes 3538944 | tf_op jit(solution)/shard_map/all_gather | solution.py:1042
  64.4 44.4 %collective-permute-start.1 = (bf16[8,480,256]{2,1,0:T(8,128)(2,1)}, bf16[8,480,256]{2,1,0:T(8,128)(2,1)}, u32[]{:S(2)}, u32[]{:S(2)}) collective-permute-start(bf16[8,480,256]{2,1,0:T(8,128)(2,1)} %bitcast.8.refs_0_.refs_2_), channel_id=1, source_target_pairs={{0,2},{1,3},{2,0},{3,1},{4,6},{5,7},{6,4},{7,5},{8,10},{9,11},{10,... | collective-permute-start | bytes 5898248 | tf_op jit(solution)/shard_map/ppermute | solution.py:52
  70.8 38.0 %collective-permute-start = (bf16[8,480,256]{2,1,0:T(8,128)(2,1)}, bf16[8,480,256]{2,1,0:T(8,128)(2,1)}, u32[]{:S(2)}, u32[]{:S(2)}) collective-permute-start(bf16[8,480,256]{2,1,0:T(8,128)(2,1)} %bitcast.8.refs_0_.refs_2_), channel_id=1, source_target_pairs={{0,1},{1,0},{2,3},{3,2},{4,5},{5,4},{6,7},{7,6},{8,9},{9,8},{10,11... | collective-permute-start | bytes 5898248 | tf_op jit(solution)/shard_map/ppermute | solution.py:52
  108.8 32.0 %collective-permute-start.3 = (bf16[8,320,256]{2,1,0:T(8,128)(2,1)}, bf16[8,320,256]{2,1,0:T(8,128)(2,1)}, u32[]{:S(2)}, u32[]{:S(2)}) collective-permute-start(bf16[8,320,256]{2,1,0:T(8,128)(2,1)} %bitcast.60), channel_id=1, source_target_pairs={{0,2},{1,3},{2,0},{3,1},{4,6},{5,7},{6,4},{7,5},{8,10},{9,11},{10,... | collective-permute-start | bytes 3932168 | tf_op jit(solution)/shard_map/ppermute | solution.py:52
  111.2 477.5 %reduce-scatter.5.cloned.1.call-start = ((), (), s32[]{:S(2)}) async-start(), calls=%async_computation.7 | async-start | bytes 7077888 | tf_op jit(solution)/shard_map/reduce_scatter | solution.py:1095
  140.8 40.6 %collective-permute-start.8 = (bf16[8,320,256]{2,1,0:T(8,128)(2,1)}, bf16[8,320,256]{2,1,0:T(8,128)(2,1)}, u32[]{:S(2)}, u32[]{:S(2)}) collective-permute-start(bf16[8,320,256]{2,1,0:T(8,128)(2,1)} %collective-permute-done.3.refs_2_.refs_8_), channel_id=1, source_target_pairs={{0,1},{1,0},{2,3},{3,2},{4,5},{5,4},{6,7},{7,6},{8,9},{9,8},{10,11... | collective-permute-start | bytes 3932168 | tf_op jit(solution)/shard_map/ppermute | solution.py:52
  154.3 69.9 %collective-permute-start.11 = (bf16[512,2048]{1,0:T(8,128)(2,1)S(1)}, bf16[512,2048]{1,0:T(8,128)(2,1)}, u32[]{:S(2)}, u32[]{:S(2)}) collective-permute-start(bf16[512,2048]{1,0:T(8,128)(2,1)S(1)} %fusion.refs_4_.refs_8_), channel_id=1, source_target_pairs={{0,2},{1,3},{2,0},{3,1},{4,6},{5,7},{6,4},{7,5},{8,10},{9,11},{10,... | collective-permute-start | bytes 6291464 | tf_op jit(solution)/shard_map/ppermute | solution.py:52
  155.8 68.4 %collective-permute-start.12 = (bf16[512,2048]{1,0:T(8,128)(2,1)S(1)}, bf16[512,2048]{1,0:T(8,128)(2,1)}, u32[]{:S(2)}, u32[]{:S(2)}) collective-permute-start(bf16[512,2048]{1,0:T(8,128)(2,1)S(1)} %fusion.refs_4_.refs_8_), channel_id=1, source_target_pairs={{0,1},{1,0},{2,3},{3,2},{4,5},{5,4},{6,7},{7,6},{8,9},{9,8},{10,11... | collective-permute-start | bytes 6291464 | tf_op jit(solution)/shard_map/ppermute | solution.py:52
  190.9 33.3 %collective-permute-start.9 = (bf16[256,2048]{1,0:T(8,128)(2,1)}, bf16[256,2048]{1,0:T(8,128)(2,1)}, u32[]{:S(2)}, u32[]{:S(2)}) collective-permute-start(bf16[256,2048]{1,0:T(8,128)(2,1)} %get-tuple-element.169.refs_0_), channel_id=1, source_target_pairs={{0,2},{1,3},{2,0},{3,1},{4,6},{5,7},{6,4},{7,5},{8,10},{9,11},{10,... | collective-permute-start | bytes 3145736 | tf_op jit(solution)/shard_map/ppermute | solution.py:52
  233.5 28.6 %collective-permute-start.14 = (bf16[256,2048]{1,0:T(8,128)(2,1)}, bf16[256,2048]{1,0:T(8,128)(2,1)}, u32[]{:S(2)}, u32[]{:S(2)}) collective-permute-start(bf16[256,2048]{1,0:T(8,128)(2,1)} %get-tuple-element.174.refs_1_), channel_id=1, source_target_pairs={{0,2},{1,3},{2,0},{3,1},{4,6},{5,7},{6,4},{7,5},{8,10},{9,11},{10,... | collective-permute-start | bytes 3145736 | tf_op jit(solution)/shard_map/ppermute | solution.py:52
  235.0 27.6 %collective-permute-start.17 = (bf16[512,2048]{1,0:T(8,128)(2,1)}, bf16[512,2048]{1,0:T(8,128)(2,1)S(1)}, u32[]{:S(2)}, u32[]{:S(2)}) collective-permute-start(bf16[512,2048]{1,0:T(8,128)(2,1)} %collective-permute-done.11.refs_4_.refs_10_), channel_id=1, source_target_pairs={{0,1},{1,0},{2,3},{3,2},{4,5},{5,4},{6,7},{7,6},{8,9},{9,8},{10,11... | collective-permute-start | bytes 6291464 | tf_op jit(solution)/shard_map/ppermute | solution.py:52
  313.5 318.5 %reduce-scatter.7.cloned.1.call-start = ((), (), s32[]{:S(2)}) async-start(), calls=%async_computation.8 | async-start | bytes 3932160 | tf_op jit(solution)/shard_map/reduce_scatter | solution.py:1112
  315.1 57.5 %collective-permute-start.18 = (bf16[512,2048]{1,0:T(8,128)(2,1)S(1)}, bf16[512,2048]{1,0:T(8,128)(2,1)}, u32[]{:S(2)}, u32[]{:S(2)}) collective-permute-start(bf16[512,2048]{1,0:T(8,128)(2,1)S(1)} %copy-done.9), channel_id=1, source_target_pairs={{0,2},{1,3},{2,0},{3,1},{4,6},{5,7},{6,4},{7,5},{8,10},{9,11},{10,... | collective-permute-start | bytes 6291464 | tf_op jit(solution)/shard_map/ppermute | solution.py:52
  316.5 56.0 %collective-permute-start.19 = (bf16[512,2048]{1,0:T(8,128)(2,1)S(1)}, bf16[512,2048]{1,0:T(8,128)(2,1)}, u32[]{:S(2)}, u32[]{:S(2)}) collective-permute-start(bf16[512,2048]{1,0:T(8,128)(2,1)S(1)} %copy-done.9), channel_id=1, source_target_pairs={{0,1},{1,0},{2,3},{3,2},{4,5},{5,4},{6,7},{7,6},{8,9},{9,8},{10,11... | collective-permute-start | bytes 6291464 | tf_op jit(solution)/shard_map/ppermute | solution.py:52
  408.0 130.0 %collective-permute-start.26 = (bf16[4,3,512,256]{3,2,1,0:T(8,128)(2,1)S(1)}, bf16[4,3,512,256]{3,2,1,0:T(8,128)(2,1)}, u32[]{:S(2)}, u32[]{:S(2)}) collective-permute-start(bf16[4,3,512,256]{3,2,1,0:T(8,128)(2,1)S(1)} %copy-done.11), channel_id=1, source_target_pairs={{0,4},{4,0},{1,5},{5,1},{2,6},{6,2},{3,7},{7,3},{8,12},{12,8},{9,1... | collective-permute-start | bytes 9437192 | tf_op jit(solution)/shard_map/ppermute | solution.py:52
  444.1 47.9 %collective-permute-start.24 = (bf16[512,2048]{1,0:T(8,128)(2,1)}, bf16[512,2048]{1,0:T(8,128)(2,1)}, u32[]{:S(2)}, u32[]{:S(2)}) collective-permute-start(bf16[512,2048]{1,0:T(8,128)(2,1)} %combine.12), channel_id=1, source_target_pairs={{0,2},{1,3},{2,0},{3,1},{4,6},{5,7},{6,4},{7,5},{8,10},{9,11},{10,... | collective-permute-start | bytes 6291464 | tf_op jit(solution)/shard_map/ppermute | solution.py:52
  551.6 248.5 %reduce-scatter.9.cloned.1.call-start = ((), (), s32[]{:S(2)}) async-start(), calls=%async_computation.9 | async-start | bytes 819200 | tf_op jit(solution)/shard_map/reduce_scatter | solution.py:1208
  552.9 35.7 %collective-permute-start.28 = (bf16[4,3,256,256]{3,2,1,0:T(8,128)(2,1)S(1)}, bf16[4,3,256,256]{3,2,1,0:T(8,128)(2,1)}, u32[]{:S(2)}, u32[]{:S(2)}) collective-permute-start(bf16[4,3,256,256]{3,2,1,0:T(8,128)(2,1)S(1)} %copy-done.12), channel_id=1, source_target_pairs={{0,4},{4,0},{1,5},{5,1},{2,6},{6,2},{3,7},{7,3},{8,12},{12,8},{9,1... | collective-permute-start | bytes 4718600 | tf_op jit(solution)/shard_map/ppermute | solution.py:52
  553.5 78.5 %collective-permute-start.25 = (bf16[512,2048]{1,0:T(8,128)(2,1)}, bf16[512,2048]{1,0:T(8,128)(2,1)}, u32[]{:S(2)}, u32[]{:S(2)}) collective-permute-start(bf16[512,2048]{1,0:T(8,128)(2,1)} %combine.14), channel_id=1, source_target_pairs={{0,2},{1,3},{2,0},{3,1},{4,6},{5,7},{6,4},{7,5},{8,10},{9,11},{10,... | collective-permute-start | bytes 6291464 | tf_op jit(solution)/shard_map/ppermute | solution.py:52
  554.8 56.2 %collective-permute-start.54 = (bf16[8,320,256]{2,1,0:T(8,128)(2,1)}, bf16[8,320,256]{2,1,0:T(8,128)(2,1)}, u32[]{:S(2)}, u32[]{:S(2)}) collective-permute-start(bf16[8,320,256]{2,1,0:T(8,128)(2,1)} %get-tuple-element.289), channel_id=1, source_target_pairs={{0,1},{1,0},{2,3},{3,2},{4,5},{5,4},{6,7},{7,6},{8,9},{9,8},{10,11... | collective-permute-start | bytes 3932168 | tf_op jit(solution)/shard_map/ppermute | solution.py:52
  555.1 106.6 %collective-permute-start.21 = (bf16[512,2048]{1,0:T(8,128)(2,1)}, bf16[512,2048]{1,0:T(8,128)(2,1)}, u32[]{:S(2)}, u32[]{:S(2)}) collective-permute-start(bf16[512,2048]{1,0:T(8,128)(2,1)} %get-tuple-element.228), channel_id=1, source_target_pairs={{0,1},{1,0},{2,3},{3,2},{4,5},{5,4},{6,7},{7,6},{8,9},{9,8},{10,11... | collective-permute-start | bytes 6291464 | tf_op jit(solution)/shard_map/ppermute | solution.py:52
  556.7 32.0 %collective-permute-start.31 = (bf16[256,640]{1,0:T(8,128)(2,1)}, bf16[256,640]{1,0:T(8,128)(2,1)}, u32[]{:S(2)}, u32[]{:S(2)}) collective-permute-start(bf16[256,640]{1,0:T(8,128)(2,1)} %get-tuple-element.261), channel_id=1, source_target_pairs={{0,1},{1,0},{2,3},{3,2},{4,5},{5,4},{6,7},{7,6},{8,9},{9,8},{10,11... | collective-permute-start | bytes 983048 | tf_op jit(solution)/shard_map/ppermute | solution.py:52
  588.7 66.3 %collective-permute-start.33 = (bf16[8,320,256]{2,1,0:T(8,128)(2,1)}, bf16[8,320,256]{2,1,0:T(8,128)(2,1)S(1)}, u32[]{:S(2)}, u32[]{:S(2)}) collective-permute-start(bf16[8,320,256]{2,1,0:T(8,128)(2,1)} %combine.16), channel_id=1, source_target_pairs={{0,2},{1,3},{2,0},{3,1},{4,6},{5,7},{6,4},{7,5},{8,10},{9,11},{10,... | collective-permute-start | bytes 3932168 | tf_op jit(solution)/shard_map/ppermute | solution.py:52
  611.0 88.2 %collective-permute-start.36 = (bf16[512,2048]{1,0:T(8,128)(2,1)}, bf16[512,2048]{1,0:T(8,128)(2,1)S(1)}, u32[]{:S(2)}, u32[]{:S(2)}) collective-permute-start(bf16[512,2048]{1,0:T(8,128)(2,1)} %collective-permute-done.18.refs_2_), channel_id=1, source_target_pairs={{0,1},{1,0},{2,3},{3,2},{4,5},{5,4},{6,7},{7,6},{8,9},{9,8},{10,11... | collective-permute-start | bytes 6291464 | tf_op jit(solution)/shard_map/ppermute | solution.py:52
  613.4 23.6 %collective-permute-start.32 = (bf16[256,640]{1,0:T(8,128)(2,1)}, bf16[256,640]{1,0:T(8,128)(2,1)}, u32[]{:S(2)}, u32[]{:S(2)}) collective-permute-start(bf16[256,640]{1,0:T(8,128)(2,1)} %combine.17), channel_id=1, source_target_pairs={{0,2},{1,3},{2,0},{3,1},{4,6},{5,7},{6,4},{7,5},{8,10},{9,11},{10,... | collective-permute-start | bytes 983048 | tf_op jit(solution)/shard_map/ppermute | solution.py:52
  659.0 34.5 %collective-permute-start.55 = (bf16[4,320,256]{2,1,0:T(8,128)(2,1)}, bf16[4,320,256]{2,1,0:T(8,128)(2,1)S(1)}, u32[]{:S(2)}, u32[]{:S(2)}) collective-permute-start(bf16[4,320,256]{2,1,0:T(8,128)(2,1)} %get-tuple-element.292), channel_id=1, source_target_pairs={{0,4},{4,0},{1,5},{5,1},{2,6},{6,2},{3,7},{7,3},{8,12},{12,8},{9,1... | collective-permute-start | bytes 1966088 | tf_op jit(solution)/shard_map/ppermute | solution.py:52
  696.7 105.0 %reduce-scatter.11.cloned.1.call-start = ((), (), s32[]{:S(2)}) async-start(), calls=%async_computation.10 | async-start | bytes 1966080 | tf_op jit(solution)/shard_map/reduce_scatter | solution.py:1112
  727.9 24.3 %collective-permute-start.43 = (bf16[4,1,480,256]{3,2,1,0:T(8,128)(2,1)}, bf16[4,1,480,256]{3,2,1,0:T(8,128)(2,1)S(1)}, u32[]{:S(2)}, u32[]{:S(2)}) collective-permute-start(bf16[4,1,480,256]{3,2,1,0:T(8,128)(2,1)} %weight_grads.12), channel_id=1, source_target_pairs={{0,4},{4,0},{1,5},{5,1},{2,6},{6,2},{3,7},{7,3},{8,12},{12,8},{9,1... | collective-permute-start | bytes 2949128 | tf_op jit(solution)/shard_map/ppermute | solution.py:52
  (82 other events, 988.6 us)
Sparse Core Ops, SparseCore 0:
  10.8 50.1 all-gather.13
  63.2 41.1 all-gather.15
  107.2 97.6 all-gather.7
  206.9 97.2 all-gather.9
  306.2 58.6 all-gather.11
  368.3 138.5 reduce-scatter.4
  551.7 59.4 reduce-scatter.6
  696.8 22.5 reduce-scatter.8
  729.6 34.8 reduce-scatter.10

commit v3 on v2

--- a/solution.py
+++ b/solution.py
@@ -116,9 +116,13 @@
         return blocks, came
 
     def total(self, value):
-        for axis, size in (("ctx", self.nc), ("near", self.nn), ("far", self.nf)):
-            value = sum([swap(value, axis, size, m) for m in range(1, size)], value)
-        return value
+        got = [swap(value, "ctx", self.nc, m) for m in range(1, self.nc)]
+        return sum(got, value), got
+
+    def total_dp(self, value, *hold):
+        value = sum([swap(value, "far", self.nf, m) for m in range(1, self.nf)], value)
+        value = after(value, *hold)
+        return sum([swap(value, "near", self.nn, m) for m in range(1, self.nn)], value)
 
     def send_outer(self, blocks):
         return [swap(b, "ctx", self.nc, m) for m, b in blocks.items() if m]
@@ -184,6 +188,7 @@
 
 def finish_grads(own, start, width, previous):
     many, units, block = own.shape
+    tile = 256 if units % 256 == 0 else units
 
     def body(own_ref, *refs):
         for k in range(many):
@@ -193,10 +198,10 @@
     return pl.pallas_call(
         body,
         out_shape=[jax.ShapeDtypeStruct((block, width), F32)] * many,
-        grid=(1,),
-        in_specs=[pl.BlockSpec((many, units, block), lambda i: (0, 0, 0))]
+        grid=(units // tile,),
+        in_specs=[pl.BlockSpec((many, tile, block), lambda i: (0, i, 0))]
         + [pl.BlockSpec(memory_space=pl.ANY)] * len(extra),
-        out_specs=[pl.BlockSpec((block, units), lambda i: (0, start // units))] * many,
+        out_specs=[pl.BlockSpec((block, tile), lambda i: (0, start // tile + i))] * many,
         input_output_aliases={1 + k: k for k in range(len(extra))},
         compiler_params=params(),
         cost_estimate=cost(),
@@ -337,21 +342,13 @@
     )(info, x, gain, qgain, kgain, cosine, sine, *w_cols)
 
 
-def project_back(
-    info, place, dq, dkv_parts, lin, x, middle_grad, gain, w_cols, qc, kc, qgain, kgain, cosine, sine, row, slots
-):
-    nc, depth, wc = place.nc, x.shape[1], w_cols[0].shape[-2]
-
-    def body(
-        info_ref, dq_ref, lin_ref, x_ref, mid_ref, gain_ref, qgain_ref, kgain_ref, cos_ref, sin_ref, *refs
-    ):
+def heads_back(info, place, dq, dkv_parts, lin, qc, kc, qgain, kgain, cosine, sine, row, slots):
+    nc, wc = place.nc, lin.shape[2]
+
+    def body(info_ref, dq_ref, lin_ref, qgain_ref, kgain_ref, cos_ref, sin_ref, *refs):
         dkv_refs, refs = refs[: len(dkv_parts)], refs[len(dkv_parts) :]
-        w_refs, refs = refs[:nc], refs[nc:]
-        out_ref, ga_ref, gq_ref, gk_ref = refs[:4]
-        dlin_refs, (w_ref, dqs, dks, dvs, dlin_ref, sem) = refs[4 : 4 + nc], refs[4 + nc :]
-        copies = slot_copies(info_ref, place, w_refs, w_ref, sem)
-        for c in copies:
-            c.start()
+        out_ref, gq_ref, gk_ref = refs[:3]
+        dlin_refs, (dqs, dks, dvs, dlin_ref) = refs[3 : 3 + nc], refs[3 + nc :]
         low, front = lane_masks(slots)
         cos, sin = cos_ref[...], sin_ref[...]
 
@@ -390,9 +387,6 @@
             gk = gk + jnp.sum(jnp.where(low, part, 0.0), 0, keepdims=True)
         gq_ref[...] = gq
         gk_ref[...] = gk
-        for c in copies:
-            c.wait()
-        grad = None
         for j in range(nc):
             dlin = jnp.concatenate(
                 [
@@ -402,26 +396,19 @@
                 ],
                 1,
             )
+            out_ref[j] = dlin.astype(BF16)
             dlin_ref[j] = dlin.T.astype(BF16)
-            part = nn(dlin.astype(BF16), w_ref[j])
-            grad = part if grad is None else grad + part
         for k, m in enumerate(place.masks):
             dlin_refs[k][...] = dlin_ref[info_ref[0] ^ m]
-        xf = x_ref[...].astype(F32)
-        inv = lax.rsqrt(jnp.mean(xf * xf, -1, keepdims=True) + EPSILON)
-        unit = xf * inv
-        ga_ref[...] = jnp.sum(grad * unit, 0, keepdims=True)
-        u = grad * gain_ref[...]
-        back_x = inv * (u - unit * jnp.mean(u * unit, -1, keepdims=True))
-        out_ref[...] = (mid_ref[...] + back_x).astype(BF16)
 
     whole = lambda i, s: (0, 0)
-    by_row = lambda i, s: (row, 0)
+    cube = lambda i, s: (0, 0, 0)
+    lane = pl.BlockSpec((1, LANES), whole)
+    table = pl.BlockSpec((slots, LANES), whole)
     return pl.pallas_call(
         body,
         out_shape=(
-            jax.ShapeDtypeStruct((slots, depth), BF16),
-            jax.ShapeDtypeStruct((1, depth), F32),
+            jax.ShapeDtypeStruct((nc, slots, wc), BF16),
             jax.ShapeDtypeStruct((1, LANES), F32),
             jax.ShapeDtypeStruct((1, LANES), F32),
             *([jax.ShapeDtypeStruct((wc, slots), BF16)] * nc),
@@ -432,40 +419,87 @@
             in_specs=[
                 pl.BlockSpec((slots, QW), whole),
                 pl.BlockSpec((nc, slots, wc), lambda i, s: (0, row, 0)),
-                pl.BlockSpec((slots, depth), by_row),
-                pl.BlockSpec((slots, depth), by_row),
-                pl.BlockSpec((1, depth), whole),
-                pl.BlockSpec((1, LANES), whole),
-                pl.BlockSpec((1, LANES), whole),
-                pl.BlockSpec((slots, LANES), whole),
-                pl.BlockSpec((slots, LANES), whole),
+                lane,
+                lane,
+                table,
+                table,
             ]
-            + [pl.BlockSpec((slots, 2 * KVW), whole)] * len(dkv_parts)
-            + [pl.BlockSpec(memory_space=pl.ANY)] * nc,
+            + [pl.BlockSpec((slots, 2 * KVW), whole)] * len(dkv_parts),
             out_specs=(
-                pl.BlockSpec((slots, depth), whole),
-                pl.BlockSpec((1, depth), whole),
-                pl.BlockSpec((1, LANES), whole),
-                pl.BlockSpec((1, LANES), whole),
+                pl.BlockSpec((nc, slots, wc), cube),
+                lane,
+                lane,
                 *([pl.BlockSpec((wc, slots), whole)] * nc),
             ),
             scratch_shapes=[
-                pltpu.VMEM((nc, wc, depth), BF16),
                 pltpu.VMEM((slots, QW), F32),
                 pltpu.VMEM((slots, KVW), F32),
                 pltpu.VMEM((slots, KVW), F32),
                 pltpu.VMEM((nc, wc, slots), BF16),
+            ],
+        ),
+        compiler_params=params(),
+        cost_estimate=cost(),
+        name="heads_back",
+    )(info, dq, lin, qgain, kgain, cosine, sine, *dkv_parts)
+
+
+def project_back(info, place, dlins, x, middle_grad, gain, w_cols, rows, slots):
+    nc, depth, wc = place.nc, x.shape[1], w_cols[0].shape[-2]
+
+    def body(info_ref, x_ref, mid_ref, gain_ref, *refs):
+        dlin_refs, refs = refs[:rows], refs[rows:]
+        w_refs, (out_ref, ga_ref, w_ref, sem) = refs[:nc], refs[nc:]
+        step = pl.program_id(0)
+
+        @pl.when(step == 0)
+        def _():
+            load_slots(info_ref, place, w_refs, w_ref, sem)
+            ga_ref[...] = jnp.zeros_like(ga_ref)
+
+        grad = None
+        for j in range(nc):
+            dlin = dlin_refs[0][j]
+            for r in range(1, rows):
+                dlin = jnp.where(step >= r, dlin_refs[r][j], dlin)
+            part = nn(dlin, w_ref[j])
+            grad = part if grad is None else grad + part
+        xf = x_ref[...].astype(F32)
+        inv = lax.rsqrt(jnp.mean(xf * xf, -1, keepdims=True) + EPSILON)
+        unit = xf * inv
+        ga_ref[...] += jnp.sum(grad * unit, 0, keepdims=True)
+        u = grad * gain_ref[...]
+        back_x = inv * (u - unit * jnp.mean(u * unit, -1, keepdims=True))
+        out_ref[...] = (mid_ref[...] + back_x).astype(BF16)
+
+    whole = lambda i, s: (0, 0)
+    by_row = lambda i, s: (i, 0)
+    return pl.pallas_call(
+        body,
+        out_shape=(
+            jax.ShapeDtypeStruct((rows * slots, depth), BF16),
+            jax.ShapeDtypeStruct((1, depth), F32),
+        ),
+        grid_spec=pltpu.PrefetchScalarGridSpec(
+            num_scalar_prefetch=1,
+            grid=(rows,),
+            in_specs=[
+                pl.BlockSpec((slots, depth), by_row),
+                pl.BlockSpec((slots, depth), by_row),
+                pl.BlockSpec((1, depth), whole),
+            ]
+            + [pl.BlockSpec((nc, slots, wc), lambda i, s: (0, 0, 0))] * rows
+            + [pl.BlockSpec(memory_space=pl.ANY)] * nc,
+            out_specs=(pl.BlockSpec((slots, depth), by_row), pl.BlockSpec((1, depth), whole)),
+            scratch_shapes=[
+                pltpu.VMEM((nc, wc, depth), BF16),
                 pltpu.SemaphoreType.DMA((nc * place.nd,)),
             ],
         ),
         compiler_params=params(),
-        cost_estimate=cost(
-            flops=2 * slots * depth * nc * wc,
-            bytes_accessed=2 * nc * depth * wc,
-            transcendentals=slots,
-        ),
+        cost_estimate=cost(),
         name="project_back",
-    )(info, dq, lin, x, middle_grad, gain, qgain, kgain, cosine, sine, *dkv_parts, *w_cols)
+    )(info, x, middle_grad, gain, *dlins, *w_cols)
 
 
 def fill_bias(bias_ref, info_ref, row, masks, slots):
@@ -501,15 +535,12 @@
             k, v = kv[:, :HD], kv[:, HD:]
             for h in range(GROUP):
                 qh = q_ref[:, h * HD : (h + 1) * HD]
-                s = nt(k, qh) + bias_ref[...]
-                m = jnp.max(s, 0, keepdims=True)
-                e = jnp.exp(s - m)
+                e = jnp.exp(nt(k, qh) + bias_ref[...])
                 l = jnp.sum(e, 0, keepdims=True)
-                p = (e * (1.0 / l)).astype(BF16)
-                o = tn(v, p)
+                o = tn(v, (e * (1.0 / l)).astype(BF16))
                 o_ref[:, h * HD : (h + 1) * HD] = o.T.astype(BF16)
                 ot_ref[h * HD : (h + 1) * HD, :] = o.astype(BF16)
-                lse_ref[0, h : h + 1, :] = m + jnp.log(l)
+                lse_ref[0, h : h + 1, :] = jnp.log(l)
 
     n = slots
     return pl.pallas_call(
@@ -1049,7 +1080,7 @@
         qkv_cols = place.gather(qkv_cross)
         out_dp = gather_dp(after(w_out.T, qkv_dp), False)
         out_cross = place.cross(after(out_dp, *place.arrived(qkv_cross)))
-        sizes = [512, 512, 256] if units == 1280 else [units]
+        sizes = [768, 512] if units == 1280 else [units]
         starts = [sum(sizes[:c]) for c in range(len(sizes))]
         chunks = []
         for start, size in zip(starts, sizes):
@@ -1058,7 +1089,8 @@
             chunks.append(gather_dp(after(local, qkv_dp), True))
 
         normed, lin, q, kv = project(
-            info, place, x, gain_one, qkv_cols, qc, kc, qgain2, kgain2, cosine, sine, rows, slots
+            info, place, x, gain_one, qkv_cols, qc, kc, qgain2, kgain2, cosine, sine,
+            rows, slots,
         )
         out_cols = place.gather(out_cross, q)
         kv_cross = place.cross(kv)
@@ -1084,11 +1116,11 @@
         if per != rows:
             n2_cross = [place.cross(jnp.concatenate(n2_cross, 0))]
 
-        sides = {"near": slice(0, half), "far": slice(half, nc)}
-        sums = {"near": None, "far": None}
+        n2_got = [place.gather(v) for v in n2_cross]
+        n2_all = [[v[i] for v in n2_got] for i in range(nc)]
+        n2_flat = [v for group in n2_all for v in group]
+        sums = [None] * nc
         ffn_grads, last_out = [], []
-        n2_near = [[c[m] for c in n2_cross] for m in masks[:half] if m in n2_cross[0]]
-        n2_all = None
 
         def whole(sets, size):
             part = weight_grads(after(everywhere, *last_out), block, sets, size)
@@ -1115,96 +1147,86 @@
             ffn_grads.append(own.reshape(3, size, block))
             return part
 
-        def scatter_core_of(k, *hold):
-            pieces = [after(s[k], *hold) for s in (*sums["near"], *sums["far"])]
-            return place.scatter_core(dict(zip(masks, pieces)))
-
+        def scatter_core_of(k, which, *hold):
+            return place.scatter_core({masks[i]: after(sums[i][k], *hold) for i in which})[0]
+
+        near_side, far_side = range(half), range(half, nc)
+        normed_cross = place.cross(after(normed, *place.arrived(n2_cross[-1])))
         waiting = []
         for c, weights in enumerate(chunks):
-            acts = None
-            for side in ("far", "near") if c == len(chunks) - 1 and c else ("near", "far"):
-                at = sides[side]
-                if n2_all is None and len(n2_near) < half:
-                    n2_all = [place.gather(v) for v in n2_cross]
-                    n2_all = [[v[i] for v in n2_all] for i in range(nc)]
-                sums[side], acts = feed_forward(
-                    after(info, *last_out), place, weights, (n2_all or n2_near)[at], bg_all[at],
-                    sums[side], acts, nc * n, at.start, c == len(chunks) - 1,
+            acts, ends = None, c == len(chunks) - 1
+            for at in (slice(half, nc), slice(0, half)) if ends else (slice(0, nc),):
+                sums[at], acts = feed_forward(
+                    after(info, *last_out), place, weights, n2_all[at], bg_all[at],
+                    None if c == 0 else sums[at], acts, nc * n, at.start, ends,
                 )
                 last_out = [acts[0]]
-                if n2_all is None:
-                    n2_all = [place.gather(v, acts[0]) for v in n2_cross]
-                    n2_all = [[v[i] for v in n2_all] for i in range(nc)]
+                if ends and at.start:
+                    grads = scatter_core_of(1, far_side)
+                    grads_got = place.send_outer(grads)
+                    last_out = [acts[0], *grads.values()]
             h, gg, ug = [[a] for a in acts]
-            n2_flat = [v for group in n2_all for v in group]
             sets = [(n2_flat, [gg, ug]), (bg_all, [h])]
-            if c == 0:
-                normed_cross = place.cross(after(normed, acts[0]))
-            if c == 1:
-                last_out = last_out + place.arrived(normed_cross)
-            if c == len(chunks) - 1:
-                grads, _ = scatter_core_of(1)
-                grad_parts = [grads[0]] + place.send_outer(grads)
-                last_out = last_out + [grads[m] for m in place.combos[1:]]
-            if c == 0 or nn_ == 1:
+            if nn_ == 1:
                 last_out = [whole(sets, sizes[c])]
             else:
                 mine, entry = send(sets, sizes[c])
                 waiting.append(entry)
                 last_out = [mine]
+            if not ends:
+                last_out = last_out + place.arrived(normed_cross)
         normed_got = place.gather(normed_cross, *last_out)
-
-        branches, _ = scatter_core_of(0, *last_out)
-        branch_far = [branches[m] for m in place.combos[1:]]
-        last_out = last_out + branch_far
+        grad_parts = [scatter_core_of(1, near_side, *last_out, *grads_got)[0], *grads_got]
+
         middle_grad, attn_grad, mixed_grad, gf = middle_back(
             after(info, *last_out), place, grad_parts, middles, bg, gain_two, out_cols, rows, slots
         )
-        branch_got = place.send_outer({m: after(b, middle_grad) for m, b in branches.items()})
+        branches = scatter_core_of(0, far_side, mixed_grad)
+        branches |= scatter_core_of(0, near_side, mixed_grad)
         w_out_all = out_weight_grads(after(every, mixed_grad), place, block, attn_grad, mixed_t)
         w_out_core, _ = place.scatter_core(dict(zip(masks, w_out_all)))
         dqs, cores = [], []
-        last_out = [mixed_grad, w_out_all[0]]
+        outer = place.combos[1:]
+        last_out = [w_out_all[0], *[w_out_core[m] for m in outer]]
         for r in range(rows):
             dq, *dkv = attend_back(
                 after(info, *last_out), q, kv_all, mixed_grad, lse[r], masks, r, slots
             )
             dqs.append(dq)
             last_out = [dq]
-            if waiting:
-                last_out = [keep(waiting.pop(0))]
             if r == 0:
-                last_out = last_out + [w_out_core[m] for m in place.combos[1:]]
                 w_out_got = place.send_outer({m: after(b, dq) for m, b in w_out_core.items()})
-                last_out = last_out + ffn_grads[:1]
+                if len(waiting) > 1:
+                    last_out = [keep(waiting.pop(0))]
+                last_out = last_out + normed_got[1:] + list(branches.values())
             cores.append(place.scatter_core(dict(zip(masks, dkv)), F32))
         dkvs = [[core[0], *place.send_outer(core)] for core, _ in cores]
-
-        out_rows = finish_rows(
-            middles, [branches[0], *branch_got], valid
-        )
-        last_out = last_out + [core[m] for core, _ in cores for m in place.combos[1:]]
-        last_out = last_out + ffn_grads[1:2] + branch_got
-
-        input_grads, dlin_got, ga, gq, gk = [], [], [], [], []
+        last_out = last_out + [core[m] for core, _ in cores for m in outer]
+
+        dlins, dlin_got, gq, gk = [], [], [], []
         for r in range(rows):
-            ig, ga_r, gq_r, gk_r, *dlin = project_back(
-                after(info, *last_out), place, dqs[r], dkvs[r], lin, x, middle_grad, gain_one, qkv_cols,
-                qc, kc, qgain2, kgain2, cosine, sine, r, slots,
+            own, gq_r, gk_r, *dlin = heads_back(
+                after(info, *last_out), place, dqs[r], dkvs[r], lin, qc, kc, qgain2, kgain2, cosine, sine,
+                r, slots,
             )
-            last_out = [ig, out_rows, *w_out_got]
-            input_grads.append(ig)
+            dlins.append(own)
             dlin_got.append(place.exchange(dlin))
-            ga.append(ga_r[0])
+            last_out = [own]
+            if r == rows - 1:
+                last_out = last_out + w_out_got
+            if waiting and r == rows - 1:
+                last_out = [keep(waiting.pop(0))]
             gq.append(gq_r[0])
             gk.append(gk_r[0])
-        halves = combine(
-            [w_out_core[0], *[after(g, input_grads[0]) for g in w_out_got]], BF16, nn_
+        input_grad, ga = project_back(
+            after(info, *last_out, *ffn_grads[:1]), place, dlins, x, middle_grad, gain_one, qkv_cols, rows, slots
         )
+        halves = combine([w_out_core[0], *[after(g, dlins[0]) for g in w_out_got]], BF16, nn_)
         halves = [halves[0]] + [
             swap(h, "near", nn_, i) for i, h in enumerate(halves[1:], 1)
         ]
-        w_out_half = combine([halves[0], *[after(h, input_grads[-1]) for h in halves[1:]]], BF16)[0]
+
+        w_out_half = combine([halves[0], *[after(h, input_grad) for h in halves[1:]]], BF16)[0]
         w_out_grad = lax.psum_scatter(
             w_out_half.reshape(nf * oc, block), "far", scatter_dimension=0, tiled=True
         )
@@ -1215,29 +1237,35 @@
                 total = total + p.astype(F32)
             return total[0]
 
+        gains, gains_got = place.total(jnp.concatenate([ga[0], gf[0], sum(gq), sum(gk)]))
         right = [dlin_got[r][i] for i in range(nc) for r in range(rows)]
         if per != rows:
             right = [jnp.concatenate(right, 1)]
         got = None
         for i in reversed(range(nn_)):
             part = weight_grads(
-                to_near_far[i], block, [(normed_got, [right])], qc + 2 * kc,
+                after(to_near_far[i], input_grad, *ffn_grads[:1]), block, [(normed_got, [right])], qc + 2 * kc,
                 got if i == 0 else None, i == 0,
             )
             if i:
+                branch_got = place.send_outer({m: after(b, part, *gains_got) for m, b in branches.items()})
                 part = swap(part, "near", nn_, i)
                 got = part if got is None else got + part
-        w_qkv_grad = summed([part[0]] + [swap(part[m], "far", nf, m) for m in range(1, nf)])
-        gains = place.total(after(jnp.concatenate([sum(ga), gf[0], sum(gq), sum(gk)]), part[0]))
+        if nn_ == 1:
+            branch_got = place.send_outer(branches)
+        out_rows = finish_rows(middles, [branches[0], *branch_got], valid)
+        gains = place.total_dp(gains, part[0])
         gq = gains[2 * depth : 2 * depth + LANES]
-        gk = gains[2 * depth + LANES :]
+        gk = gains[2 * depth + LANES : 2 * depth + 2 * LANES]
+        far_got = [swap(part[m], "far", nf, m) for m in range(1, nf)]
+        w_qkv_grad = summed([part[0]] + [after(g, out_rows) for g in far_got])
 
         grads = None
         for own, start in zip(ffn_grads, starts):
             grads = finish_grads(own, start, units, grads)
         return (
             out_rows.reshape(rows, slots, depth),
-            jnp.stack(input_grads, 0),
+            input_grad.reshape(rows, slots, depth),
             gains[:depth],
             w_qkv_grad[:qc].T,
             w_qkv_grad[qc : qc + kc].T,

time: 822 us -> 731 us (0.89)
  Pallas kernels: 459 us -> 417 us
  waiting for transfers between devices: 267 us -> 225 us
    ppermute x56, waiting for transfers between devices: 215 us -> 173 us  [swap(): return lax.ppermute(value, axis, [(i, i ^ mask) for i in range(size)])]
    pallas_call x6 -> x3, Pallas kernels: 148 us -> 120 us  [feed_forward(): pl.pallas_call(body, out_shape=(*[jax.ShapeDtypeStruct((tokens, depth), s...]
    pallas_call x2, Pallas kernels: 41.3 us -> 32.5 us  [attend(): pl.pallas_call(body, out_shape=(jax.ShapeDtypeStruct((n, QW), BF16), jax....]
    pallas_call x7 -> x6, Pallas kernels: 81.9 us -> 76.5 us  [weight_grads(): pl.pallas_call(body, out_shape=shapes, grid_spec=pltpu.PrefetchScalarGrid...]
    pallas_call x2 -> x3, Pallas kernels: 36.2 us -> 37.2 us  [the longest x2 23.4 us: heads_back(): pl.pallas_call(body, out_shape=(jax.ShapeDtypeStruct((nc, slots, wc), BF1...]
    all_gather x5 -> x4, waiting for transfers between devices: 52 us -> 52 us  [gather_dp(): return lax.all_gather(value, place.dp, axis=0, tiled=tiled)]
  transfers between devices with their start and end apart: 65 -> 63, of which waited for: 24 -> 25; matrix products, arithmetic and copies ran while one was open for 2% -> 2% of each run, Pallas kernels for 56% -> 49%
where the time goes in v3:
time: 731 us; the launch traced here: 725 us
  Pallas kernels  417 us (57%)
  waiting for transfers between devices  225 us (31%)
  starting transfers between devices  36.7 us (5%)
  local copies, waits for them, and re-layouts  20 us (3%)
  between operations  15.1 us (2%)
  other arithmetic  11 us (2%)
    ppermute x56, waiting for transfers between devices, swap(): return lax.ppermute(value, axis, [(i, i ^ mask) for i in range(size)])  173 us
    pallas_call x3, Pallas kernels, feed_forward(): pl.pallas_call(body, out_shape=(*[jax.ShapeDtypeStruct((tokens, depth), s...  120 us
    pallas_call x6, Pallas kernels, weight_grads(): pl.pallas_call(body, out_shape=shapes, grid_spec=pltpu.PrefetchScalarGrid...  76.5 us
    all_gather x4, waiting for transfers between devices, gather_dp(): return lax.all_gather(value, place.dp, axis=0, tiled=tiled)  52 us
    pallas_call x2, Pallas kernels, attend_back(): pl.pallas_call(body, out_shape=(jax.ShapeDtypeStruct((n, QW), F32), *[jax...  43.8 us
    ppermute x56, starting transfers between devices, swap(): return lax.ppermute(value, axis, [(i, i ^ mask) for i in range(size)])  36.4 us
    pallas_call x12, Pallas kernels, combine(): pl.pallas_call(body, out_shape=[jax.ShapeDtypeStruct(out, kind)] * pieces...  32.9 us
    pallas_call x2, Pallas kernels, attend(): pl.pallas_call(body, out_shape=(jax.ShapeDtypeStruct((n, QW), BF16), jax....  32.5 us
  transfers between devices with their start and end apart: 63, of which 25 were waited for; matrix products, arithmetic and copies ran while one was open for 2% of the time, Pallas kernels for 49%

profile of v3, /device:TPU:0, one launch (start us, length us, event | category | flops | bytes accessed | tf_op | source)
XLA Modules:
  0.0 725.4 jit_solution(16556060091041471606)
XLA Ops:
  9.1 52.0 %all-gather.11.cloned.1.call-done = bf16[3840,256]{1,0:T(8,128)(2,1)} async-done(((bf16[480,256]{1,0:T(8,128)(2,1)}), bf16[3840,256]{1,0:T(8,128)(2,1)}) %all-gather.11.cloned.1.call-update) | async-done | bytes 1966096 | tf_op jit(solution)/shard_map/all_gather | solution.py:1073
  70.0 38.2 %collective-permute-done.1.refs_2_.refs_4_ = bf16[8,480,256]{2,1,0:T(8,128)(2,1)} collective-permute-done((bf16[8,480,256]{2,1,0:T(8,128)(2,1)}, bf16[8,480,256]{2,1,0:T(8,128)(2,1)}, u32[]{:S(2)}, u32[]{:S(2)}) %collective-permute-start.1) | collective-permute-done | bytes 1966112 | tf_op jit(solution)/shard_map/ppermute | solution.py:52
  112.6 19.4 %project.1 = (bf16[512,2048]{1,0:T(8,128)(2,1)}, f32[4,512,480]{2,1,0:T(8,128)}, bf16[512,1280]{1,0:T(8,128)(2,1)}, bf16[512,640]{1,0:T(8,128)(2,1)}) custom-call(s32[3]{0:T(128)} %pad_add_fusion.info_ref, bf16[512,2048]{1,0:T(8,128)(2,1)} %bitcast.50, f32[1,2048]{1,0:T(1,128)} %bitcast.74, f32[1,128]{1,0:T(1,128)} %broadcast_in_dim_tile.6.qgain_ref, ...), custom_call_target="tpu_custom_call" | custom-call | flops 1 | bytes 1 | tf_op jit(solution)/shard_map/project/pallas_call | solution.py:306
  134.1 6.1 collective-permute-done.3.refs_2_.refs_8_
  140.2 13.5 %collective-permute-done.6.refs_2_ = bf16[512,640]{1,0:T(8,128)(2,1)S(1)} collective-permute-done((bf16[512,640]{1,0:T(8,128)(2,1)}, bf16[512,640]{1,0:T(8,128)(2,1)S(1)}, u32[]{:S(2)}, u32[]{:S(2)}) %collective-permute-start.6) | collective-permute-done | bytes 655392 | tf_op jit(solution)/shard_map/ppermute | solution.py:52
  160.5 16.2 %attend.2 = (bf16[256,1280]{1,0:T(8,128)(2,1)}, bf16[1280,256]{1,0:T(8,128)(2,1)}, f32[5,4,256]{2,1,0:T(4,128)}) custom-call(s32[3]{0:T(128)} %pad_add_fusion.info_ref, bf16[512,1280]{1,0:T(8,128)(2,1)} %get-tuple-element.148.q_ref, bf16[512,640]{1,0:T(8,128)(2,1)} %get-tuple-element.144.refs_0_, bf16[512,640]{1,0:T(8,128)(2,1)} %copy-done.10, ...), custom_call_target="tpu_custom_call" | custom-call | flops 1 | bytes 1 | tf_op jit(solution)/shard_map/attend/pallas_call | solution.py:546
  176.7 9.0 %out_project.2 = (f32[256,2048]{1,0:T(8,128)}, bf16[256,2048]{1,0:T(8,128)(2,1)}) custom-call(s32[3]{0:T(128)} %pad_add_fusion.info_ref, bf16[256,1280]{1,0:T(8,128)(2,1)} %get-tuple-element.145.mixed_ref, bf16[512,2048]{1,0:T(8,128)(2,1)} %bitcast.51, f32[1,2048]{1,0:T(1,128)} %bitcast.69, bf16[8,320,256]{2,1,0:T(8,128)(2,1)} %bitcast.57, ...), custom_call_target="tpu_custom_call" | custom-call | flops 1 | bytes 1 | tf_op jit(solution)/shard_map/out_project/pallas_call | solution.py:664
  186.2 16.3 %attend.3 = (bf16[256,1280]{1,0:T(8,128)(2,1)}, bf16[1280,256]{1,0:T(8,128)(2,1)}, f32[5,4,256]{2,1,0:T(4,128)}) custom-call(s32[3]{0:T(128)} %pad_add_fusion.info_ref, bf16[512,1280]{1,0:T(8,128)(2,1)} %get-tuple-element.148.q_ref, bf16[512,640]{1,0:T(8,128)(2,1)} %get-tuple-element.144.refs_0_, bf16[512,640]{1,0:T(8,128)(2,1)} %copy-done.10, ...), custom_call_target="tpu_custom_call" | custom-call | flops 1 | bytes 1 | tf_op jit(solution)/shard_map/attend/pallas_call | solution.py:546
  202.5 21.1 %collective-permute-done.9.refs_4_.refs_0_ = bf16[256,2048]{1,0:T(8,128)(2,1)} collective-permute-done((bf16[256,2048]{1,0:T(8,128)(2,1)}, bf16[256,2048]{1,0:T(8,128)(2,1)}, u32[]{:S(2)}, u32[]{:S(2)}) %collective-permute-start.9) | collective-permute-done | bytes 1048608 | tf_op jit(solution)/shard_map/ppermute | solution.py:52
  223.7 9.0 %out_project.3 = (f32[256,2048]{1,0:T(8,128)}, bf16[256,2048]{1,0:T(8,128)(2,1)}) custom-call(s32[3]{0:T(128)} %pad_add_fusion.info_ref, bf16[256,1280]{1,0:T(8,128)(2,1)} %get-tuple-element.152.mixed_ref, bf16[512,2048]{1,0:T(8,128)(2,1)} %bitcast.52, f32[1,2048]{1,0:T(1,128)} %bitcast.70, bf16[8,320,256]{2,1,0:T(8,128)(2,1)} %bitcast.58, ...), custom_call_target="tpu_custom_call" | custom-call | flops 1 | bytes 1 | tf_op jit(solution)/shard_map/out_project/pallas_call | solution.py:664
  235.6 22.9 %collective-permute-done.14.refs_5_.refs_1_ = bf16[256,2048]{1,0:T(8,128)(2,1)S(1)} collective-permute-done((bf16[256,2048]{1,0:T(8,128)(2,1)}, bf16[256,2048]{1,0:T(8,128)(2,1)S(1)}, u32[]{:S(2)}, u32[]{:S(2)}) %collective-permute-start.14) | collective-permute-done | bytes 1048608 | tf_op jit(solution)/shard_map/ppermute | solution.py:52
  260.5 6.5 collective-permute-done.15.refs_6_.refs_2_
  270.4 58.6 %feed_forward.3 = (f32[512,2048]{1,0:T(8,128)}, f32[512,2048]{1,0:T(8,128)}, f32[512,2048]{1,0:T(8,128)}, f32[512,2048]{1,0:T(8,128)}, f32[512,2048]{1,0:T(8,128...) custom-call(s32[3]{0:T(128)} %pad_add_fusion.info_ref, ...), custom_call_target="tpu_custom_call" | custom-call | flops 1 | bytes 1 | tf_op jit(solution)/shard_map/feed_forward/pallas_call | solution.py:910
  329.0 17.5 %weight_grads.6 = bf16[4,3,768,256]{3,2,1,0:T(8,128)(2,1)} custom-call(s32[4]{0:T(128)} %copy-done.34, bf16[256,2048]{1,0:T(8,128)(2,1)} %get-tuple-element.150.refs_0_, bf16[256,2048]{1,0:T(8,128)(2,1)} %get-tuple-element.155.refs_1_, bf16[256,2048]{1,0:T(8,128)(2,1)} %copy-done.2, bf16[256,2048]{1,0:T(8,128)(2,1)} %copy-done.3, ...), custom_call_target="tpu_custom_call" | custom-call | flops 1 | bytes 1 | tf_op jit(solution)/shard_map/weight_grads/pallas_call | solution.py:973
  346.6 37.3 %feed_forward.4 = (bf16[512,2048]{1,0:T(8,128)(2,1)}, bf16[512,2048]{1,0:T(8,128)(2,1)}, bf16[512,2048]{1,0:T(8,128)(2,1)}, bf16[512,2048]{1,0:T(8,128)(2,1)}, b...) custom-call(s32[3]{0:T(128)} %pad_add_fusion.info_ref, ...), custom_call_target="tpu_custom_call" | custom-call | flops 1 | bytes 1 | tf_op jit(solution)/shard_map/feed_forward/pallas_call | solution.py:910
  394.1 24.6 %feed_forward.5 = (bf16[512,2048]{1,0:T(8,128)(2,1)}, bf16[512,2048]{1,0:T(8,128)(2,1)}, bf16[512,2048]{1,0:T(8,128)(2,1)}, bf16[512,2048]{1,0:T(8,128)(2,1)}, b...) custom-call(s32[3]{0:T(128)} %pad_add_fusion.info_ref, ...), custom_call_target="tpu_custom_call", output_to_operand_aliasing={{4}: (12, {}), {5}: (13, {}), {6}: (14, {})} | custom-call | flops 1 | bytes 1 | tf_op jit(solution)/shard_map/feed_forward/pallas_call | solution.py:910
  418.8 13.3 %weight_grads.7 = bf16[4,3,512,256]{3,2,1,0:T(8,128)(2,1)} custom-call(s32[4]{0:T(128)} %copy-done.34, bf16[256,2048]{1,0:T(8,128)(2,1)} %get-tuple-element.150.refs_0_, bf16[256,2048]{1,0:T(8,128)(2,1)} %get-tuple-element.155.refs_1_, bf16[256,2048]{1,0:T(8,128)(2,1)} %copy-done.2, bf16[256,2048]{1,0:T(8,128)(2,1)} %copy-done.3, ...), custom_call_target="tpu_custom_call" | custom-call | flops 1 | bytes 1 | tf_op jit(solution)/shard_map/weight_grads/pallas_call | solution.py:973
  432.0 9.0 %collective-permute-done.21.refs_1_ = bf16[512,2048]{1,0:T(8,128)(2,1)S(1)} collective-permute-done((bf16[512,2048]{1,0:T(8,128)(2,1)}, bf16[512,2048]{1,0:T(8,128)(2,1)S(1)}, u32[]{:S(2)}, u32[]{:S(2)}) %collective-permute-start.21) | collective-permute-done | bytes 2097184 | tf_op jit(solution)/shard_map/ppermute | solution.py:52
  449.0 14.9 %middle_back.1 = (f32[512,2048]{1,0:T(8,128)}, bf16[512,2048]{1,0:T(8,128)(2,1)}, bf16[512,1280]{1,0:T(8,128)(2,1)}, f32[1,2048]{1,0:T(1,128)}) custom-call(s32[3]{0:T(128)} %pad_add_fusion.info_ref, bf16[512,2048]{1,0:T(8,128)(2,1)} %combine.13.refs_0_, bf16[512,2048]{1,0:T(8,128)(2,1)} %copy-done.13, f32[256,2048]{1,0:T(8,128)} %get-tuple-element.147.refs_2_.refs_0_, ...), custom_call_target="tpu_custom_call" | custom-call | flops 1 | bytes 1 | tf_op jit(solution)/shard_map/middle_back/pallas_call | solution.py:729
  463.9 9.2 %out_weight_grads.1 = (bf16[8,320,256]{2,1,0:T(8,128)(2,1)}, bf16[8,320,256]{2,1,0:T(8,128)(2,1)}, bf16[8,320,256]{2,1,0:T(8,128)(2,1)}, bf16[8,320,256]{2,1,0:T(8,128)(2,1)}) custom-call(s32[9]{0:T(128)} %pad_add_fusion.1.order_ref, bf16[512,2048]{1,0:T(8,128)(2,1)} %get-tuple-element.197.left_ref, bf16[1280,256]{1,0:T(8,128)(2,1)} %get-tuple-element.198.refs_0_, ...), custom_call_target="tpu_custom_call" | custom-call | flops 1 | bytes 1 | tf_op jit(solution)/shard_map/out_weight_grads/pallas_call | solution.py:1003
  480.5 22.0 %attend_back.2 = (f32[256,1280]{1,0:T(8,128)}, bf16[256,640]{1,0:T(8,128)(2,1)}, bf16[256,640]{1,0:T(8,128)(2,1)}, bf16[256,640]{1,0:T(8,128)(2,1)}, bf16[256,640]{1,0:T(8,128)(2,1)}) custom-call(s32[3]{0:T(128)} %pad_add_fusion.info_ref, bf16[512,1280]{1,0:T(8,128)(2,1)} %get-tuple-element.148.q_ref, bf16[512,1280]{1,0:T(8,128)(2,1)} %get-tuple-element.188.do_ref, ...), custom_call_target="tpu_custom_call" | custom-call | flops 1 | bytes 1 | tf_op jit(solution)/shard_map/attend_back/pallas_call | solution.py:617
  502.5 17.9 %weight_grads.8 = bf16[4,3,768,256]{3,2,1,0:T(8,128)(2,1)} custom-call(s32[4]{0:T(128)} %copy-done.35, bf16[256,2048]{1,0:T(8,128)(2,1)} %get-tuple-element.150.refs_0_, bf16[256,2048]{1,0:T(8,128)(2,1)} %get-tuple-element.155.refs_1_, bf16[256,2048]{1,0:T(8,128)(2,1)} %copy-done.2, bf16[256,2048]{1,0:T(8,128)(2,1)} %copy-done.3, ...), custom_call_target="tpu_custom_call" | custom-call | flops 1 | bytes 1 | tf_op jit(solution)/shard_map/weight_grads/pallas_call | solution.py:973
  535.0 21.8 %attend_back.3 = (f32[256,1280]{1,0:T(8,128)}, bf16[256,640]{1,0:T(8,128)(2,1)}, bf16[256,640]{1,0:T(8,128)(2,1)}, bf16[256,640]{1,0:T(8,128)(2,1)}, bf16[256,640]{1,0:T(8,128)(2,1)}) custom-call(s32[3]{0:T(128)} %pad_add_fusion.info_ref, bf16[512,1280]{1,0:T(8,128)(2,1)} %get-tuple-element.148.q_ref, bf16[512,1280]{1,0:T(8,128)(2,1)} %get-tuple-element.188.do_ref, ...), custom_call_target="tpu_custom_call" | custom-call | flops 1 | bytes 1 | tf_op jit(solution)/shard_map/attend_back/pallas_call | solution.py:617
  571.5 11.6 %heads_back.2 = (bf16[4,256,480]{2,1,0:T(8,128)(2,1)}, f32[1,128]{1,0:T(1,128)}, f32[1,128]{1,0:T(1,128)}, bf16[480,256]{1,0:T(8,128)(2,1)}, bf16[480,256]{1,0:T...) custom-call(s32[3]{0:T(128)} %pad_add_fusion.info_ref, f32[256,1280]{1,0:T(8,128)} %get-tuple-element.205.dq_ref, ...), custom_call_target="tpu_custom_call" | custom-call | flops 1 | bytes 1 | tf_op jit(solution)/shard_map/heads_back/pallas_call | solution.py:408
  583.8 11.9 %heads_back.3 = (bf16[4,256,480]{2,1,0:T(8,128)(2,1)}, f32[1,128]{1,0:T(1,128)}, f32[1,128]{1,0:T(1,128)}, bf16[480,256]{1,0:T(8,128)(2,1)}, bf16[480,256]{1,0:T...) custom-call(s32[3]{0:T(128)} %pad_add_fusion.info_ref, f32[256,1280]{1,0:T(8,128)} %get-tuple-element.210.dq_ref, ...), custom_call_target="tpu_custom_call" | custom-call | flops 1 | bytes 1 | tf_op jit(solution)/shard_map/heads_back/pallas_call | solution.py:408
  595.7 13.5 %weight_grads.9 = bf16[4,3,512,256]{3,2,1,0:T(8,128)(2,1)} custom-call(s32[4]{0:T(128)} %copy-done.35, bf16[256,2048]{1,0:T(8,128)(2,1)} %get-tuple-element.150.refs_0_, bf16[256,2048]{1,0:T(8,128)(2,1)} %get-tuple-element.155.refs_1_, bf16[256,2048]{1,0:T(8,128)(2,1)} %copy-done.2, bf16[256,2048]{1,0:T(8,128)(2,1)} %copy-done.3, ...), custom_call_target="tpu_custom_call" | custom-call | flops 1 | bytes 1 | tf_op jit(solution)/shard_map/weight_grads/pallas_call | solution.py:973
  624.9 13.8 %project_back.1 = (bf16[512,2048]{1,0:T(8,128)(2,1)}, f32[1,2048]{1,0:T(1,128)}) custom-call(s32[3]{0:T(128)} %pad_add_fusion.info_ref, bf16[512,2048]{1,0:T(8,128)(2,1)} %bitcast.53, f32[512,2048]{1,0:T(8,128)} %get-tuple-element.227.mid_ref, f32[1,2048]{1,0:T(1,128)} %bitcast.75, bf16[4,256,480]{2,1,0:T(8,128)(2,1)} %get-tuple-element.219.refs_0_, ...), custom_call_target="tpu_custom_call" | custom-call | flops 1 | bytes 1 | tf_op jit(solution)/shard_map/project_back/pallas_call | solution.py:477
  644.4 7.0 weight_grads.10
  669.9 8.3 %collective-permute-done.49.refs_12_ = bf16[4,1,480,256]{3,2,1,0:T(8,128)(2,1)S(1)} collective-permute-done((bf16[4,1,480,256]{3,2,1,0:T(8,128)(2,1)}, bf16[4,1,480,256]{3,2,1,0:T(8,128)(2,1)S(1)}, u32[]{:S(2)}, u32[]{:S(2)}) %collective-permute-start.49) | collective-permute-done | bytes 983072 | tf_op jit(solution)/shard_map/ppermute | solution.py:52
  679.1 7.3 %weight_grads.11 = (bf16[1,480,256]{2,1,0:T(8,128)(2,1)}, bf16[1,480,256]{2,1,0:T(8,128)(2,1)}, bf16[1,480,256]{2,1,0:T(8,128)(2,1)}, bf16[1,480,256]{2,1,0:T(8,128)(2,1)}) custom-call(s32[4]{0:T(128)} %get-tuple-element.245.order_ref, bf16[512,2048]{1,0:T(8,128)(2,1)} %get-tuple-element.161.refs_0_, bf16[512,2048]{1,0:T(8,128)(2,1)} %collective-permute-done.19.refs_1_, ...), custom_call_target="tpu_custom_call" | custom-call | flops 1 | bytes 1 | tf_op jit(solution)/shard_map/weight_grads/pallas_call | solution.py:973
  702.0 6.6 finish_rows.1
  708.6 8.2 %collective-permute-done.52 = bf16[1,480,256]{2,1,0:T(8,128)(2,1)S(1)} collective-permute-done((bf16[1,480,256]{2,1,0:T(8,128)(2,1)}, bf16[1,480,256]{2,1,0:T(8,128)(2,1)S(1)}, u32[]{:S(2)}, u32[]{:S(2)}) %collective-permute-start.52) | collective-permute-done | bytes 245792 | tf_op jit(solution)/shard_map/ppermute | solution.py:52
  (281 shorter events, 145.9 us)
Async XLA Ops:
  7.2 53.8 %all-gather.11.cloned.1.call-start = ((), (), s32[]{:S(2)}) async-start(), calls=%async_computation.8 | async-start | bytes 2211840 | tf_op jit(solution)/shard_map/all_gather | solution.py:1073
  9.0 99.2 %all-gather.13.cloned.1.call-start = ((), (), s32[]{:S(2)}) async-start(), calls=%async_computation.9 | async-start | bytes 1474560 | tf_op jit(solution)/shard_map/all_gather | solution.py:1073
  61.1 207.9 %all-gather.7.cloned.1.call-start = ((), (), s32[]{:S(2)}) async-start(), calls=%async_computation.3 | async-start | bytes 10616832 | tf_op jit(solution)/shard_map/all_gather | solution.py:1073
  62.4 284.2 %all-gather.9.cloned.1.call-start = ((), (), s32[]{:S(2)}) async-start(), calls=%async_computation.4 | async-start | bytes 7077888 | tf_op jit(solution)/shard_map/all_gather | solution.py:1073
  63.6 561.3 %reduce-scatter.4.cloned.1.call-start = ((), (), s32[]{:S(2)}) async-start(), calls=%async_computation.5 | async-start | bytes 5898240 | tf_op jit(solution)/shard_map/reduce_scatter | solution.py:1144
  63.8 44.4 %collective-permute-start.1 = (bf16[8,480,256]{2,1,0:T(8,128)(2,1)}, bf16[8,480,256]{2,1,0:T(8,128)(2,1)}, u32[]{:S(2)}, u32[]{:S(2)}) collective-permute-start(bf16[8,480,256]{2,1,0:T(8,128)(2,1)} %bitcast.8.refs_0_.refs_2_), channel_id=1, source_target_pairs={{0,2},{1,3},{2,0},{3,1},{4,6},{5,7},{6,4},{7,5},{8,10},{9,11},{10,... | collective-permute-start | bytes 5898248 | tf_op jit(solution)/shard_map/ppermute | solution.py:52
  69.9 38.3 %collective-permute-start = (bf16[8,480,256]{2,1,0:T(8,128)(2,1)}, bf16[8,480,256]{2,1,0:T(8,128)(2,1)}, u32[]{:S(2)}, u32[]{:S(2)}) collective-permute-start(bf16[8,480,256]{2,1,0:T(8,128)(2,1)} %bitcast.8.refs_0_.refs_2_), channel_id=1, source_target_pairs={{0,1},{1,0},{2,3},{3,2},{4,5},{5,4},{6,7},{7,6},{8,9},{9,8},{10,11... | collective-permute-start | bytes 5898248 | tf_op jit(solution)/shard_map/ppermute | solution.py:52
  108.3 32.0 %collective-permute-start.3 = (bf16[8,320,256]{2,1,0:T(8,128)(2,1)}, bf16[8,320,256]{2,1,0:T(8,128)(2,1)}, u32[]{:S(2)}, u32[]{:S(2)}) collective-permute-start(bf16[8,320,256]{2,1,0:T(8,128)(2,1)} %bitcast.56), channel_id=1, source_target_pairs={{0,2},{1,3},{2,0},{3,1},{4,6},{5,7},{6,4},{7,5},{8,10},{9,11},{10,... | collective-permute-start | bytes 3932168 | tf_op jit(solution)/shard_map/ppermute | solution.py:52
  132.0 21.7 %collective-permute-start.6 = (bf16[512,640]{1,0:T(8,128)(2,1)}, bf16[512,640]{1,0:T(8,128)(2,1)S(1)}, u32[]{:S(2)}, u32[]{:S(2)}) collective-permute-start(bf16[512,640]{1,0:T(8,128)(2,1)} %get-tuple-element.144.refs_0_), channel_id=1, source_target_pairs={{0,2},{1,3},{2,0},{3,1},{4,6},{5,7},{6,4},{7,5},{8,10},{9,11},{10,... | collective-permute-start | bytes 1966088 | tf_op jit(solution)/shard_map/ppermute | solution.py:52
  133.6 22.2 %collective-permute-start.4 = (bf16[8,320,256]{2,1,0:T(8,128)(2,1)S(1)}, bf16[8,320,256]{2,1,0:T(8,128)(2,1)S(1)}, u32[]{:S(2)}, u32[]{:S(2)}) collective-permute-start(bf16[8,320,256]{2,1,0:T(8,128)(2,1)S(1)} %bitcast.60), channel_id=1, source_target_pairs={{0,1},{1,0},{2,3},{3,2},{4,5},{5,4},{6,7},{7,6},{8,9},{9,8},{10,11... | collective-permute-start | bytes 3932168 | tf_op jit(solution)/shard_map/ppermute | solution.py:52
  140.2 36.5 %collective-permute-start.8 = (bf16[8,320,256]{2,1,0:T(8,128)(2,1)}, bf16[8,320,256]{2,1,0:T(8,128)(2,1)}, u32[]{:S(2)}, u32[]{:S(2)}) collective-permute-start(bf16[8,320,256]{2,1,0:T(8,128)(2,1)} %collective-permute-done.3.refs_2_.refs_8_), channel_id=1, source_target_pairs={{0,1},{1,0},{2,3},{3,2},{4,5},{5,4},{6,7},{7,6},{8,9},{9,8},{10,11... | collective-permute-start | bytes 3932168 | tf_op jit(solution)/shard_map/ppermute | solution.py:52
  153.7 69.9 %collective-permute-start.11 = (bf16[512,2048]{1,0:T(8,128)(2,1)S(1)}, bf16[512,2048]{1,0:T(8,128)(2,1)}, u32[]{:S(2)}, u32[]{:S(2)}) collective-permute-start(bf16[512,2048]{1,0:T(8,128)(2,1)S(1)} %fusion.refs_8_.refs_4_), channel_id=1, source_target_pairs={{0,2},{1,3},{2,0},{3,1},{4,6},{5,7},{6,4},{7,5},{8,10},{9,11},{10,... | collective-permute-start | bytes 6291464 | tf_op jit(solution)/shard_map/ppermute | solution.py:52
  155.3 68.4 %collective-permute-start.12 = (bf16[512,2048]{1,0:T(8,128)(2,1)S(1)}, bf16[512,2048]{1,0:T(8,128)(2,1)}, u32[]{:S(2)}, u32[]{:S(2)}) collective-permute-start(bf16[512,2048]{1,0:T(8,128)(2,1)S(1)} %fusion.refs_8_.refs_4_), channel_id=1, source_target_pairs={{0,1},{1,0},{2,3},{3,2},{4,5},{5,4},{6,7},{7,6},{8,9},{9,8},{10,11... | collective-permute-start | bytes 6291464 | tf_op jit(solution)/shard_map/ppermute | solution.py:52
  185.8 37.8 %collective-permute-start.9 = (bf16[256,2048]{1,0:T(8,128)(2,1)}, bf16[256,2048]{1,0:T(8,128)(2,1)}, u32[]{:S(2)}, u32[]{:S(2)}) collective-permute-start(bf16[256,2048]{1,0:T(8,128)(2,1)} %get-tuple-element.150.refs_0_), channel_id=1, source_target_pairs={{0,2},{1,3},{2,0},{3,1},{4,6},{5,7},{6,4},{7,5},{8,10},{9,11},{10,... | collective-permute-start | bytes 3145736 | tf_op jit(solution)/shard_map/ppermute | solution.py:52
  232.7 25.8 %collective-permute-start.14 = (bf16[256,2048]{1,0:T(8,128)(2,1)}, bf16[256,2048]{1,0:T(8,128)(2,1)S(1)}, u32[]{:S(2)}, u32[]{:S(2)}) collective-permute-start(bf16[256,2048]{1,0:T(8,128)(2,1)} %get-tuple-element.155.refs_1_), channel_id=1, source_target_pairs={{0,2},{1,3},{2,0},{3,1},{4,6},{5,7},{6,4},{7,5},{8,10},{9,11},{10,... | collective-permute-start | bytes 3145736 | tf_op jit(solution)/shard_map/ppermute | solution.py:52
  234.2 34.7 %collective-permute-start.17 = (bf16[512,2048]{1,0:T(8,128)(2,1)}, bf16[512,2048]{1,0:T(8,128)(2,1)S(1)}, u32[]{:S(2)}, u32[]{:S(2)}) collective-permute-start(bf16[512,2048]{1,0:T(8,128)(2,1)} %collective-permute-done.11.refs_10_.refs_4_), channel_id=1, source_target_pairs={{0,1},{1,0},{2,3},{3,2},{4,5},{5,4},{6,7},{7,6},{8,9},{9,8},{10,11... | collective-permute-start | bytes 6291464 | tf_op jit(solution)/shard_map/ppermute | solution.py:52
  258.5 88.0 %collective-permute-start.18 = (bf16[512,2048]{1,0:T(8,128)(2,1)}, bf16[512,2048]{1,0:T(8,128)(2,1)}, u32[]{:S(2)}, u32[]{:S(2)}) collective-permute-start(bf16[512,2048]{1,0:T(8,128)(2,1)} %get-tuple-element.161.refs_0_), channel_id=1, source_target_pairs={{0,2},{1,3},{2,0},{3,1},{4,6},{5,7},{6,4},{7,5},{8,10},{9,11},{10,... | collective-permute-start | bytes 6291464 | tf_op jit(solution)/shard_map/ppermute | solution.py:52
  260.0 86.5 %collective-permute-start.19 = (bf16[512,2048]{1,0:T(8,128)(2,1)}, bf16[512,2048]{1,0:T(8,128)(2,1)}, u32[]{:S(2)}, u32[]{:S(2)}) collective-permute-start(bf16[512,2048]{1,0:T(8,128)(2,1)} %get-tuple-element.161.refs_0_), channel_id=1, source_target_pairs={{0,1},{1,0},{2,3},{3,2},{4,5},{5,4},{6,7},{7,6},{8,9},{9,8},{10,11... | collective-permute-start | bytes 6291464 | tf_op jit(solution)/shard_map/ppermute | solution.py:52
  393.0 48.1 %collective-permute-start.21 = (bf16[512,2048]{1,0:T(8,128)(2,1)}, bf16[512,2048]{1,0:T(8,128)(2,1)S(1)}, u32[]{:S(2)}, u32[]{:S(2)}) collective-permute-start(bf16[512,2048]{1,0:T(8,128)(2,1)} %combine.12), channel_id=1, source_target_pairs={{0,2},{1,3},{2,0},{3,1},{4,6},{5,7},{6,4},{7,5},{8,10},{9,11},{10,... | collective-permute-start | bytes 6291464 | tf_op jit(solution)/shard_map/ppermute | solution.py:52
  393.6 108.9 %collective-permute-start.26 = (bf16[4,3,768,256]{3,2,1,0:T(8,128)(2,1)}, bf16[4,3,768,256]{3,2,1,0:T(8,128)(2,1)}, u32[]{:S(2)}, u32[]{:S(2)}) collective-permute-start(bf16[4,3,768,256]{3,2,1,0:T(8,128)(2,1)} %weight_grads.6), channel_id=1, source_target_pairs={{0,4},{4,0},{1,5},{5,1},{2,6},{6,2},{3,7},{7,3},{8,12},{12,8},{9,1... | collective-permute-start | bytes 14155784 | tf_op jit(solution)/shard_map/ppermute | solution.py:52
  520.4 172.1 %reduce-scatter.8.cloned.1.call-start = ((), (), s32[]{:S(2)}) async-start(), calls=%async_computation.7 | async-start | bytes 3932160 | tf_op jit(solution)/shard_map/reduce_scatter | solution.py:1144
  520.4 75.3 %collective-permute-start.35 = (bf16[4,3,512,256]{3,2,1,0:T(8,128)(2,1)}, bf16[4,3,512,256]{3,2,1,0:T(8,128)(2,1)}, u32[]{:S(2)}, u32[]{:S(2)}) collective-permute-start(bf16[4,3,512,256]{3,2,1,0:T(8,128)(2,1)} %weight_grads.7), channel_id=1, source_target_pairs={{0,4},{4,0},{1,5},{5,1},{2,6},{6,2},{3,7},{7,3},{8,12},{12,8},{9,1... | collective-permute-start | bytes 9437192 | tf_op jit(solution)/shard_map/ppermute | solution.py:52
  521.6 74.1 %collective-permute-start.34 = (bf16[8,320,256]{2,1,0:T(8,128)(2,1)}, bf16[8,320,256]{2,1,0:T(8,128)(2,1)S(1)}, u32[]{:S(2)}, u32[]{:S(2)}) collective-permute-start(bf16[8,320,256]{2,1,0:T(8,128)(2,1)} %combine.16), channel_id=1, source_target_pairs={{0,2},{1,3},{2,0},{3,1},{4,6},{5,7},{6,4},{7,5},{8,10},{9,11},{10,... | collective-permute-start | bytes 3932168 | tf_op jit(solution)/shard_map/ppermute | solution.py:52
  525.6 31.8 %collective-permute-start.28 = (bf16[256,640]{1,0:T(8,128)(2,1)}, bf16[256,640]{1,0:T(8,128)(2,1)S(1)}, u32[]{:S(2)}, u32[]{:S(2)}) collective-permute-start(bf16[256,640]{1,0:T(8,128)(2,1)} %get-tuple-element.212), channel_id=1, source_target_pairs={{0,1},{1,0},{2,3},{3,2},{4,5},{5,4},{6,7},{7,6},{8,9},{9,8},{10,11... | collective-permute-start | bytes 983048 | tf_op jit(solution)/shard_map/ppermute | solution.py:52
  562.6 20.5 %collective-permute-start.33 = (bf16[256,640]{1,0:T(8,128)(2,1)}, bf16[256,640]{1,0:T(8,128)(2,1)S(1)}, u32[]{:S(2)}, u32[]{:S(2)}) collective-permute-start(bf16[256,640]{1,0:T(8,128)(2,1)} %combine.18), channel_id=1, source_target_pairs={{0,2},{1,3},{2,0},{3,1},{4,6},{5,7},{6,4},{7,5},{8,10},{9,11},{10,... | collective-permute-start | bytes 983048 | tf_op jit(solution)/shard_map/ppermute | solution.py:52
  609.3 91.1 %reduce-scatter.6.cloned.1.call-start = ((), (), s32[]{:S(2)}) async-start(), calls=%async_computation.6 | async-start | bytes 819200 | tf_op jit(solution)/shard_map/reduce_scatter | solution.py:1230
  618.2 21.3 %collective-permute-start.38 = (bf16[480,256]{1,0:T(8,128)(2,1)}, bf16[480,256]{1,0:T(8,128)(2,1)S(1)}, u32[]{:S(2)}, u32[]{:S(2)}) collective-permute-start(bf16[480,256]{1,0:T(8,128)(2,1)} %get-tuple-element.234), channel_id=1, source_target_pairs={{0,2},{1,3},{2,0},{3,1},{4,6},{5,7},{6,4},{7,5},{8,10},{9,11},{10,... | collective-permute-start | bytes 737288 | tf_op jit(solution)/shard_map/ppermute | solution.py:52
  618.3 22.9 %collective-permute-start.40 = (bf16[480,256]{1,0:T(8,128)(2,1)}, bf16[480,256]{1,0:T(8,128)(2,1)S(1)}, u32[]{:S(2)}, u32[]{:S(2)}) collective-permute-start(bf16[480,256]{1,0:T(8,128)(2,1)} %get-tuple-element.236), channel_id=1, source_target_pairs={{0,3},{1,2},{2,1},{3,0},{4,7},{5,6},{6,5},{7,4},{8,11},{9,10},{10,... | collective-permute-start | bytes 737288 | tf_op jit(solution)/shard_map/ppermute | solution.py:52
  623.5 20.1 %collective-permute-start.41 = (bf16[480,256]{1,0:T(8,128)(2,1)S(1)}, bf16[480,256]{1,0:T(8,128)(2,1)S(1)}, u32[]{:S(2)}, u32[]{:S(2)}) collective-permute-start(bf16[480,256]{1,0:T(8,128)(2,1)S(1)} %copy-done.38), channel_id=1, source_target_pairs={{0,3},{1,2},{2,1},{3,0},{4,7},{5,6},{6,5},{7,4},{8,11},{9,10},{10,... | collective-permute-start | bytes 737288 | tf_op jit(solution)/shard_map/ppermute | solution.py:52
  651.4 50.6 %collective-permute-start.45 = (bf16[512,2048]{1,0:T(8,128)(2,1)S(1)}, bf16[512,2048]{1,0:T(8,128)(2,1)}, u32[]{:S(2)}, u32[]{:S(2)}) collective-permute-start(bf16[512,2048]{1,0:T(8,128)(2,1)S(1)} %copy-done.12), channel_id=1, source_target_pairs={{0,2},{1,3},{2,0},{3,1},{4,6},{5,7},{6,4},{7,5},{8,10},{9,11},{10,... | collective-permute-start | bytes 6291464 | tf_op jit(solution)/shard_map/ppermute | solution.py:52
  652.1 26.1 %collective-permute-start.49 = (bf16[4,1,480,256]{3,2,1,0:T(8,128)(2,1)}, bf16[4,1,480,256]{3,2,1,0:T(8,128)(2,1)S(1)}, u32[]{:S(2)}, u32[]{:S(2)}) collective-permute-start(bf16[4,1,480,256]{3,2,1,0:T(8,128)(2,1)} %weight_grads.10), channel_id=1, source_target_pairs={{0,4},{4,0},{1,5},{5,1},{2,6},{6,2},{3,7},{7,3},{8,12},{12,8},{9,1... | collective-permute-start | bytes 2949128 | tf_op jit(solution)/shard_map/ppermute | solution.py:52
  696.3 20.5 %collective-permute-start.52 = (bf16[1,480,256]{2,1,0:T(8,128)(2,1)}, bf16[1,480,256]{2,1,0:T(8,128)(2,1)S(1)}, u32[]{:S(2)}, u32[]{:S(2)}) collective-permute-start(bf16[1,480,256]{2,1,0:T(8,128)(2,1)} %get-tuple-element.250), channel_id=1, source_target_pairs={{0,16},{8,24},{16,0},{24,8},{1,17},{9,25},{17,1},{25,9},{2,18},{10... | collective-permute-start | bytes 737288 | tf_op jit(solution)/shard_map/ppermute | solution.py:52
  (85 other events, 840.1 us)
Sparse Core Ops, SparseCore 0:
  10.8 50.1 all-gather.10
  63.2 41.1 all-gather.12
  107.2 136.7 all-gather.6
  246.0 97.1 all-gather.8
  520.5 83.8 reduce-scatter.3
  609.4 60.8 reduce-scatter.7
  672.5 22.3 reduce-scatter.5

commit v4 on v3

--- a/solution.py
+++ b/solution.py
@@ -128,6 +128,93 @@
         return [swap(b, "ctx", self.nc, m) for m, b in blocks.items() if m]
 
 
+def gather_all(place, own):
+    nc, nn_, nf = place.nc, place.nn, place.nf
+    outer, bits, masks = place.combos[1:], place.core, place.masks
+    count = nc * nn_ * nf
+
+    def body(own_ref, *refs):
+        out_refs, (send_sem, recv_sem, own_sem) = refs[:nc], refs[nc:]
+        here = {a: lax.axis_index(a) for a in ("far", "near", "ctx")}
+        barrier = pltpu.get_barrier_semaphore()
+        partners = [("far", m) for m in range(1, nf)] + [("near", m) for m in range(1, nn_)]
+        partners += [("ctx", m) for m in (*outer, *bits)]
+        for axis, m in partners:
+            pl.semaphore_signal(
+                barrier, inc=1, device_id={axis: here[axis] ^ m}, device_id_type=pl.DeviceIdType.MESH
+            )
+        pl.semaphore_wait(barrier, len(partners))
+        kept = pltpu.make_async_copy(own_ref, out_refs[0].at[0, 0], own_sem)
+        kept.start()
+
+        def place_of(k, i, f):
+            return out_refs[masks.index(k)].at[i, f]
+
+        sent = {}
+
+        def send(source, key, axis, m):
+            n = (masks.index(key[0]) * nn_ + key[1]) * nf + key[2]
+            sent[key] = pltpu.make_async_remote_copy(
+                src_ref=source,
+                dst_ref=place_of(*key),
+                send_sem=send_sem.at[n],
+                recv_sem=recv_sem.at[n],
+                device_id={axis: here[axis] ^ m},
+                device_id_type=pl.DeviceIdType.MESH,
+            )
+            sent[key].start()
+
+        def to_group(source, i, f):
+            for m in (*outer, *bits):
+                send(source, (m, i, f), "ctx", m)
+
+        for f in range(1, nf):
+            send(own_ref, (0, 0, f), "far", f)
+        for i in range(1, nn_):
+            send(own_ref, (0, i, 0), "near", i)
+        to_group(own_ref, 0, 0)
+        for f in range(nf):
+            if f:
+                sent[0, 0, f].wait_recv()
+                for i in range(1, nn_):
+                    send(place_of(0, 0, f), (0, i, f), "near", i)
+                to_group(place_of(0, 0, f), 0, f)
+            for i in range(1, nn_):
+                sent[0, i, f].wait_recv()
+                to_group(place_of(0, i, f), i, f)
+        for f in range(nf):
+            for i in range(nn_):
+                for m in outer:
+                    sent[m, i, f].wait_recv()
+                    for bit in bits:
+                        send(place_of(m, i, f), (m | bit, i, f), "ctx", bit)
+        for (k, i, f), copy in sent.items():
+            if any(k & bit for bit in bits):
+                copy.wait_recv()
+            copy.wait_send()
+        kept.wait()
+
+    columns, block = own.shape
+    return list(
+        pl.pallas_call(
+            body,
+            out_shape=[jax.ShapeDtypeStruct((nn_, nf, columns, block), BF16)] * nc,
+            in_specs=[pl.BlockSpec(memory_space=pltpu.VMEM)],
+            out_specs=[pl.BlockSpec(memory_space=pl.ANY)] * nc,
+            scratch_shapes=[
+                pltpu.SemaphoreType.DMA((count,)),
+                pltpu.SemaphoreType.DMA((count,)),
+                pltpu.SemaphoreType.DMA,
+            ],
+            compiler_params=pltpu.CompilerParams(
+                vmem_limit_bytes=VMEM_LIMIT, collective_id=0, has_side_effects=True
+            ),
+            cost_estimate=cost(),
+            name="gather_all",
+        )(own)
+    )
+
+
 def combine(parts, kind, pieces=1):
     shape = parts[0].shape
     tile = 256 if pieces == 1 and shape[0] % 256 == 0 else shape[0]
@@ -240,16 +327,24 @@
 
 def slot_copies(info_ref, place, w_refs, slots_ref, sem):
     copies = []
+    flat = len(w_refs[0].shape) == 3
+    far, near = info_ref.shape[0] - 2, info_ref.shape[0] - 1
     for k, m in enumerate(place.masks):
-        block = w_refs[k].shape[2]
-        for i in range(place.nd):
-            copies.append(
-                pltpu.make_async_copy(
-                    w_refs[k].at[i],
-                    slots_ref.at[info_ref[0] ^ m, :, i * block : (i + 1) * block],
-                    sem.at[len(copies)],
+        block = w_refs[k].shape[-1]
+        for i in range(place.nn):
+            for f in range(place.nf):
+                if flat:
+                    source, at = w_refs[k].at[place.block(f, i)], place.block(f, i)
+                else:
+                    source, at = w_refs[k].at[i, f], place.block(info_ref[far] ^ f, info_ref[near] ^ i)
+                start = at * block if flat else pl.multiple_of(at * block, block)
+                copies.append(
+                    pltpu.make_async_copy(
+                        source,
+                        slots_ref.at[info_ref[0] ^ m, :, pl.ds(start, block)],
+                        sem.at[len(copies)],
+                    )
                 )
-            )
     return copies
 
 
@@ -1062,7 +1157,9 @@
         every = jnp.concatenate([*to_near, spot[None].astype(jnp.int32)], 0)
         positions = spot * slots + jnp.arange(slots, dtype=jnp.int32)
         cosine, sine = rope_tables(positions)
-        info = jnp.concatenate([spot[None].astype(jnp.int32), lengths])
+        info = jnp.concatenate(
+            [spot[None].astype(jnp.int32), lengths, jnp.stack([far, near]).astype(jnp.int32)]
+        )
         valid = (positions[None, :] < lengths[:, None]).astype(F32).reshape(n, 1)
         qgain2 = jnp.tile(query_gain, 2)[None, :]
         kgain2 = jnp.tile(key_gain, 2)[None, :]
@@ -1073,20 +1170,16 @@
             return lax.all_gather(value, place.dp, axis=0, tiled=tiled)
 
         bg = (cotangent.reshape(n, depth).astype(F32) * valid).astype(BF16)
-        qkv_dp = gather_dp(jnp.concatenate([w_query.T, w_key.T, w_value.T], 0), False)
-        qkv_cross = place.cross(
-            qkv_dp, bg, info, valid, cosine, sine, qgain2, kgain2, *to_near, every
-        )
-        qkv_cols = place.gather(qkv_cross)
-        out_dp = gather_dp(after(w_out.T, qkv_dp), False)
-        out_cross = place.cross(after(out_dp, *place.arrived(qkv_cross)))
+        qkv_cols = gather_all(place, jnp.concatenate([w_query.T, w_key.T, w_value.T], 0))
+        out_dp = gather_dp(w_out.T, False)
+        out_cross = place.cross(after(out_dp, qkv_cols[1]))
         sizes = [768, 512] if units == 1280 else [units]
         starts = [sum(sizes[:c]) for c in range(len(sizes))]
         chunks = []
         for start, size in zip(starts, sizes):
             at = slice(start, start + size)
             local = jnp.concatenate([w_gate[:, at], w_up[:, at], w_down[:, at]], 0)
-            chunks.append(gather_dp(after(local, qkv_dp), True))
+            chunks.append(gather_dp(after(local, qkv_cols[1]), True))
 
         normed, lin, q, kv = project(
             info, place, x, gain_one, qkv_cols, qc, kc, qgain2, kgain2, cosine, sine,

time: 731 us -> 687 us (0.940)
  waiting for transfers between devices: 225 us -> 128 us
  Pallas kernels: 417 us -> 474 us
    pallas_call x0 -> x1, Pallas kernels: none -> 56.8 us  [gather_all(): pl.pallas_call(body, out_shape=[jax.ShapeDtypeStruct((nn_, nf, columns, b...]
    all_gather x4 -> x3, waiting for transfers between devices: 52 us -> 0.24 us  [gather_dp(): return lax.all_gather(value, place.dp, axis=0, tiled=tiled)]
    ppermute x56 -> x53, waiting for transfers between devices: 173 us -> 127 us  [swap(): return lax.ppermute(value, axis, [(i, i ^ mask) for i in range(size)])]
    ppermute x56 -> x53, starting transfers between devices: 36.4 us -> 36.2 us  [swap(): return lax.ppermute(value, axis, [(i, i ^ mask) for i in range(size)])]
  transfers between devices with their start and end apart: 63 -> 59, of which waited for: 25 -> 23; matrix products, arithmetic and copies ran while one was open for 2% -> 2% of each run, Pallas kernels for 49% -> 61%
where the time goes in v4:
time: 687 us; the launch traced here: 681 us
  Pallas kernels  474 us (69%)
  waiting for transfers between devices  128 us (19%)
  starting transfers between devices  36.5 us (5%)
  local copies, waits for them, and re-layouts  16 us (2%)
  between operations  15 us (2%)
  other arithmetic  11.5 us (2%)
    ppermute x53, waiting for transfers between devices, swap(): return lax.ppermute(value, axis, [(i, i ^ mask) for i in range(size)])  127 us
    pallas_call x3, Pallas kernels, feed_forward(): pl.pallas_call(body, out_shape=(*[jax.ShapeDtypeStruct((tokens, depth), s...  121 us
    pallas_call x6, Pallas kernels, weight_grads(): pl.pallas_call(body, out_shape=shapes, grid_spec=pltpu.PrefetchScalarGrid...  76.5 us
    pallas_call x1, Pallas kernels, gather_all(): pl.pallas_call(body, out_shape=[jax.ShapeDtypeStruct((nn_, nf, columns, b...  56.8 us
    pallas_call x2, Pallas kernels, attend_back(): pl.pallas_call(body, out_shape=(jax.ShapeDtypeStruct((n, QW), F32), *[jax...  43.7 us
    ppermute x53, starting transfers between devices, swap(): return lax.ppermute(value, axis, [(i, i ^ mask) for i in range(size)])  36.2 us
    pallas_call x12, Pallas kernels, combine(): pl.pallas_call(body, out_shape=[jax.ShapeDtypeStruct(out, kind)] * pieces...  32.7 us
    pallas_call x2, Pallas kernels, attend(): pl.pallas_call(body, out_shape=(jax.ShapeDtypeStruct((n, QW), BF16), jax....  32.4 us
  transfers between devices with their start and end apart: 59, of which 23 were waited for; matrix products, arithmetic and copies ran while one was open for 2% of the time, Pallas kernels for 61%

profile of v4, /device:TPU:0, one launch (start us, length us, event | category | flops | bytes accessed | tf_op | source)
XLA Modules:
  0.0 681.3 jit_solution(17255308432462473042)
XLA Ops:
  9.7 56.8 %gather_all.1 = (bf16[2,4,480,256]{3,2,1,0:T(8,128)(2,1)}, bf16[2,4,480,256]{3,2,1,0:T(8,128)(2,1)}, bf16[2,4,480,256]{3,2,1,0:T(8,128)(2,1)}, bf16[2,4,480,256]{3,2,1,0:T(8,128)(2,1)}) custom-call(bf16[480,256]{1,0:T(8,128)(2,1)} %pad_maximum_fusion.2.own_ref), custom_call_target="tpu_custom_call" | custom-call | flops 1 | bytes 1 | tf_op jit(solution)/shard_map/gather_all/pallas_call | solution.py:199
  73.4 19.5 %project.1 = (bf16[512,2048]{1,0:T(8,128)(2,1)}, f32[4,512,480]{2,1,0:T(8,128)}, bf16[512,1280]{1,0:T(8,128)(2,1)}, bf16[512,640]{1,0:T(8,128)(2,1)}) custom-call(s32[5]{0:T(128)} %pad_add_fusion.info_ref, bf16[512,2048]{1,0:T(8,128)(2,1)} %bitcast.51, f32[1,2048]{1,0:T(1,128)} %bitcast.76, f32[1,128]{1,0:T(1,128)} %broadcast_in_dim_tile.6.qgain_ref, ...), custom_call_target="tpu_custom_call" | custom-call | flops 1 | bytes 1 | tf_op jit(solution)/shard_map/project/pallas_call | solution.py:401
  95.0 6.0 collective-permute-done.refs_2_.refs_8_
  103.0 11.4 %collective-permute-done.3.refs_2_ = bf16[512,640]{1,0:T(8,128)(2,1)S(1)} collective-permute-done((bf16[512,640]{1,0:T(8,128)(2,1)}, bf16[512,640]{1,0:T(8,128)(2,1)S(1)}, u32[]{:S(2)}, u32[]{:S(2)}) %collective-permute-start.3) | collective-permute-done | bytes 655392 | tf_op jit(solution)/shard_map/ppermute | solution.py:52
  120.5 16.1 %attend.2 = (bf16[256,1280]{1,0:T(8,128)(2,1)}, bf16[1280,256]{1,0:T(8,128)(2,1)}, f32[5,4,256]{2,1,0:T(4,128)}) custom-call(s32[5]{0:T(128)} %pad_add_fusion.info_ref, bf16[512,1280]{1,0:T(8,128)(2,1)} %get-tuple-element.152.q_ref, bf16[512,640]{1,0:T(8,128)(2,1)} %get-tuple-element.148.refs_0_, bf16[512,640]{1,0:T(8,128)(2,1)} %copy-done.7, ...), custom_call_target="tpu_custom_call" | custom-call | flops 1 | bytes 1 | tf_op jit(solution)/shard_map/attend/pallas_call | solution.py:641
  136.6 9.0 %out_project.2 = (f32[256,2048]{1,0:T(8,128)}, bf16[256,2048]{1,0:T(8,128)(2,1)}) custom-call(s32[5]{0:T(128)} %pad_add_fusion.info_ref, bf16[256,1280]{1,0:T(8,128)(2,1)} %get-tuple-element.149.mixed_ref, bf16[512,2048]{1,0:T(8,128)(2,1)} %bitcast.52, f32[1,2048]{1,0:T(1,128)} %bitcast.71, bf16[8,320,256]{2,1,0:T(8,128)(2,1)} %bitcast.58, ...), custom_call_target="tpu_custom_call" | custom-call | flops 1 | bytes 1 | tf_op jit(solution)/shard_map/out_project/pallas_call | solution.py:759
  146.9 16.3 %attend.3 = (bf16[256,1280]{1,0:T(8,128)(2,1)}, bf16[1280,256]{1,0:T(8,128)(2,1)}, f32[5,4,256]{2,1,0:T(4,128)}) custom-call(s32[5]{0:T(128)} %pad_add_fusion.info_ref, bf16[512,1280]{1,0:T(8,128)(2,1)} %get-tuple-element.152.q_ref, bf16[512,640]{1,0:T(8,128)(2,1)} %get-tuple-element.148.refs_0_, bf16[512,640]{1,0:T(8,128)(2,1)} %copy-done.7, ...), custom_call_target="tpu_custom_call" | custom-call | flops 1 | bytes 1 | tf_op jit(solution)/shard_map/attend/pallas_call | solution.py:641
  163.3 20.9 %collective-permute-done.6.refs_4_.refs_0_ = bf16[256,2048]{1,0:T(8,128)(2,1)S(1)} collective-permute-done((bf16[256,2048]{1,0:T(8,128)(2,1)}, bf16[256,2048]{1,0:T(8,128)(2,1)S(1)}, u32[]{:S(2)}, u32[]{:S(2)}) %collective-permute-start.6) | collective-permute-done | bytes 1048608 | tf_op jit(solution)/shard_map/ppermute | solution.py:52
  184.1 9.0 %out_project.3 = (f32[256,2048]{1,0:T(8,128)}, bf16[256,2048]{1,0:T(8,128)(2,1)}) custom-call(s32[5]{0:T(128)} %pad_add_fusion.info_ref, bf16[256,1280]{1,0:T(8,128)(2,1)} %get-tuple-element.156.mixed_ref, bf16[512,2048]{1,0:T(8,128)(2,1)} %bitcast.53, f32[1,2048]{1,0:T(1,128)} %bitcast.72, bf16[8,320,256]{2,1,0:T(8,128)(2,1)} %bitcast.59, ...), custom_call_target="tpu_custom_call" | custom-call | flops 1 | bytes 1 | tf_op jit(solution)/shard_map/out_project/pallas_call | solution.py:759
  196.1 23.0 %collective-permute-done.11.refs_5_.refs_1_ = bf16[256,2048]{1,0:T(8,128)(2,1)} collective-permute-done((bf16[256,2048]{1,0:T(8,128)(2,1)}, bf16[256,2048]{1,0:T(8,128)(2,1)}, u32[]{:S(2)}, u32[]{:S(2)}) %collective-permute-start.11) | collective-permute-done | bytes 1048608 | tf_op jit(solution)/shard_map/ppermute | solution.py:52
  221.0 5.8 collective-permute-done.12.refs_6_.refs_2_
  227.4 58.6 %feed_forward.3 = (f32[512,2048]{1,0:T(8,128)}, f32[512,2048]{1,0:T(8,128)}, f32[512,2048]{1,0:T(8,128)}, f32[512,2048]{1,0:T(8,128)}, f32[512,2048]{1,0:T(8,128...) custom-call(s32[5]{0:T(128)} %pad_add_fusion.info_ref, ...), custom_call_target="tpu_custom_call" | custom-call | flops 1 | bytes 1 | tf_op jit(solution)/shard_map/feed_forward/pallas_call | solution.py:1005
  286.1 17.5 %weight_grads.6 = bf16[4,3,768,256]{3,2,1,0:T(8,128)(2,1)} custom-call(s32[4]{0:T(128)} %fusion.4.order_ref, bf16[256,2048]{1,0:T(8,128)(2,1)} %get-tuple-element.154.refs_0_, bf16[256,2048]{1,0:T(8,128)(2,1)} %get-tuple-element.159.refs_1_, bf16[256,2048]{1,0:T(8,128)(2,1)} %collective-permute-done.7.refs_2_, bf16[256,2048]{1,0:T(8,128)(2,1)} %copy-done.3, ...), custom_call_target="tpu_custom_call" | custom-call | flops 1 | bytes 1 | tf_op jit(solution)/shard_map/weight_grads/pallas_call | solution.py:1068
  303.8 37.3 %feed_forward.4 = (bf16[512,2048]{1,0:T(8,128)(2,1)}, bf16[512,2048]{1,0:T(8,128)(2,1)}, bf16[512,2048]{1,0:T(8,128)(2,1)}, bf16[512,2048]{1,0:T(8,128)(2,1)}, b...) custom-call(s32[5]{0:T(128)} %pad_add_fusion.info_ref, ...), custom_call_target="tpu_custom_call" | custom-call | flops 1 | bytes 1 | tf_op jit(solution)/shard_map/feed_forward/pallas_call | solution.py:1005
  341.2 4.3 collective-permute-done.17.refs_1_
  352.3 24.7 %feed_forward.5 = (bf16[512,2048]{1,0:T(8,128)(2,1)}, bf16[512,2048]{1,0:T(8,128)(2,1)}, bf16[512,2048]{1,0:T(8,128)(2,1)}, bf16[512,2048]{1,0:T(8,128)(2,1)}, b...) custom-call(s32[5]{0:T(128)} %pad_add_fusion.info_ref, ...), custom_call_target="tpu_custom_call", output_to_operand_aliasing={{4}: (12, {}), {5}: (13, {}), {6}: (14, {})} | custom-call | flops 1 | bytes 1 | tf_op jit(solution)/shard_map/feed_forward/pallas_call | solution.py:1005
  377.0 13.3 %weight_grads.7 = bf16[4,3,512,256]{3,2,1,0:T(8,128)(2,1)} custom-call(s32[4]{0:T(128)} %fusion.4.order_ref, bf16[256,2048]{1,0:T(8,128)(2,1)} %get-tuple-element.154.refs_0_, bf16[256,2048]{1,0:T(8,128)(2,1)} %get-tuple-element.159.refs_1_, bf16[256,2048]{1,0:T(8,128)(2,1)} %collective-permute-done.7.refs_2_, bf16[256,2048]{1,0:T(8,128)(2,1)} %copy-done.3, ...), custom_call_target="tpu_custom_call" | custom-call | flops 1 | bytes 1 | tf_op jit(solution)/shard_map/weight_grads/pallas_call | solution.py:1068
  390.3 7.8 %collective-permute-done.18.refs_1_ = bf16[512,2048]{1,0:T(8,128)(2,1)S(1)} collective-permute-done((bf16[512,2048]{1,0:T(8,128)(2,1)}, bf16[512,2048]{1,0:T(8,128)(2,1)S(1)}, u32[]{:S(2)}, u32[]{:S(2)}) %collective-permute-start.18) | collective-permute-done | bytes 2097184 | tf_op jit(solution)/shard_map/ppermute | solution.py:52
  406.1 14.9 %middle_back.1 = (f32[512,2048]{1,0:T(8,128)}, bf16[512,2048]{1,0:T(8,128)(2,1)}, bf16[512,1280]{1,0:T(8,128)(2,1)}, f32[1,2048]{1,0:T(1,128)}) custom-call(s32[5]{0:T(128)} %pad_add_fusion.info_ref, bf16[512,2048]{1,0:T(8,128)(2,1)} %combine.13.refs_0_, bf16[512,2048]{1,0:T(8,128)(2,1)} %copy-done.10, f32[256,2048]{1,0:T(8,128)} %get-tuple-element.151.refs_2_.refs_0_, ...), custom_call_target="tpu_custom_call" | custom-call | flops 1 | bytes 1 | tf_op jit(solution)/shard_map/middle_back/pallas_call | solution.py:824
  421.0 9.2 %out_weight_grads.1 = (bf16[8,320,256]{2,1,0:T(8,128)(2,1)}, bf16[8,320,256]{2,1,0:T(8,128)(2,1)}, bf16[8,320,256]{2,1,0:T(8,128)(2,1)}, bf16[8,320,256]{2,1,0:T(8,128)(2,1)}) custom-call(s32[9]{0:T(128)} %pad_add_fusion.1.order_ref, bf16[512,2048]{1,0:T(8,128)(2,1)} %get-tuple-element.201.left_ref, bf16[1280,256]{1,0:T(8,128)(2,1)} %get-tuple-element.202.refs_0_, ...), custom_call_target="tpu_custom_call" | custom-call | flops 1 | bytes 1 | tf_op jit(solution)/shard_map/out_weight_grads/pallas_call | solution.py:1098
  437.6 21.9 %attend_back.2 = (f32[256,1280]{1,0:T(8,128)}, bf16[256,640]{1,0:T(8,128)(2,1)}, bf16[256,640]{1,0:T(8,128)(2,1)}, bf16[256,640]{1,0:T(8,128)(2,1)}, bf16[256,640]{1,0:T(8,128)(2,1)}) custom-call(s32[5]{0:T(128)} %pad_add_fusion.info_ref, bf16[512,1280]{1,0:T(8,128)(2,1)} %get-tuple-element.152.q_ref, bf16[512,1280]{1,0:T(8,128)(2,1)} %get-tuple-element.192.do_ref, ...), custom_call_target="tpu_custom_call" | custom-call | flops 1 | bytes 1 | tf_op jit(solution)/shard_map/attend_back/pallas_call | solution.py:712
  459.5 17.9 %weight_grads.8 = bf16[4,3,768,256]{3,2,1,0:T(8,128)(2,1)} custom-call(s32[4]{0:T(128)} %copy-done.32, bf16[256,2048]{1,0:T(8,128)(2,1)} %get-tuple-element.154.refs_0_, bf16[256,2048]{1,0:T(8,128)(2,1)} %get-tuple-element.159.refs_1_, bf16[256,2048]{1,0:T(8,128)(2,1)} %collective-permute-done.7.refs_2_, bf16[256,2048]{1,0:T(8,128)(2,1)} %copy-done.3, ...), custom_call_target="tpu_custom_call" | custom-call | flops 1 | bytes 1 | tf_op jit(solution)/shard_map/weight_grads/pallas_call | solution.py:1068
  492.0 21.8 %attend_back.3 = (f32[256,1280]{1,0:T(8,128)}, bf16[256,640]{1,0:T(8,128)(2,1)}, bf16[256,640]{1,0:T(8,128)(2,1)}, bf16[256,640]{1,0:T(8,128)(2,1)}, bf16[256,640]{1,0:T(8,128)(2,1)}) custom-call(s32[5]{0:T(128)} %pad_add_fusion.info_ref, bf16[512,1280]{1,0:T(8,128)(2,1)} %get-tuple-element.152.q_ref, bf16[512,1280]{1,0:T(8,128)(2,1)} %get-tuple-element.192.do_ref, ...), custom_call_target="tpu_custom_call" | custom-call | flops 1 | bytes 1 | tf_op jit(solution)/shard_map/attend_back/pallas_call | solution.py:712
  528.5 11.6 %heads_back.2 = (bf16[4,256,480]{2,1,0:T(8,128)(2,1)}, f32[1,128]{1,0:T(1,128)}, f32[1,128]{1,0:T(1,128)}, bf16[480,256]{1,0:T(8,128)(2,1)}, bf16[480,256]{1,0:T...) custom-call(s32[5]{0:T(128)} %pad_add_fusion.info_ref, f32[256,1280]{1,0:T(8,128)} %get-tuple-element.209.dq_ref, ...), custom_call_target="tpu_custom_call" | custom-call | flops 1 | bytes 1 | tf_op jit(solution)/shard_map/heads_back/pallas_call | solution.py:503
  540.8 11.8 %heads_back.3 = (bf16[4,256,480]{2,1,0:T(8,128)(2,1)}, f32[1,128]{1,0:T(1,128)}, f32[1,128]{1,0:T(1,128)}, bf16[480,256]{1,0:T(8,128)(2,1)}, bf16[480,256]{1,0:T...) custom-call(s32[5]{0:T(128)} %pad_add_fusion.info_ref, f32[256,1280]{1,0:T(8,128)} %get-tuple-element.214.dq_ref, ...), custom_call_target="tpu_custom_call" | custom-call | flops 1 | bytes 1 | tf_op jit(solution)/shard_map/heads_back/pallas_call | solution.py:503
  552.7 13.5 %weight_grads.9 = bf16[4,3,512,256]{3,2,1,0:T(8,128)(2,1)} custom-call(s32[4]{0:T(128)} %copy-done.32, bf16[256,2048]{1,0:T(8,128)(2,1)} %get-tuple-element.154.refs_0_, bf16[256,2048]{1,0:T(8,128)(2,1)} %get-tuple-element.159.refs_1_, bf16[256,2048]{1,0:T(8,128)(2,1)} %collective-permute-done.7.refs_2_, bf16[256,2048]{1,0:T(8,128)(2,1)} %copy-done.3, ...), custom_call_target="tpu_custom_call" | custom-call | flops 1 | bytes 1 | tf_op jit(solution)/shard_map/weight_grads/pallas_call | solution.py:1068
  582.1 13.8 %project_back.1 = (bf16[512,2048]{1,0:T(8,128)(2,1)}, f32[1,2048]{1,0:T(1,128)}) custom-call(s32[5]{0:T(128)} %pad_add_fusion.info_ref, bf16[512,2048]{1,0:T(8,128)(2,1)} %bitcast.54, f32[512,2048]{1,0:T(8,128)} %get-tuple-element.231.mid_ref, f32[1,2048]{1,0:T(1,128)} %bitcast.77, bf16[4,256,480]{2,1,0:T(8,128)(2,1)} %get-tuple-element.223.refs_0_, ...), custom_call_target="tpu_custom_call" | custom-call | flops 1 | bytes 1 | tf_op jit(solution)/shard_map/project_back/pallas_call | solution.py:572
  601.4 7.0 %weight_grads.10 = bf16[4,1,480,256]{3,2,1,0:T(8,128)(2,1)} custom-call(s32[4]{0:T(128)} %get-tuple-element.233.order_ref, bf16[512,2048]{1,0:T(8,128)(2,1)} %get-tuple-element.165.refs_0_, bf16[512,2048]{1,0:T(8,128)(2,1)} %collective-permute-done.16.refs_1_, bf16[512,2048]{1,0:T(8,128)(2,1)} %collective-permute-done.15.refs_2_, ...), custom_call_target="tpu_custom_call" | custom-call | flops 1 | bytes 1 | tf_op jit(solution)/shard_map/weight_grads/pallas_call | solution.py:1068
  625.3 9.8 %collective-permute-done.46.refs_12_ = bf16[4,1,480,256]{3,2,1,0:T(8,128)(2,1)S(1)} collective-permute-done((bf16[4,1,480,256]{3,2,1,0:T(8,128)(2,1)}, bf16[4,1,480,256]{3,2,1,0:T(8,128)(2,1)S(1)}, u32[]{:S(2)}, u32[]{:S(2)}) %collective-permute-start.46) | collective-permute-done | bytes 983072 | tf_op jit(solution)/shard_map/ppermute | solution.py:52
  636.1 7.4 %weight_grads.11 = (bf16[1,480,256]{2,1,0:T(8,128)(2,1)}, bf16[1,480,256]{2,1,0:T(8,128)(2,1)}, bf16[1,480,256]{2,1,0:T(8,128)(2,1)}, bf16[1,480,256]{2,1,0:T(8,128)(2,1)}) custom-call(s32[4]{0:T(128)} %get-tuple-element.249.order_ref, bf16[512,2048]{1,0:T(8,128)(2,1)} %get-tuple-element.165.refs_0_, bf16[512,2048]{1,0:T(8,128)(2,1)} %collective-permute-done.16.refs_1_, ...), custom_call_target="tpu_custom_call" | custom-call | flops 1 | bytes 1 | tf_op jit(solution)/shard_map/weight_grads/pallas_call | solution.py:1068
  659.0 6.6 finish_rows.1
  665.6 7.2 %collective-permute-done.49 = bf16[1,480,256]{2,1,0:T(8,128)(2,1)S(1)} collective-permute-done((bf16[1,480,256]{2,1,0:T(8,128)(2,1)}, bf16[1,480,256]{2,1,0:T(8,128)(2,1)S(1)}, u32[]{:S(2)}, u32[]{:S(2)}) %collective-permute-start.49) | collective-permute-done | bytes 245792 | tf_op jit(solution)/shard_map/ppermute | solution.py:52
  (267 shorter events, 134.5 us)
Async XLA Ops:
  7.2 61.8 %all-gather.9.cloned.1.call-start = ((), (), s32[]{:S(2)}) async-start(), calls=%async_computation.8 | async-start | bytes 1474560 | tf_op jit(solution)/shard_map/all_gather | solution.py:1170
  8.0 219.5 %all-gather.5.cloned.1.call-start = ((), (), s32[]{:S(2)}) async-start(), calls=%async_computation.3 | async-start | bytes 10616832 | tf_op jit(solution)/shard_map/all_gather | solution.py:1170
  67.6 236.2 %all-gather.7.cloned.1.call-start = ((), (), s32[]{:S(2)}) async-start(), calls=%async_computation.4 | async-start | bytes 7077888 | tf_op jit(solution)/shard_map/all_gather | solution.py:1170
  68.9 513.1 %reduce-scatter.4.cloned.1.call-start = ((), (), s32[]{:S(2)}) async-start(), calls=%async_computation.5 | async-start | bytes 5898240 | tf_op jit(solution)/shard_map/reduce_scatter | solution.py:1237
  69.0 32.0 %collective-permute-start = (bf16[8,320,256]{2,1,0:T(8,128)(2,1)}, bf16[8,320,256]{2,1,0:T(8,128)(2,1)}, u32[]{:S(2)}, u32[]{:S(2)}) collective-permute-start(bf16[8,320,256]{2,1,0:T(8,128)(2,1)} %bitcast.57), channel_id=1, source_target_pairs={{0,2},{1,3},{2,0},{3,1},{4,6},{5,7},{6,4},{7,5},{8,10},{9,11},{10,... | collective-permute-start | bytes 3932168 | tf_op jit(solution)/shard_map/ppermute | solution.py:52
  93.0 21.4 %collective-permute-start.3 = (bf16[512,640]{1,0:T(8,128)(2,1)}, bf16[512,640]{1,0:T(8,128)(2,1)S(1)}, u32[]{:S(2)}, u32[]{:S(2)}) collective-permute-start(bf16[512,640]{1,0:T(8,128)(2,1)} %get-tuple-element.148.refs_0_), channel_id=1, source_target_pairs={{0,2},{1,3},{2,0},{3,1},{4,6},{5,7},{6,4},{7,5},{8,10},{9,11},{10,... | collective-permute-start | bytes 1966088 | tf_op jit(solution)/shard_map/ppermute | solution.py:52
  94.4 20.0 %collective-permute-start.2 = (bf16[512,640]{1,0:T(8,128)(2,1)}, bf16[512,640]{1,0:T(8,128)(2,1)S(1)}, u32[]{:S(2)}, u32[]{:S(2)}) collective-permute-start(bf16[512,640]{1,0:T(8,128)(2,1)} %get-tuple-element.148.refs_0_), channel_id=1, source_target_pairs={{0,1},{1,0},{2,3},{3,2},{4,5},{5,4},{6,7},{7,6},{8,9},{9,8},{10,11... | collective-permute-start | bytes 1966088 | tf_op jit(solution)/shard_map/ppermute | solution.py:52
  94.5 21.3 %collective-permute-start.1 = (bf16[8,320,256]{2,1,0:T(8,128)(2,1)S(1)}, bf16[8,320,256]{2,1,0:T(8,128)(2,1)S(1)}, u32[]{:S(2)}, u32[]{:S(2)}) collective-permute-start(bf16[8,320,256]{2,1,0:T(8,128)(2,1)S(1)} %bitcast.61), channel_id=1, source_target_pairs={{0,1},{1,0},{2,3},{3,2},{4,5},{5,4},{6,7},{7,6},{8,9},{9,8},{10,11... | collective-permute-start | bytes 3932168 | tf_op jit(solution)/shard_map/ppermute | solution.py:52
  101.0 35.6 %collective-permute-start.5 = (bf16[8,320,256]{2,1,0:T(8,128)(2,1)}, bf16[8,320,256]{2,1,0:T(8,128)(2,1)}, u32[]{:S(2)}, u32[]{:S(2)}) collective-permute-start(bf16[8,320,256]{2,1,0:T(8,128)(2,1)} %collective-permute-done.refs_2_.refs_8_), channel_id=1, source_target_pairs={{0,1},{1,0},{2,3},{3,2},{4,5},{5,4},{6,7},{7,6},{8,9},{9,8},{10,11... | collective-permute-start | bytes 3932168 | tf_op jit(solution)/shard_map/ppermute | solution.py:52
  114.4 48.9 %collective-permute-start.8 = (bf16[512,2048]{1,0:T(8,128)(2,1)S(1)}, bf16[512,2048]{1,0:T(8,128)(2,1)}, u32[]{:S(2)}, u32[]{:S(2)}) collective-permute-start(bf16[512,2048]{1,0:T(8,128)(2,1)S(1)} %fusion.refs_8_.refs_4_), channel_id=1, source_target_pairs={{0,2},{1,3},{2,0},{3,1},{4,6},{5,7},{6,4},{7,5},{8,10},{9,11},{10,... | collective-permute-start | bytes 6291464 | tf_op jit(solution)/shard_map/ppermute | solution.py:52
  115.3 48.0 %collective-permute-start.9 = (bf16[512,2048]{1,0:T(8,128)(2,1)S(1)}, bf16[512,2048]{1,0:T(8,128)(2,1)}, u32[]{:S(2)}, u32[]{:S(2)}) collective-permute-start(bf16[512,2048]{1,0:T(8,128)(2,1)S(1)} %fusion.refs_8_.refs_4_), channel_id=1, source_target_pairs={{0,1},{1,0},{2,3},{3,2},{4,5},{5,4},{6,7},{7,6},{8,9},{9,8},{10,11... | collective-permute-start | bytes 6291464 | tf_op jit(solution)/shard_map/ppermute | solution.py:52
  145.6 38.5 %collective-permute-start.6 = (bf16[256,2048]{1,0:T(8,128)(2,1)}, bf16[256,2048]{1,0:T(8,128)(2,1)S(1)}, u32[]{:S(2)}, u32[]{:S(2)}) collective-permute-start(bf16[256,2048]{1,0:T(8,128)(2,1)} %get-tuple-element.154.refs_0_), channel_id=1, source_target_pairs={{0,2},{1,3},{2,0},{3,1},{4,6},{5,7},{6,4},{7,5},{8,10},{9,11},{10,... | collective-permute-start | bytes 3145736 | tf_op jit(solution)/shard_map/ppermute | solution.py:52
  146.9 37.2 %collective-permute-start.7 = (bf16[256,2048]{1,0:T(8,128)(2,1)}, bf16[256,2048]{1,0:T(8,128)(2,1)}, u32[]{:S(2)}, u32[]{:S(2)}) collective-permute-start(bf16[256,2048]{1,0:T(8,128)(2,1)} %get-tuple-element.154.refs_0_), channel_id=1, source_target_pairs={{0,1},{1,0},{2,3},{3,2},{4,5},{5,4},{6,7},{7,6},{8,9},{9,8},{10,11... | collective-permute-start | bytes 3145736 | tf_op jit(solution)/shard_map/ppermute | solution.py:52
  193.2 25.9 %collective-permute-start.11 = (bf16[256,2048]{1,0:T(8,128)(2,1)}, bf16[256,2048]{1,0:T(8,128)(2,1)}, u32[]{:S(2)}, u32[]{:S(2)}) collective-permute-start(bf16[256,2048]{1,0:T(8,128)(2,1)} %get-tuple-element.159.refs_1_), channel_id=1, source_target_pairs={{0,2},{1,3},{2,0},{3,1},{4,6},{5,7},{6,4},{7,5},{8,10},{9,11},{10,... | collective-permute-start | bytes 3145736 | tf_op jit(solution)/shard_map/ppermute | solution.py:52
  194.1 26.9 %collective-permute-start.14 = (bf16[512,2048]{1,0:T(8,128)(2,1)}, bf16[512,2048]{1,0:T(8,128)(2,1)S(1)}, u32[]{:S(2)}, u32[]{:S(2)}) collective-permute-start(bf16[512,2048]{1,0:T(8,128)(2,1)} %collective-permute-done.8.refs_10_.refs_4_), channel_id=1, source_target_pairs={{0,1},{1,0},{2,3},{3,2},{4,5},{5,4},{6,7},{7,6},{8,9},{9,8},{10,11... | collective-permute-start | bytes 6291464 | tf_op jit(solution)/shard_map/ppermute | solution.py:52
  219.1 84.5 %collective-permute-start.15 = (bf16[512,2048]{1,0:T(8,128)(2,1)}, bf16[512,2048]{1,0:T(8,128)(2,1)}, u32[]{:S(2)}, u32[]{:S(2)}) collective-permute-start(bf16[512,2048]{1,0:T(8,128)(2,1)} %get-tuple-element.165.refs_0_), channel_id=1, source_target_pairs={{0,2},{1,3},{2,0},{3,1},{4,6},{5,7},{6,4},{7,5},{8,10},{9,11},{10,... | collective-permute-start | bytes 6291464 | tf_op jit(solution)/shard_map/ppermute | solution.py:52
  219.9 83.7 %collective-permute-start.16 = (bf16[512,2048]{1,0:T(8,128)(2,1)}, bf16[512,2048]{1,0:T(8,128)(2,1)}, u32[]{:S(2)}, u32[]{:S(2)}) collective-permute-start(bf16[512,2048]{1,0:T(8,128)(2,1)} %get-tuple-element.165.refs_0_), channel_id=1, source_target_pairs={{0,1},{1,0},{2,3},{3,2},{4,5},{5,4},{6,7},{7,6},{8,9},{9,8},{10,11... | collective-permute-start | bytes 6291464 | tf_op jit(solution)/shard_map/ppermute | solution.py:52
  350.3 47.9 %collective-permute-start.18 = (bf16[512,2048]{1,0:T(8,128)(2,1)}, bf16[512,2048]{1,0:T(8,128)(2,1)S(1)}, u32[]{:S(2)}, u32[]{:S(2)}) collective-permute-start(bf16[512,2048]{1,0:T(8,128)(2,1)} %combine.12), channel_id=1, source_target_pairs={{0,2},{1,3},{2,0},{3,1},{4,6},{5,7},{6,4},{7,5},{8,10},{9,11},{10,... | collective-permute-start | bytes 6291464 | tf_op jit(solution)/shard_map/ppermute | solution.py:52
  351.8 107.8 %collective-permute-start.23 = (bf16[4,3,768,256]{3,2,1,0:T(8,128)(2,1)}, bf16[4,3,768,256]{3,2,1,0:T(8,128)(2,1)}, u32[]{:S(2)}, u32[]{:S(2)}) collective-permute-start(bf16[4,3,768,256]{3,2,1,0:T(8,128)(2,1)} %weight_grads.6), channel_id=1, source_target_pairs={{0,4},{4,0},{1,5},{5,1},{2,6},{6,2},{3,7},{7,3},{8,12},{12,8},{9,1... | collective-permute-start | bytes 14155784 | tf_op jit(solution)/shard_map/ppermute | solution.py:52
  477.4 172.0 %reduce-scatter.8.cloned.1.call-start = ((), (), s32[]{:S(2)}) async-start(), calls=%async_computation.7 | async-start | bytes 3932160 | tf_op jit(solution)/shard_map/reduce_scatter | solution.py:1237
  477.5 75.2 %collective-permute-start.32 = (bf16[4,3,512,256]{3,2,1,0:T(8,128)(2,1)}, bf16[4,3,512,256]{3,2,1,0:T(8,128)(2,1)}, u32[]{:S(2)}, u32[]{:S(2)}) collective-permute-start(bf16[4,3,512,256]{3,2,1,0:T(8,128)(2,1)} %weight_grads.7), channel_id=1, source_target_pairs={{0,4},{4,0},{1,5},{5,1},{2,6},{6,2},{3,7},{7,3},{8,12},{12,8},{9,1... | collective-permute-start | bytes 9437192 | tf_op jit(solution)/shard_map/ppermute | solution.py:52
  478.6 74.0 %collective-permute-start.31 = (bf16[8,320,256]{2,1,0:T(8,128)(2,1)}, bf16[8,320,256]{2,1,0:T(8,128)(2,1)S(1)}, u32[]{:S(2)}, u32[]{:S(2)}) collective-permute-start(bf16[8,320,256]{2,1,0:T(8,128)(2,1)} %combine.16), channel_id=1, source_target_pairs={{0,2},{1,3},{2,0},{3,1},{4,6},{5,7},{6,4},{7,5},{8,10},{9,11},{10,... | collective-permute-start | bytes 3932168 | tf_op jit(solution)/shard_map/ppermute | solution.py:52
  482.6 31.8 %collective-permute-start.25 = (bf16[256,640]{1,0:T(8,128)(2,1)}, bf16[256,640]{1,0:T(8,128)(2,1)S(1)}, u32[]{:S(2)}, u32[]{:S(2)}) collective-permute-start(bf16[256,640]{1,0:T(8,128)(2,1)} %get-tuple-element.216), channel_id=1, source_target_pairs={{0,1},{1,0},{2,3},{3,2},{4,5},{5,4},{6,7},{7,6},{8,9},{9,8},{10,11... | collective-permute-start | bytes 983048 | tf_op jit(solution)/shard_map/ppermute | solution.py:52
  520.3 19.8 %collective-permute-start.30 = (bf16[256,640]{1,0:T(8,128)(2,1)}, bf16[256,640]{1,0:T(8,128)(2,1)S(1)}, u32[]{:S(2)}, u32[]{:S(2)}) collective-permute-start(bf16[256,640]{1,0:T(8,128)(2,1)} %combine.18), channel_id=1, source_target_pairs={{0,2},{1,3},{2,0},{3,1},{4,6},{5,7},{6,4},{7,5},{8,10},{9,11},{10,... | collective-permute-start | bytes 983048 | tf_op jit(solution)/shard_map/ppermute | solution.py:52
  566.3 91.0 %reduce-scatter.6.cloned.1.call-start = ((), (), s32[]{:S(2)}) async-start(), calls=%async_computation.6 | async-start | bytes 819200 | tf_op jit(solution)/shard_map/reduce_scatter | solution.py:1323
  575.1 21.5 %collective-permute-start.35 = (bf16[480,256]{1,0:T(8,128)(2,1)}, bf16[480,256]{1,0:T(8,128)(2,1)S(1)}, u32[]{:S(2)}, u32[]{:S(2)}) collective-permute-start(bf16[480,256]{1,0:T(8,128)(2,1)} %get-tuple-element.238), channel_id=1, source_target_pairs={{0,2},{1,3},{2,0},{3,1},{4,6},{5,7},{6,4},{7,5},{8,10},{9,11},{10,... | collective-permute-start | bytes 737288 | tf_op jit(solution)/shard_map/ppermute | solution.py:52
  576.8 21.5 %collective-permute-start.37 = (bf16[480,256]{1,0:T(8,128)(2,1)}, bf16[480,256]{1,0:T(8,128)(2,1)S(1)}, u32[]{:S(2)}, u32[]{:S(2)}) collective-permute-start(bf16[480,256]{1,0:T(8,128)(2,1)} %get-tuple-element.240), channel_id=1, source_target_pairs={{0,3},{1,2},{2,1},{3,0},{4,7},{5,6},{6,5},{7,4},{8,11},{9,10},{10,... | collective-permute-start | bytes 737288 | tf_op jit(solution)/shard_map/ppermute | solution.py:52
  580.3 19.8 %collective-permute-start.36 = (bf16[480,256]{1,0:T(8,128)(2,1)S(1)}, bf16[480,256]{1,0:T(8,128)(2,1)S(1)}, u32[]{:S(2)}, u32[]{:S(2)}) collective-permute-start(bf16[480,256]{1,0:T(8,128)(2,1)S(1)} %copy-done.36), channel_id=1, source_target_pairs={{0,2},{1,3},{2,0},{3,1},{4,6},{5,7},{6,4},{7,5},{8,10},{9,11},{10,... | collective-permute-start | bytes 737288 | tf_op jit(solution)/shard_map/ppermute | solution.py:52
  608.4 50.6 %collective-permute-start.42 = (bf16[512,2048]{1,0:T(8,128)(2,1)S(1)}, bf16[512,2048]{1,0:T(8,128)(2,1)}, u32[]{:S(2)}, u32[]{:S(2)}) collective-permute-start(bf16[512,2048]{1,0:T(8,128)(2,1)S(1)} %copy-done.9), channel_id=1, source_target_pairs={{0,2},{1,3},{2,0},{3,1},{4,6},{5,7},{6,4},{7,5},{8,10},{9,11},{10,... | collective-permute-start | bytes 6291464 | tf_op jit(solution)/shard_map/ppermute | solution.py:52
  609.8 25.3 %collective-permute-start.46 = (bf16[4,1,480,256]{3,2,1,0:T(8,128)(2,1)}, bf16[4,1,480,256]{3,2,1,0:T(8,128)(2,1)S(1)}, u32[]{:S(2)}, u32[]{:S(2)}) collective-permute-start(bf16[4,1,480,256]{3,2,1,0:T(8,128)(2,1)} %weight_grads.10), channel_id=1, source_target_pairs={{0,4},{4,0},{1,5},{5,1},{2,6},{6,2},{3,7},{7,3},{8,12},{12,8},{9,1... | collective-permute-start | bytes 2949128 | tf_op jit(solution)/shard_map/ppermute | solution.py:52
  652.2 20.5 %collective-permute-start.49 = (bf16[1,480,256]{2,1,0:T(8,128)(2,1)}, bf16[1,480,256]{2,1,0:T(8,128)(2,1)S(1)}, u32[]{:S(2)}, u32[]{:S(2)}) collective-permute-start(bf16[1,480,256]{2,1,0:T(8,128)(2,1)} %get-tuple-element.254), channel_id=1, source_target_pairs={{0,16},{8,24},{16,0},{24,8},{1,17},{9,25},{17,1},{25,9},{2,18},{10... | collective-permute-start | bytes 737288 | tf_op jit(solution)/shard_map/ppermute | solution.py:52
  653.8 18.9 %collective-permute-start.50 = (bf16[1,480,256]{2,1,0:T(8,128)(2,1)S(1)}, bf16[1,480,256]{2,1,0:T(8,128)(2,1)S(1)}, u32[]{:S(2)}, u32[]{:S(2)}) collective-permute-start(bf16[1,480,256]{2,1,0:T(8,128)(2,1)S(1)} %copy-done.38), channel_id=1, source_target_pairs={{0,24},{8,16},{16,8},{24,0},{1,25},{9,17},{17,9},{25,1},{2,26},{10... | collective-permute-start | bytes 737288 | tf_op jit(solution)/shard_map/ppermute | solution.py:52
  (78 other events, 766.8 us)
Sparse Core Ops, SparseCore 0:
  10.2 54.6 all-gather.8
  67.8 136.5 all-gather.4
  206.6 97.1 all-gather.6
  477.6 83.4 reduce-scatter.3
  566.4 60.7 reduce-scatter.7
  629.3 22.1 reduce-scatter.5

commit v5 on v4

--- a/solution.py
+++ b/solution.py
@@ -632,7 +632,7 @@
                 qh = q_ref[:, h * HD : (h + 1) * HD]
                 e = jnp.exp(nt(k, qh) + bias_ref[...])
                 l = jnp.sum(e, 0, keepdims=True)
-                o = tn(v, (e * (1.0 / l)).astype(BF16))
+                o = tn(v, e.astype(BF16)) * (1.0 / l)
                 o_ref[:, h * HD : (h + 1) * HD] = o.T.astype(BF16)
                 ot_ref[h * HD : (h + 1) * HD, :] = o.astype(BF16)
                 lse_ref[0, h : h + 1, :] = jnp.log(l)

time: 687 us -> 687 us (level)
  transfers between devices with their start and end apart: 59 -> 59, of which waited for: 23 -> 24; matrix products, arithmetic and copies ran while one was open for 2% -> 2% of each run, Pallas kernels for 61% -> 60%
where the time goes in v5:
time: 687 us; the launch traced here: 681 us
  Pallas kernels  468 us (68%)
  waiting for transfers between devices  134 us (20%)
  starting transfers between devices  36.5 us (5%)
  local copies, waits for them, and re-layouts  16 us (2%)
  between operations  15 us (2%)
  other arithmetic  11.5 us (2%)
    ppermute x53, waiting for transfers between devices, swap(): return lax.ppermute(value, axis, [(i, i ^ mask) for i in range(size)])  133 us
    pallas_call x3, Pallas kernels, feed_forward(): pl.pallas_call(body, out_shape=(*[jax.ShapeDtypeStruct((tokens, depth), s...  121 us
    pallas_call x6, Pallas kernels, weight_grads(): pl.pallas_call(body, out_shape=shapes, grid_spec=pltpu.PrefetchScalarGrid...  76.5 us
    pallas_call x1, Pallas kernels, gather_all(): pl.pallas_call(body, out_shape=[jax.ShapeDtypeStruct((nn_, nf, columns, b...  56.8 us
    pallas_call x2, Pallas kernels, attend_back(): pl.pallas_call(body, out_shape=(jax.ShapeDtypeStruct((n, QW), F32), *[jax...  43.7 us
    ppermute x53, starting transfers between devices, swap(): return lax.ppermute(value, axis, [(i, i ^ mask) for i in range(size)])  36.2 us
    pallas_call x12, Pallas kernels, combine(): pl.pallas_call(body, out_shape=[jax.ShapeDtypeStruct(out, kind)] * pieces...  32.7 us
    pallas_call x2, Pallas kernels, attend(): pl.pallas_call(body, out_shape=(jax.ShapeDtypeStruct((n, QW), BF16), jax....  26.3 us
  transfers between devices with their start and end apart: 59, of which 24 were waited for; matrix products, arithmetic and copies ran while one was open for 2% of the time, Pallas kernels for 60%

profile of v5, /device:TPU:0, one launch (start us, length us, event | category | flops | bytes accessed | tf_op | source)
XLA Modules:
  0.0 681.3 jit_solution(11794132976620887182)
XLA Ops:
  9.7 56.8 %gather_all.1 = (bf16[2,4,480,256]{3,2,1,0:T(8,128)(2,1)}, bf16[2,4,480,256]{3,2,1,0:T(8,128)(2,1)}, bf16[2,4,480,256]{3,2,1,0:T(8,128)(2,1)}, bf16[2,4,480,256]{3,2,1,0:T(8,128)(2,1)}) custom-call(bf16[480,256]{1,0:T(8,128)(2,1)} %pad_maximum_fusion.2.own_ref), custom_call_target="tpu_custom_call" | custom-call | flops 1 | bytes 1 | tf_op jit(solution)/shard_map/gather_all/pallas_call | solution.py:199
  73.4 19.5 %project.1 = (bf16[512,2048]{1,0:T(8,128)(2,1)}, f32[4,512,480]{2,1,0:T(8,128)}, bf16[512,1280]{1,0:T(8,128)(2,1)}, bf16[512,640]{1,0:T(8,128)(2,1)}) custom-call(s32[5]{0:T(128)} %pad_add_fusion.info_ref, bf16[512,2048]{1,0:T(8,128)(2,1)} %bitcast.51, f32[1,2048]{1,0:T(1,128)} %bitcast.76, f32[1,128]{1,0:T(1,128)} %broadcast_in_dim_tile.6.qgain_ref, ...), custom_call_target="tpu_custom_call" | custom-call | flops 1 | bytes 1 | tf_op jit(solution)/shard_map/project/pallas_call | solution.py:401
  95.0 6.0 collective-permute-done.refs_2_.refs_8_
  103.0 11.4 %collective-permute-done.3.refs_2_ = bf16[512,640]{1,0:T(8,128)(2,1)S(1)} collective-permute-done((bf16[512,640]{1,0:T(8,128)(2,1)}, bf16[512,640]{1,0:T(8,128)(2,1)S(1)}, u32[]{:S(2)}, u32[]{:S(2)}) %collective-permute-start.3) | collective-permute-done | bytes 655392 | tf_op jit(solution)/shard_map/ppermute | solution.py:52
  120.5 13.0 %attend.2 = (bf16[256,1280]{1,0:T(8,128)(2,1)}, bf16[1280,256]{1,0:T(8,128)(2,1)}, f32[5,4,256]{2,1,0:T(4,128)}) custom-call(s32[5]{0:T(128)} %pad_add_fusion.info_ref, bf16[512,1280]{1,0:T(8,128)(2,1)} %get-tuple-element.152.q_ref, bf16[512,640]{1,0:T(8,128)(2,1)} %get-tuple-element.148.refs_0_, bf16[512,640]{1,0:T(8,128)(2,1)} %copy-done.7, ...), custom_call_target="tpu_custom_call" | custom-call | flops 1 | bytes 1 | tf_op jit(solution)/shard_map/attend/pallas_call | solution.py:641
  133.5 9.0 %out_project.2 = (f32[256,2048]{1,0:T(8,128)}, bf16[256,2048]{1,0:T(8,128)(2,1)}) custom-call(s32[5]{0:T(128)} %pad_add_fusion.info_ref, bf16[256,1280]{1,0:T(8,128)(2,1)} %get-tuple-element.149.mixed_ref, bf16[512,2048]{1,0:T(8,128)(2,1)} %bitcast.52, f32[1,2048]{1,0:T(1,128)} %bitcast.71, bf16[8,320,256]{2,1,0:T(8,128)(2,1)} %bitcast.58, ...), custom_call_target="tpu_custom_call" | custom-call | flops 1 | bytes 1 | tf_op jit(solution)/shard_map/out_project/pallas_call | solution.py:759
  143.8 13.3 %attend.3 = (bf16[256,1280]{1,0:T(8,128)(2,1)}, bf16[1280,256]{1,0:T(8,128)(2,1)}, f32[5,4,256]{2,1,0:T(4,128)}) custom-call(s32[5]{0:T(128)} %pad_add_fusion.info_ref, bf16[512,1280]{1,0:T(8,128)(2,1)} %get-tuple-element.152.q_ref, bf16[512,640]{1,0:T(8,128)(2,1)} %get-tuple-element.148.refs_0_, bf16[512,640]{1,0:T(8,128)(2,1)} %copy-done.7, ...), custom_call_target="tpu_custom_call" | custom-call | flops 1 | bytes 1 | tf_op jit(solution)/shard_map/attend/pallas_call | solution.py:641
  157.1 6.0 collective-permute-done.8.refs_10_.refs_4_
  163.1 21.0 %collective-permute-done.6.refs_4_.refs_0_ = bf16[256,2048]{1,0:T(8,128)(2,1)S(1)} collective-permute-done((bf16[256,2048]{1,0:T(8,128)(2,1)}, bf16[256,2048]{1,0:T(8,128)(2,1)S(1)}, u32[]{:S(2)}, u32[]{:S(2)}) %collective-permute-start.6) | collective-permute-done | bytes 1048608 | tf_op jit(solution)/shard_map/ppermute | solution.py:52
  184.1 9.0 %out_project.3 = (f32[256,2048]{1,0:T(8,128)}, bf16[256,2048]{1,0:T(8,128)(2,1)}) custom-call(s32[5]{0:T(128)} %pad_add_fusion.info_ref, bf16[256,1280]{1,0:T(8,128)(2,1)} %get-tuple-element.156.mixed_ref, bf16[512,2048]{1,0:T(8,128)(2,1)} %bitcast.53, f32[1,2048]{1,0:T(1,128)} %bitcast.72, bf16[8,320,256]{2,1,0:T(8,128)(2,1)} %bitcast.59, ...), custom_call_target="tpu_custom_call" | custom-call | flops 1 | bytes 1 | tf_op jit(solution)/shard_map/out_project/pallas_call | solution.py:759
  196.1 23.0 %collective-permute-done.11.refs_5_.refs_1_ = bf16[256,2048]{1,0:T(8,128)(2,1)} collective-permute-done((bf16[256,2048]{1,0:T(8,128)(2,1)}, bf16[256,2048]{1,0:T(8,128)(2,1)}, u32[]{:S(2)}, u32[]{:S(2)}) %collective-permute-start.11) | collective-permute-done | bytes 1048608 | tf_op jit(solution)/shard_map/ppermute | solution.py:52
  221.0 5.8 collective-permute-done.12.refs_6_.refs_2_
  227.4 58.6 %feed_forward.3 = (f32[512,2048]{1,0:T(8,128)}, f32[512,2048]{1,0:T(8,128)}, f32[512,2048]{1,0:T(8,128)}, f32[512,2048]{1,0:T(8,128)}, f32[512,2048]{1,0:T(8,128...) custom-call(s32[5]{0:T(128)} %pad_add_fusion.info_ref, ...), custom_call_target="tpu_custom_call" | custom-call | flops 1 | bytes 1 | tf_op jit(solution)/shard_map/feed_forward/pallas_call | solution.py:1005
  286.1 17.5 %weight_grads.6 = bf16[4,3,768,256]{3,2,1,0:T(8,128)(2,1)} custom-call(s32[4]{0:T(128)} %fusion.4.order_ref, bf16[256,2048]{1,0:T(8,128)(2,1)} %get-tuple-element.154.refs_0_, bf16[256,2048]{1,0:T(8,128)(2,1)} %get-tuple-element.159.refs_1_, bf16[256,2048]{1,0:T(8,128)(2,1)} %collective-permute-done.7.refs_2_, bf16[256,2048]{1,0:T(8,128)(2,1)} %copy-done.3, ...), custom_call_target="tpu_custom_call" | custom-call | flops 1 | bytes 1 | tf_op jit(solution)/shard_map/weight_grads/pallas_call | solution.py:1068
  303.8 37.3 %feed_forward.4 = (bf16[512,2048]{1,0:T(8,128)(2,1)}, bf16[512,2048]{1,0:T(8,128)(2,1)}, bf16[512,2048]{1,0:T(8,128)(2,1)}, bf16[512,2048]{1,0:T(8,128)(2,1)}, b...) custom-call(s32[5]{0:T(128)} %pad_add_fusion.info_ref, ...), custom_call_target="tpu_custom_call" | custom-call | flops 1 | bytes 1 | tf_op jit(solution)/shard_map/feed_forward/pallas_call | solution.py:1005
  352.3 24.7 %feed_forward.5 = (bf16[512,2048]{1,0:T(8,128)(2,1)}, bf16[512,2048]{1,0:T(8,128)(2,1)}, bf16[512,2048]{1,0:T(8,128)(2,1)}, bf16[512,2048]{1,0:T(8,128)(2,1)}, b...) custom-call(s32[5]{0:T(128)} %pad_add_fusion.info_ref, ...), custom_call_target="tpu_custom_call", output_to_operand_aliasing={{4}: (12, {}), {5}: (13, {}), {6}: (14, {})} | custom-call | flops 1 | bytes 1 | tf_op jit(solution)/shard_map/feed_forward/pallas_call | solution.py:1005
  377.0 13.3 %weight_grads.7 = bf16[4,3,512,256]{3,2,1,0:T(8,128)(2,1)} custom-call(s32[4]{0:T(128)} %fusion.4.order_ref, bf16[256,2048]{1,0:T(8,128)(2,1)} %get-tuple-element.154.refs_0_, bf16[256,2048]{1,0:T(8,128)(2,1)} %get-tuple-element.159.refs_1_, bf16[256,2048]{1,0:T(8,128)(2,1)} %collective-permute-done.7.refs_2_, bf16[256,2048]{1,0:T(8,128)(2,1)} %copy-done.3, ...), custom_call_target="tpu_custom_call" | custom-call | flops 1 | bytes 1 | tf_op jit(solution)/shard_map/weight_grads/pallas_call | solution.py:1068
  390.3 7.8 %collective-permute-done.18.refs_1_ = bf16[512,2048]{1,0:T(8,128)(2,1)S(1)} collective-permute-done((bf16[512,2048]{1,0:T(8,128)(2,1)}, bf16[512,2048]{1,0:T(8,128)(2,1)S(1)}, u32[]{:S(2)}, u32[]{:S(2)}) %collective-permute-start.18) | collective-permute-done | bytes 2097184 | tf_op jit(solution)/shard_map/ppermute | solution.py:52
  406.1 14.9 %middle_back.1 = (f32[512,2048]{1,0:T(8,128)}, bf16[512,2048]{1,0:T(8,128)(2,1)}, bf16[512,1280]{1,0:T(8,128)(2,1)}, f32[1,2048]{1,0:T(1,128)}) custom-call(s32[5]{0:T(128)} %pad_add_fusion.info_ref, bf16[512,2048]{1,0:T(8,128)(2,1)} %combine.13.refs_0_, bf16[512,2048]{1,0:T(8,128)(2,1)} %copy-done.10, f32[256,2048]{1,0:T(8,128)} %get-tuple-element.151.refs_2_.refs_0_, ...), custom_call_target="tpu_custom_call" | custom-call | flops 1 | bytes 1 | tf_op jit(solution)/shard_map/middle_back/pallas_call | solution.py:824
  421.0 9.2 %out_weight_grads.1 = (bf16[8,320,256]{2,1,0:T(8,128)(2,1)}, bf16[8,320,256]{2,1,0:T(8,128)(2,1)}, bf16[8,320,256]{2,1,0:T(8,128)(2,1)}, bf16[8,320,256]{2,1,0:T(8,128)(2,1)}) custom-call(s32[9]{0:T(128)} %pad_add_fusion.1.order_ref, bf16[512,2048]{1,0:T(8,128)(2,1)} %get-tuple-element.201.left_ref, bf16[1280,256]{1,0:T(8,128)(2,1)} %get-tuple-element.202.refs_0_, ...), custom_call_target="tpu_custom_call" | custom-call | flops 1 | bytes 1 | tf_op jit(solution)/shard_map/out_weight_grads/pallas_call | solution.py:1098
  437.6 21.9 %attend_back.2 = (f32[256,1280]{1,0:T(8,128)}, bf16[256,640]{1,0:T(8,128)(2,1)}, bf16[256,640]{1,0:T(8,128)(2,1)}, bf16[256,640]{1,0:T(8,128)(2,1)}, bf16[256,640]{1,0:T(8,128)(2,1)}) custom-call(s32[5]{0:T(128)} %pad_add_fusion.info_ref, bf16[512,1280]{1,0:T(8,128)(2,1)} %get-tuple-element.152.q_ref, bf16[512,1280]{1,0:T(8,128)(2,1)} %get-tuple-element.192.do_ref, ...), custom_call_target="tpu_custom_call" | custom-call | flops 1 | bytes 1 | tf_op jit(solution)/shard_map/attend_back/pallas_call | solution.py:712
  459.5 17.9 %weight_grads.8 = bf16[4,3,768,256]{3,2,1,0:T(8,128)(2,1)} custom-call(s32[4]{0:T(128)} %copy-done.32, bf16[256,2048]{1,0:T(8,128)(2,1)} %get-tuple-element.154.refs_0_, bf16[256,2048]{1,0:T(8,128)(2,1)} %get-tuple-element.159.refs_1_, bf16[256,2048]{1,0:T(8,128)(2,1)} %collective-permute-done.7.refs_2_, bf16[256,2048]{1,0:T(8,128)(2,1)} %copy-done.3, ...), custom_call_target="tpu_custom_call" | custom-call | flops 1 | bytes 1 | tf_op jit(solution)/shard_map/weight_grads/pallas_call | solution.py:1068
  492.0 21.8 %attend_back.3 = (f32[256,1280]{1,0:T(8,128)}, bf16[256,640]{1,0:T(8,128)(2,1)}, bf16[256,640]{1,0:T(8,128)(2,1)}, bf16[256,640]{1,0:T(8,128)(2,1)}, bf16[256,640]{1,0:T(8,128)(2,1)}) custom-call(s32[5]{0:T(128)} %pad_add_fusion.info_ref, bf16[512,1280]{1,0:T(8,128)(2,1)} %get-tuple-element.152.q_ref, bf16[512,1280]{1,0:T(8,128)(2,1)} %get-tuple-element.192.do_ref, ...), custom_call_target="tpu_custom_call" | custom-call | flops 1 | bytes 1 | tf_op jit(solution)/shard_map/attend_back/pallas_call | solution.py:712
  528.5 11.6 %heads_back.2 = (bf16[4,256,480]{2,1,0:T(8,128)(2,1)}, f32[1,128]{1,0:T(1,128)}, f32[1,128]{1,0:T(1,128)}, bf16[480,256]{1,0:T(8,128)(2,1)}, bf16[480,256]{1,0:T...) custom-call(s32[5]{0:T(128)} %pad_add_fusion.info_ref, f32[256,1280]{1,0:T(8,128)} %get-tuple-element.209.dq_ref, ...), custom_call_target="tpu_custom_call" | custom-call | flops 1 | bytes 1 | tf_op jit(solution)/shard_map/heads_back/pallas_call | solution.py:503
  540.8 11.8 %heads_back.3 = (bf16[4,256,480]{2,1,0:T(8,128)(2,1)}, f32[1,128]{1,0:T(1,128)}, f32[1,128]{1,0:T(1,128)}, bf16[480,256]{1,0:T(8,128)(2,1)}, bf16[480,256]{1,0:T...) custom-call(s32[5]{0:T(128)} %pad_add_fusion.info_ref, f32[256,1280]{1,0:T(8,128)} %get-tuple-element.214.dq_ref, ...), custom_call_target="tpu_custom_call" | custom-call | flops 1 | bytes 1 | tf_op jit(solution)/shard_map/heads_back/pallas_call | solution.py:503
  552.7 13.5 %weight_grads.9 = bf16[4,3,512,256]{3,2,1,0:T(8,128)(2,1)} custom-call(s32[4]{0:T(128)} %copy-done.32, bf16[256,2048]{1,0:T(8,128)(2,1)} %get-tuple-element.154.refs_0_, bf16[256,2048]{1,0:T(8,128)(2,1)} %get-tuple-element.159.refs_1_, bf16[256,2048]{1,0:T(8,128)(2,1)} %collective-permute-done.7.refs_2_, bf16[256,2048]{1,0:T(8,128)(2,1)} %copy-done.3, ...), custom_call_target="tpu_custom_call" | custom-call | flops 1 | bytes 1 | tf_op jit(solution)/shard_map/weight_grads/pallas_call | solution.py:1068
  582.1 13.8 %project_back.1 = (bf16[512,2048]{1,0:T(8,128)(2,1)}, f32[1,2048]{1,0:T(1,128)}) custom-call(s32[5]{0:T(128)} %pad_add_fusion.info_ref, bf16[512,2048]{1,0:T(8,128)(2,1)} %bitcast.54, f32[512,2048]{1,0:T(8,128)} %get-tuple-element.231.mid_ref, f32[1,2048]{1,0:T(1,128)} %bitcast.77, bf16[4,256,480]{2,1,0:T(8,128)(2,1)} %get-tuple-element.223.refs_0_, ...), custom_call_target="tpu_custom_call" | custom-call | flops 1 | bytes 1 | tf_op jit(solution)/shard_map/project_back/pallas_call | solution.py:572
  601.3 7.0 %weight_grads.10 = bf16[4,1,480,256]{3,2,1,0:T(8,128)(2,1)} custom-call(s32[4]{0:T(128)} %get-tuple-element.233.order_ref, bf16[512,2048]{1,0:T(8,128)(2,1)} %get-tuple-element.165.refs_0_, bf16[512,2048]{1,0:T(8,128)(2,1)} %collective-permute-done.16.refs_1_, bf16[512,2048]{1,0:T(8,128)(2,1)} %collective-permute-done.15.refs_2_, ...), custom_call_target="tpu_custom_call" | custom-call | flops 1 | bytes 1 | tf_op jit(solution)/shard_map/weight_grads/pallas_call | solution.py:1068
  625.2 9.9 %collective-permute-done.46.refs_12_ = bf16[4,1,480,256]{3,2,1,0:T(8,128)(2,1)S(1)} collective-permute-done((bf16[4,1,480,256]{3,2,1,0:T(8,128)(2,1)}, bf16[4,1,480,256]{3,2,1,0:T(8,128)(2,1)S(1)}, u32[]{:S(2)}, u32[]{:S(2)}) %collective-permute-start.46) | collective-permute-done | bytes 983072 | tf_op jit(solution)/shard_map/ppermute | solution.py:52
  636.1 7.4 %weight_grads.11 = (bf16[1,480,256]{2,1,0:T(8,128)(2,1)}, bf16[1,480,256]{2,1,0:T(8,128)(2,1)}, bf16[1,480,256]{2,1,0:T(8,128)(2,1)}, bf16[1,480,256]{2,1,0:T(8,128)(2,1)}) custom-call(s32[4]{0:T(128)} %get-tuple-element.249.order_ref, bf16[512,2048]{1,0:T(8,128)(2,1)} %get-tuple-element.165.refs_0_, bf16[512,2048]{1,0:T(8,128)(2,1)} %collective-permute-done.16.refs_1_, ...), custom_call_target="tpu_custom_call" | custom-call | flops 1 | bytes 1 | tf_op jit(solution)/shard_map/weight_grads/pallas_call | solution.py:1068
  659.0 6.6 finish_rows.1
  665.6 7.2 %collective-permute-done.49 = bf16[1,480,256]{2,1,0:T(8,128)(2,1)S(1)} collective-permute-done((bf16[1,480,256]{2,1,0:T(8,128)(2,1)}, bf16[1,480,256]{2,1,0:T(8,128)(2,1)S(1)}, u32[]{:S(2)}, u32[]{:S(2)}) %collective-permute-start.49) | collective-permute-done | bytes 245792 | tf_op jit(solution)/shard_map/ppermute | solution.py:52
  (267 shorter events, 138.7 us)
Async XLA Ops:
  7.2 61.8 %all-gather.9.cloned.1.call-start = ((), (), s32[]{:S(2)}) async-start(), calls=%async_computation.8 | async-start | bytes 1474560 | tf_op jit(solution)/shard_map/all_gather | solution.py:1170
  8.0 219.5 %all-gather.5.cloned.1.call-start = ((), (), s32[]{:S(2)}) async-start(), calls=%async_computation.3 | async-start | bytes 10616832 | tf_op jit(solution)/shard_map/all_gather | solution.py:1170
  67.6 236.2 %all-gather.7.cloned.1.call-start = ((), (), s32[]{:S(2)}) async-start(), calls=%async_computation.4 | async-start | bytes 7077888 | tf_op jit(solution)/shard_map/all_gather | solution.py:1170
  68.9 513.1 %reduce-scatter.4.cloned.1.call-start = ((), (), s32[]{:S(2)}) async-start(), calls=%async_computation.5 | async-start | bytes 5898240 | tf_op jit(solution)/shard_map/reduce_scatter | solution.py:1237
  69.0 32.0 %collective-permute-start = (bf16[8,320,256]{2,1,0:T(8,128)(2,1)}, bf16[8,320,256]{2,1,0:T(8,128)(2,1)}, u32[]{:S(2)}, u32[]{:S(2)}) collective-permute-start(bf16[8,320,256]{2,1,0:T(8,128)(2,1)} %bitcast.57), channel_id=1, source_target_pairs={{0,2},{1,3},{2,0},{3,1},{4,6},{5,7},{6,4},{7,5},{8,10},{9,11},{10,... | collective-permute-start | bytes 3932168 | tf_op jit(solution)/shard_map/ppermute | solution.py:52
  93.0 21.4 %collective-permute-start.3 = (bf16[512,640]{1,0:T(8,128)(2,1)}, bf16[512,640]{1,0:T(8,128)(2,1)S(1)}, u32[]{:S(2)}, u32[]{:S(2)}) collective-permute-start(bf16[512,640]{1,0:T(8,128)(2,1)} %get-tuple-element.148.refs_0_), channel_id=1, source_target_pairs={{0,2},{1,3},{2,0},{3,1},{4,6},{5,7},{6,4},{7,5},{8,10},{9,11},{10,... | collective-permute-start | bytes 1966088 | tf_op jit(solution)/shard_map/ppermute | solution.py:52
  94.4 20.0 %collective-permute-start.2 = (bf16[512,640]{1,0:T(8,128)(2,1)}, bf16[512,640]{1,0:T(8,128)(2,1)S(1)}, u32[]{:S(2)}, u32[]{:S(2)}) collective-permute-start(bf16[512,640]{1,0:T(8,128)(2,1)} %get-tuple-element.148.refs_0_), channel_id=1, source_target_pairs={{0,1},{1,0},{2,3},{3,2},{4,5},{5,4},{6,7},{7,6},{8,9},{9,8},{10,11... | collective-permute-start | bytes 1966088 | tf_op jit(solution)/shard_map/ppermute | solution.py:52
  94.5 21.3 %collective-permute-start.1 = (bf16[8,320,256]{2,1,0:T(8,128)(2,1)S(1)}, bf16[8,320,256]{2,1,0:T(8,128)(2,1)S(1)}, u32[]{:S(2)}, u32[]{:S(2)}) collective-permute-start(bf16[8,320,256]{2,1,0:T(8,128)(2,1)S(1)} %bitcast.61), channel_id=1, source_target_pairs={{0,1},{1,0},{2,3},{3,2},{4,5},{5,4},{6,7},{7,6},{8,9},{9,8},{10,11... | collective-permute-start | bytes 3932168 | tf_op jit(solution)/shard_map/ppermute | solution.py:52
  101.0 32.5 %collective-permute-start.5 = (bf16[8,320,256]{2,1,0:T(8,128)(2,1)}, bf16[8,320,256]{2,1,0:T(8,128)(2,1)}, u32[]{:S(2)}, u32[]{:S(2)}) collective-permute-start(bf16[8,320,256]{2,1,0:T(8,128)(2,1)} %collective-permute-done.refs_2_.refs_8_), channel_id=1, source_target_pairs={{0,1},{1,0},{2,3},{3,2},{4,5},{5,4},{6,7},{7,6},{8,9},{9,8},{10,11... | collective-permute-start | bytes 3932168 | tf_op jit(solution)/shard_map/ppermute | solution.py:52
  114.4 48.7 %collective-permute-start.8 = (bf16[512,2048]{1,0:T(8,128)(2,1)S(1)}, bf16[512,2048]{1,0:T(8,128)(2,1)}, u32[]{:S(2)}, u32[]{:S(2)}) collective-permute-start(bf16[512,2048]{1,0:T(8,128)(2,1)S(1)} %fusion.refs_8_.refs_4_), channel_id=1, source_target_pairs={{0,2},{1,3},{2,0},{3,1},{4,6},{5,7},{6,4},{7,5},{8,10},{9,11},{10,... | collective-permute-start | bytes 6291464 | tf_op jit(solution)/shard_map/ppermute | solution.py:52
  115.3 47.8 %collective-permute-start.9 = (bf16[512,2048]{1,0:T(8,128)(2,1)S(1)}, bf16[512,2048]{1,0:T(8,128)(2,1)}, u32[]{:S(2)}, u32[]{:S(2)}) collective-permute-start(bf16[512,2048]{1,0:T(8,128)(2,1)S(1)} %fusion.refs_8_.refs_4_), channel_id=1, source_target_pairs={{0,1},{1,0},{2,3},{3,2},{4,5},{5,4},{6,7},{7,6},{8,9},{9,8},{10,11... | collective-permute-start | bytes 6291464 | tf_op jit(solution)/shard_map/ppermute | solution.py:52
  142.5 41.6 %collective-permute-start.6 = (bf16[256,2048]{1,0:T(8,128)(2,1)}, bf16[256,2048]{1,0:T(8,128)(2,1)S(1)}, u32[]{:S(2)}, u32[]{:S(2)}) collective-permute-start(bf16[256,2048]{1,0:T(8,128)(2,1)} %get-tuple-element.154.refs_0_), channel_id=1, source_target_pairs={{0,2},{1,3},{2,0},{3,1},{4,6},{5,7},{6,4},{7,5},{8,10},{9,11},{10,... | collective-permute-start | bytes 3145736 | tf_op jit(solution)/shard_map/ppermute | solution.py:52
  143.8 40.3 %collective-permute-start.7 = (bf16[256,2048]{1,0:T(8,128)(2,1)}, bf16[256,2048]{1,0:T(8,128)(2,1)}, u32[]{:S(2)}, u32[]{:S(2)}) collective-permute-start(bf16[256,2048]{1,0:T(8,128)(2,1)} %get-tuple-element.154.refs_0_), channel_id=1, source_target_pairs={{0,1},{1,0},{2,3},{3,2},{4,5},{5,4},{6,7},{7,6},{8,9},{9,8},{10,11... | collective-permute-start | bytes 3145736 | tf_op jit(solution)/shard_map/ppermute | solution.py:52
  193.2 25.9 %collective-permute-start.11 = (bf16[256,2048]{1,0:T(8,128)(2,1)}, bf16[256,2048]{1,0:T(8,128)(2,1)}, u32[]{:S(2)}, u32[]{:S(2)}) collective-permute-start(bf16[256,2048]{1,0:T(8,128)(2,1)} %get-tuple-element.159.refs_1_), channel_id=1, source_target_pairs={{0,2},{1,3},{2,0},{3,1},{4,6},{5,7},{6,4},{7,5},{8,10},{9,11},{10,... | collective-permute-start | bytes 3145736 | tf_op jit(solution)/shard_map/ppermute | solution.py:52
  194.1 26.9 %collective-permute-start.14 = (bf16[512,2048]{1,0:T(8,128)(2,1)}, bf16[512,2048]{1,0:T(8,128)(2,1)S(1)}, u32[]{:S(2)}, u32[]{:S(2)}) collective-permute-start(bf16[512,2048]{1,0:T(8,128)(2,1)} %collective-permute-done.8.refs_10_.refs_4_), channel_id=1, source_target_pairs={{0,1},{1,0},{2,3},{3,2},{4,5},{5,4},{6,7},{7,6},{8,9},{9,8},{10,11... | collective-permute-start | bytes 6291464 | tf_op jit(solution)/shard_map/ppermute | solution.py:52
  219.1 84.5 %collective-permute-start.15 = (bf16[512,2048]{1,0:T(8,128)(2,1)}, bf16[512,2048]{1,0:T(8,128)(2,1)}, u32[]{:S(2)}, u32[]{:S(2)}) collective-permute-start(bf16[512,2048]{1,0:T(8,128)(2,1)} %get-tuple-element.165.refs_0_), channel_id=1, source_target_pairs={{0,2},{1,3},{2,0},{3,1},{4,6},{5,7},{6,4},{7,5},{8,10},{9,11},{10,... | collective-permute-start | bytes 6291464 | tf_op jit(solution)/shard_map/ppermute | solution.py:52
  219.9 83.7 %collective-permute-start.16 = (bf16[512,2048]{1,0:T(8,128)(2,1)}, bf16[512,2048]{1,0:T(8,128)(2,1)}, u32[]{:S(2)}, u32[]{:S(2)}) collective-permute-start(bf16[512,2048]{1,0:T(8,128)(2,1)} %get-tuple-element.165.refs_0_), channel_id=1, source_target_pairs={{0,1},{1,0},{2,3},{3,2},{4,5},{5,4},{6,7},{7,6},{8,9},{9,8},{10,11... | collective-permute-start | bytes 6291464 | tf_op jit(solution)/shard_map/ppermute | solution.py:52
  350.3 47.9 %collective-permute-start.18 = (bf16[512,2048]{1,0:T(8,128)(2,1)}, bf16[512,2048]{1,0:T(8,128)(2,1)S(1)}, u32[]{:S(2)}, u32[]{:S(2)}) collective-permute-start(bf16[512,2048]{1,0:T(8,128)(2,1)} %combine.12), channel_id=1, source_target_pairs={{0,2},{1,3},{2,0},{3,1},{4,6},{5,7},{6,4},{7,5},{8,10},{9,11},{10,... | collective-permute-start | bytes 6291464 | tf_op jit(solution)/shard_map/ppermute | solution.py:52
  351.8 107.8 %collective-permute-start.23 = (bf16[4,3,768,256]{3,2,1,0:T(8,128)(2,1)}, bf16[4,3,768,256]{3,2,1,0:T(8,128)(2,1)}, u32[]{:S(2)}, u32[]{:S(2)}) collective-permute-start(bf16[4,3,768,256]{3,2,1,0:T(8,128)(2,1)} %weight_grads.6), channel_id=1, source_target_pairs={{0,4},{4,0},{1,5},{5,1},{2,6},{6,2},{3,7},{7,3},{8,12},{12,8},{9,1... | collective-permute-start | bytes 14155784 | tf_op jit(solution)/shard_map/ppermute | solution.py:52
  477.4 172.0 %reduce-scatter.8.cloned.1.call-start = ((), (), s32[]{:S(2)}) async-start(), calls=%async_computation.7 | async-start | bytes 3932160 | tf_op jit(solution)/shard_map/reduce_scatter | solution.py:1237
  477.5 75.2 %collective-permute-start.32 = (bf16[4,3,512,256]{3,2,1,0:T(8,128)(2,1)}, bf16[4,3,512,256]{3,2,1,0:T(8,128)(2,1)}, u32[]{:S(2)}, u32[]{:S(2)}) collective-permute-start(bf16[4,3,512,256]{3,2,1,0:T(8,128)(2,1)} %weight_grads.7), channel_id=1, source_target_pairs={{0,4},{4,0},{1,5},{5,1},{2,6},{6,2},{3,7},{7,3},{8,12},{12,8},{9,1... | collective-permute-start | bytes 9437192 | tf_op jit(solution)/shard_map/ppermute | solution.py:52
  478.6 74.0 %collective-permute-start.31 = (bf16[8,320,256]{2,1,0:T(8,128)(2,1)}, bf16[8,320,256]{2,1,0:T(8,128)(2,1)S(1)}, u32[]{:S(2)}, u32[]{:S(2)}) collective-permute-start(bf16[8,320,256]{2,1,0:T(8,128)(2,1)} %combine.16), channel_id=1, source_target_pairs={{0,2},{1,3},{2,0},{3,1},{4,6},{5,7},{6,4},{7,5},{8,10},{9,11},{10,... | collective-permute-start | bytes 3932168 | tf_op jit(solution)/shard_map/ppermute | solution.py:52
  482.6 31.8 %collective-permute-start.25 = (bf16[256,640]{1,0:T(8,128)(2,1)}, bf16[256,640]{1,0:T(8,128)(2,1)S(1)}, u32[]{:S(2)}, u32[]{:S(2)}) collective-permute-start(bf16[256,640]{1,0:T(8,128)(2,1)} %get-tuple-element.216), channel_id=1, source_target_pairs={{0,1},{1,0},{2,3},{3,2},{4,5},{5,4},{6,7},{7,6},{8,9},{9,8},{10,11... | collective-permute-start | bytes 983048 | tf_op jit(solution)/shard_map/ppermute | solution.py:52
  520.3 19.8 %collective-permute-start.30 = (bf16[256,640]{1,0:T(8,128)(2,1)}, bf16[256,640]{1,0:T(8,128)(2,1)S(1)}, u32[]{:S(2)}, u32[]{:S(2)}) collective-permute-start(bf16[256,640]{1,0:T(8,128)(2,1)} %combine.18), channel_id=1, source_target_pairs={{0,2},{1,3},{2,0},{3,1},{4,6},{5,7},{6,4},{7,5},{8,10},{9,11},{10,... | collective-permute-start | bytes 983048 | tf_op jit(solution)/shard_map/ppermute | solution.py:52
  566.3 91.0 %reduce-scatter.6.cloned.1.call-start = ((), (), s32[]{:S(2)}) async-start(), calls=%async_computation.6 | async-start | bytes 819200 | tf_op jit(solution)/shard_map/reduce_scatter | solution.py:1323
  575.1 21.5 %collective-permute-start.35 = (bf16[480,256]{1,0:T(8,128)(2,1)}, bf16[480,256]{1,0:T(8,128)(2,1)S(1)}, u32[]{:S(2)}, u32[]{:S(2)}) collective-permute-start(bf16[480,256]{1,0:T(8,128)(2,1)} %get-tuple-element.238), channel_id=1, source_target_pairs={{0,2},{1,3},{2,0},{3,1},{4,6},{5,7},{6,4},{7,5},{8,10},{9,11},{10,... | collective-permute-start | bytes 737288 | tf_op jit(solution)/shard_map/ppermute | solution.py:52
  576.8 21.4 %collective-permute-start.37 = (bf16[480,256]{1,0:T(8,128)(2,1)}, bf16[480,256]{1,0:T(8,128)(2,1)S(1)}, u32[]{:S(2)}, u32[]{:S(2)}) collective-permute-start(bf16[480,256]{1,0:T(8,128)(2,1)} %get-tuple-element.240), channel_id=1, source_target_pairs={{0,3},{1,2},{2,1},{3,0},{4,7},{5,6},{6,5},{7,4},{8,11},{9,10},{10,... | collective-permute-start | bytes 737288 | tf_op jit(solution)/shard_map/ppermute | solution.py:52
  579.7 18.8 %collective-permute-start.34 = (bf16[480,256]{1,0:T(8,128)(2,1)S(1)}, bf16[480,256]{1,0:T(8,128)(2,1)S(1)}, u32[]{:S(2)}, u32[]{:S(2)}) collective-permute-start(bf16[480,256]{1,0:T(8,128)(2,1)S(1)} %copy-done.37), channel_id=1, source_target_pairs={{0,1},{1,0},{2,3},{3,2},{4,5},{5,4},{6,7},{7,6},{8,9},{9,8},{10,11... | collective-permute-start | bytes 737288 | tf_op jit(solution)/shard_map/ppermute | solution.py:52
  608.3 50.7 %collective-permute-start.42 = (bf16[512,2048]{1,0:T(8,128)(2,1)S(1)}, bf16[512,2048]{1,0:T(8,128)(2,1)}, u32[]{:S(2)}, u32[]{:S(2)}) collective-permute-start(bf16[512,2048]{1,0:T(8,128)(2,1)S(1)} %copy-done.9), channel_id=1, source_target_pairs={{0,2},{1,3},{2,0},{3,1},{4,6},{5,7},{6,4},{7,5},{8,10},{9,11},{10,... | collective-permute-start | bytes 6291464 | tf_op jit(solution)/shard_map/ppermute | solution.py:52
  609.0 26.1 %collective-permute-start.46 = (bf16[4,1,480,256]{3,2,1,0:T(8,128)(2,1)}, bf16[4,1,480,256]{3,2,1,0:T(8,128)(2,1)S(1)}, u32[]{:S(2)}, u32[]{:S(2)}) collective-permute-start(bf16[4,1,480,256]{3,2,1,0:T(8,128)(2,1)} %weight_grads.10), channel_id=1, source_target_pairs={{0,4},{4,0},{1,5},{5,1},{2,6},{6,2},{3,7},{7,3},{8,12},{12,8},{9,1... | collective-permute-start | bytes 2949128 | tf_op jit(solution)/shard_map/ppermute | solution.py:52
  652.2 20.5 %collective-permute-start.49 = (bf16[1,480,256]{2,1,0:T(8,128)(2,1)}, bf16[1,480,256]{2,1,0:T(8,128)(2,1)S(1)}, u32[]{:S(2)}, u32[]{:S(2)}) collective-permute-start(bf16[1,480,256]{2,1,0:T(8,128)(2,1)} %get-tuple-element.254), channel_id=1, source_target_pairs={{0,16},{8,24},{16,0},{24,8},{1,17},{9,25},{17,1},{25,9},{2,18},{10... | collective-permute-start | bytes 737288 | tf_op jit(solution)/shard_map/ppermute | solution.py:52
  653.8 18.9 %collective-permute-start.50 = (bf16[1,480,256]{2,1,0:T(8,128)(2,1)S(1)}, bf16[1,480,256]{2,1,0:T(8,128)(2,1)S(1)}, u32[]{:S(2)}, u32[]{:S(2)}) collective-permute-start(bf16[1,480,256]{2,1,0:T(8,128)(2,1)S(1)} %copy-done.38), channel_id=1, source_target_pairs={{0,24},{8,16},{16,8},{24,0},{1,25},{9,17},{17,9},{25,1},{2,26},{10... | collective-permute-start | bytes 737288 | tf_op jit(solution)/shard_map/ppermute | solution.py:52
  (78 other events, 765.3 us)
Sparse Core Ops, SparseCore 0:
  10.2 54.6 all-gather.8
  67.8 136.5 all-gather.4
  206.6 97.1 all-gather.6
  477.6 83.4 reduce-scatter.3
  566.4 60.7 reduce-scatter.7
  629.3 22.1 reduce-scatter.5

commit v6 on v4

--- a/solution.py
+++ b/solution.py
@@ -1314,7 +1314,7 @@
         input_grad, ga = project_back(
             after(info, *last_out, *ffn_grads[:1]), place, dlins, x, middle_grad, gain_one, qkv_cols, rows, slots
         )
-        halves = combine([w_out_core[0], *[after(g, dlins[0]) for g in w_out_got]], BF16, nn_)
+        halves = combine([w_out_core[0], *[after(g, input_grad) for g in w_out_got]], BF16, nn_)
         halves = [halves[0]] + [
             swap(h, "near", nn_, i) for i, h in enumerate(halves[1:], 1)
         ]

time: 687 us -> 688 us (level)
  transfers between devices with their start and end apart: 59 -> 59, of which waited for: 23 -> 24; matrix products, arithmetic and copies ran while one was open for 2% -> 2% of each run, Pallas kernels for 61% -> 61%
where the time goes in v6:
time: 688 us; the launch traced here: 682 us
  Pallas kernels  474 us (69%)
  waiting for transfers between devices  131 us (19%)
  starting transfers between devices  35.3 us (5%)
  local copies, waits for them, and re-layouts  16.1 us (2%)
  between operations  15 us (2%)
  other arithmetic  10.8 us (2%)
    ppermute x53, waiting for transfers between devices, swap(): return lax.ppermute(value, axis, [(i, i ^ mask) for i in range(size)])  130 us
    pallas_call x3, Pallas kernels, feed_forward(): pl.pallas_call(body, out_shape=(*[jax.ShapeDtypeStruct((tokens, depth), s...  121 us
    pallas_call x6, Pallas kernels, weight_grads(): pl.pallas_call(body, out_shape=shapes, grid_spec=pltpu.PrefetchScalarGrid...  76.5 us
    pallas_call x1, Pallas kernels, gather_all(): pl.pallas_call(body, out_shape=[jax.ShapeDtypeStruct((nn_, nf, columns, b...  56.8 us
    pallas_call x2, Pallas kernels, attend_back(): pl.pallas_call(body, out_shape=(jax.ShapeDtypeStruct((n, QW), F32), *[jax...  43.8 us
    ppermute x53, starting transfers between devices, swap(): return lax.ppermute(value, axis, [(i, i ^ mask) for i in range(size)])  35 us
    pallas_call x12, Pallas kernels, combine(): pl.pallas_call(body, out_shape=[jax.ShapeDtypeStruct(out, kind)] * pieces...  32.8 us
    pallas_call x2, Pallas kernels, attend(): pl.pallas_call(body, out_shape=(jax.ShapeDtypeStruct((n, QW), BF16), jax....  32.3 us
  transfers between devices with their start and end apart: 59, of which 24 were waited for; matrix products, arithmetic and copies ran while one was open for 2% of the time, Pallas kernels for 61%

profile of v6, /device:TPU:0, one launch (start us, length us, event | category | flops | bytes accessed | tf_op | source)
XLA Modules:
  0.0 682.5 jit_solution(4735075453188083280)
XLA Ops:
  9.7 56.8 %gather_all.1 = (bf16[2,4,480,256]{3,2,1,0:T(8,128)(2,1)}, bf16[2,4,480,256]{3,2,1,0:T(8,128)(2,1)}, bf16[2,4,480,256]{3,2,1,0:T(8,128)(2,1)}, bf16[2,4,480,256]{3,2,1,0:T(8,128)(2,1)}) custom-call(bf16[480,256]{1,0:T(8,128)(2,1)} %pad_maximum_fusion.2.own_ref), custom_call_target="tpu_custom_call" | custom-call | flops 1 | bytes 1 | tf_op jit(solution)/shard_map/gather_all/pallas_call | solution.py:199
  73.5 19.5 %project.1 = (bf16[512,2048]{1,0:T(8,128)(2,1)}, f32[4,512,480]{2,1,0:T(8,128)}, bf16[512,1280]{1,0:T(8,128)(2,1)}, bf16[512,640]{1,0:T(8,128)(2,1)}) custom-call(s32[5]{0:T(128)} %pad_add_fusion.info_ref, bf16[512,2048]{1,0:T(8,128)(2,1)} %bitcast.51, f32[1,2048]{1,0:T(1,128)} %bitcast.76, f32[1,128]{1,0:T(1,128)} %broadcast_in_dim_tile.6.qgain_ref, ...), custom_call_target="tpu_custom_call" | custom-call | flops 1 | bytes 1 | tf_op jit(solution)/shard_map/project/pallas_call | solution.py:401
  95.0 6.0 collective-permute-done.refs_2_.refs_8_
  103.0 11.4 %collective-permute-done.3.refs_2_ = bf16[512,640]{1,0:T(8,128)(2,1)S(1)} collective-permute-done((bf16[512,640]{1,0:T(8,128)(2,1)}, bf16[512,640]{1,0:T(8,128)(2,1)S(1)}, u32[]{:S(2)}, u32[]{:S(2)}) %collective-permute-start.3) | collective-permute-done | bytes 655392 | tf_op jit(solution)/shard_map/ppermute | solution.py:52
  120.5 16.0 %attend.2 = (bf16[256,1280]{1,0:T(8,128)(2,1)}, bf16[1280,256]{1,0:T(8,128)(2,1)}, f32[5,4,256]{2,1,0:T(4,128)}) custom-call(s32[5]{0:T(128)} %pad_add_fusion.info_ref, bf16[512,1280]{1,0:T(8,128)(2,1)} %get-tuple-element.152.q_ref, bf16[512,640]{1,0:T(8,128)(2,1)} %get-tuple-element.148.refs_0_, bf16[512,640]{1,0:T(8,128)(2,1)} %copy-done.7, ...), custom_call_target="tpu_custom_call" | custom-call | flops 1 | bytes 1 | tf_op jit(solution)/shard_map/attend/pallas_call | solution.py:641
  136.5 9.0 %out_project.2 = (f32[256,2048]{1,0:T(8,128)}, bf16[256,2048]{1,0:T(8,128)(2,1)}) custom-call(s32[5]{0:T(128)} %pad_add_fusion.info_ref, bf16[256,1280]{1,0:T(8,128)(2,1)} %get-tuple-element.149.mixed_ref, bf16[512,2048]{1,0:T(8,128)(2,1)} %bitcast.52, f32[1,2048]{1,0:T(1,128)} %bitcast.71, bf16[8,320,256]{2,1,0:T(8,128)(2,1)} %bitcast.58, ...), custom_call_target="tpu_custom_call" | custom-call | flops 1 | bytes 1 | tf_op jit(solution)/shard_map/out_project/pallas_call | solution.py:759
  145.8 16.3 %attend.3 = (bf16[256,1280]{1,0:T(8,128)(2,1)}, bf16[1280,256]{1,0:T(8,128)(2,1)}, f32[5,4,256]{2,1,0:T(4,128)}) custom-call(s32[5]{0:T(128)} %pad_add_fusion.info_ref, bf16[512,1280]{1,0:T(8,128)(2,1)} %get-tuple-element.152.q_ref, bf16[512,640]{1,0:T(8,128)(2,1)} %get-tuple-element.148.refs_0_, bf16[512,640]{1,0:T(8,128)(2,1)} %copy-done.7, ...), custom_call_target="tpu_custom_call" | custom-call | flops 1 | bytes 1 | tf_op jit(solution)/shard_map/attend/pallas_call | solution.py:641
  163.1 21.0 %collective-permute-done.6.refs_4_.refs_0_ = bf16[256,2048]{1,0:T(8,128)(2,1)S(1)} collective-permute-done((bf16[256,2048]{1,0:T(8,128)(2,1)}, bf16[256,2048]{1,0:T(8,128)(2,1)S(1)}, u32[]{:S(2)}, u32[]{:S(2)}) %collective-permute-start.6) | collective-permute-done | bytes 1048608 | tf_op jit(solution)/shard_map/ppermute | solution.py:52
  184.1 9.0 %out_project.3 = (f32[256,2048]{1,0:T(8,128)}, bf16[256,2048]{1,0:T(8,128)(2,1)}) custom-call(s32[5]{0:T(128)} %pad_add_fusion.info_ref, bf16[256,1280]{1,0:T(8,128)(2,1)} %get-tuple-element.156.mixed_ref, bf16[512,2048]{1,0:T(8,128)(2,1)} %bitcast.53, f32[1,2048]{1,0:T(1,128)} %bitcast.72, bf16[8,320,256]{2,1,0:T(8,128)(2,1)} %bitcast.59, ...), custom_call_target="tpu_custom_call" | custom-call | flops 1 | bytes 1 | tf_op jit(solution)/shard_map/out_project/pallas_call | solution.py:759
  196.1 23.0 %collective-permute-done.11.refs_5_.refs_1_ = bf16[256,2048]{1,0:T(8,128)(2,1)} collective-permute-done((bf16[256,2048]{1,0:T(8,128)(2,1)}, bf16[256,2048]{1,0:T(8,128)(2,1)}, u32[]{:S(2)}, u32[]{:S(2)}) %collective-permute-start.11) | collective-permute-done | bytes 1048608 | tf_op jit(solution)/shard_map/ppermute | solution.py:52
  221.0 5.8 collective-permute-done.12.refs_6_.refs_2_
  227.4 58.6 %feed_forward.3 = (f32[512,2048]{1,0:T(8,128)}, f32[512,2048]{1,0:T(8,128)}, f32[512,2048]{1,0:T(8,128)}, f32[512,2048]{1,0:T(8,128)}, f32[512,2048]{1,0:T(8,128...) custom-call(s32[5]{0:T(128)} %pad_add_fusion.info_ref, ...), custom_call_target="tpu_custom_call" | custom-call | flops 1 | bytes 1 | tf_op jit(solution)/shard_map/feed_forward/pallas_call | solution.py:1005
  286.1 17.5 %weight_grads.6 = bf16[4,3,768,256]{3,2,1,0:T(8,128)(2,1)} custom-call(s32[4]{0:T(128)} %fusion.4.order_ref, bf16[256,2048]{1,0:T(8,128)(2,1)} %get-tuple-element.154.refs_0_, bf16[256,2048]{1,0:T(8,128)(2,1)} %get-tuple-element.159.refs_1_, bf16[256,2048]{1,0:T(8,128)(2,1)} %collective-permute-done.7.refs_2_, bf16[256,2048]{1,0:T(8,128)(2,1)} %copy-done.3, ...), custom_call_target="tpu_custom_call" | custom-call | flops 1 | bytes 1 | tf_op jit(solution)/shard_map/weight_grads/pallas_call | solution.py:1068
  303.8 37.3 %feed_forward.4 = (bf16[512,2048]{1,0:T(8,128)(2,1)}, bf16[512,2048]{1,0:T(8,128)(2,1)}, bf16[512,2048]{1,0:T(8,128)(2,1)}, bf16[512,2048]{1,0:T(8,128)(2,1)}, b...) custom-call(s32[5]{0:T(128)} %pad_add_fusion.info_ref, ...), custom_call_target="tpu_custom_call" | custom-call | flops 1 | bytes 1 | tf_op jit(solution)/shard_map/feed_forward/pallas_call | solution.py:1005
  352.3 24.7 %feed_forward.5 = (bf16[512,2048]{1,0:T(8,128)(2,1)}, bf16[512,2048]{1,0:T(8,128)(2,1)}, bf16[512,2048]{1,0:T(8,128)(2,1)}, bf16[512,2048]{1,0:T(8,128)(2,1)}, b...) custom-call(s32[5]{0:T(128)} %pad_add_fusion.info_ref, ...), custom_call_target="tpu_custom_call", output_to_operand_aliasing={{4}: (12, {}), {5}: (13, {}), {6}: (14, {})} | custom-call | flops 1 | bytes 1 | tf_op jit(solution)/shard_map/feed_forward/pallas_call | solution.py:1005
  377.0 13.3 %weight_grads.7 = bf16[4,3,512,256]{3,2,1,0:T(8,128)(2,1)} custom-call(s32[4]{0:T(128)} %fusion.4.order_ref, bf16[256,2048]{1,0:T(8,128)(2,1)} %get-tuple-element.154.refs_0_, bf16[256,2048]{1,0:T(8,128)(2,1)} %get-tuple-element.159.refs_1_, bf16[256,2048]{1,0:T(8,128)(2,1)} %collective-permute-done.7.refs_2_, bf16[256,2048]{1,0:T(8,128)(2,1)} %copy-done.3, ...), custom_call_target="tpu_custom_call" | custom-call | flops 1 | bytes 1 | tf_op jit(solution)/shard_map/weight_grads/pallas_call | solution.py:1068
  390.3 7.9 %collective-permute-done.18.refs_1_ = bf16[512,2048]{1,0:T(8,128)(2,1)S(1)} collective-permute-done((bf16[512,2048]{1,0:T(8,128)(2,1)}, bf16[512,2048]{1,0:T(8,128)(2,1)S(1)}, u32[]{:S(2)}, u32[]{:S(2)}) %collective-permute-start.18) | collective-permute-done | bytes 2097184 | tf_op jit(solution)/shard_map/ppermute | solution.py:52
  406.1 14.9 %middle_back.1 = (f32[512,2048]{1,0:T(8,128)}, bf16[512,2048]{1,0:T(8,128)(2,1)}, bf16[512,1280]{1,0:T(8,128)(2,1)}, f32[1,2048]{1,0:T(1,128)}) custom-call(s32[5]{0:T(128)} %pad_add_fusion.info_ref, bf16[512,2048]{1,0:T(8,128)(2,1)} %combine.13.refs_0_, bf16[512,2048]{1,0:T(8,128)(2,1)} %copy-done.10, f32[256,2048]{1,0:T(8,128)} %get-tuple-element.151.refs_2_.refs_0_, ...), custom_call_target="tpu_custom_call" | custom-call | flops 1 | bytes 1 | tf_op jit(solution)/shard_map/middle_back/pallas_call | solution.py:824
  421.0 9.2 %out_weight_grads.1 = (bf16[8,320,256]{2,1,0:T(8,128)(2,1)}, bf16[8,320,256]{2,1,0:T(8,128)(2,1)}, bf16[8,320,256]{2,1,0:T(8,128)(2,1)}, bf16[8,320,256]{2,1,0:T(8,128)(2,1)}) custom-call(s32[9]{0:T(128)} %pad_add_fusion.1.order_ref, bf16[512,2048]{1,0:T(8,128)(2,1)} %get-tuple-element.201.left_ref, bf16[1280,256]{1,0:T(8,128)(2,1)} %get-tuple-element.202.refs_0_, ...), custom_call_target="tpu_custom_call" | custom-call | flops 1 | bytes 1 | tf_op jit(solution)/shard_map/out_weight_grads/pallas_call | solution.py:1098
  437.6 22.0 %attend_back.2 = (f32[256,1280]{1,0:T(8,128)}, bf16[256,640]{1,0:T(8,128)(2,1)}, bf16[256,640]{1,0:T(8,128)(2,1)}, bf16[256,640]{1,0:T(8,128)(2,1)}, bf16[256,640]{1,0:T(8,128)(2,1)}) custom-call(s32[5]{0:T(128)} %pad_add_fusion.info_ref, bf16[512,1280]{1,0:T(8,128)(2,1)} %get-tuple-element.152.q_ref, bf16[512,1280]{1,0:T(8,128)(2,1)} %get-tuple-element.192.do_ref, ...), custom_call_target="tpu_custom_call" | custom-call | flops 1 | bytes 1 | tf_op jit(solution)/shard_map/attend_back/pallas_call | solution.py:712
  459.6 17.9 %weight_grads.8 = bf16[4,3,768,256]{3,2,1,0:T(8,128)(2,1)} custom-call(s32[4]{0:T(128)} %copy-done.32, bf16[256,2048]{1,0:T(8,128)(2,1)} %get-tuple-element.154.refs_0_, bf16[256,2048]{1,0:T(8,128)(2,1)} %get-tuple-element.159.refs_1_, bf16[256,2048]{1,0:T(8,128)(2,1)} %collective-permute-done.7.refs_2_, bf16[256,2048]{1,0:T(8,128)(2,1)} %copy-done.3, ...), custom_call_target="tpu_custom_call" | custom-call | flops 1 | bytes 1 | tf_op jit(solution)/shard_map/weight_grads/pallas_call | solution.py:1068
  492.0 21.8 %attend_back.3 = (f32[256,1280]{1,0:T(8,128)}, bf16[256,640]{1,0:T(8,128)(2,1)}, bf16[256,640]{1,0:T(8,128)(2,1)}, bf16[256,640]{1,0:T(8,128)(2,1)}, bf16[256,640]{1,0:T(8,128)(2,1)}) custom-call(s32[5]{0:T(128)} %pad_add_fusion.info_ref, bf16[512,1280]{1,0:T(8,128)(2,1)} %get-tuple-element.152.q_ref, bf16[512,1280]{1,0:T(8,128)(2,1)} %get-tuple-element.192.do_ref, ...), custom_call_target="tpu_custom_call" | custom-call | flops 1 | bytes 1 | tf_op jit(solution)/shard_map/attend_back/pallas_call | solution.py:712
  528.5 11.6 %heads_back.2 = (bf16[4,256,480]{2,1,0:T(8,128)(2,1)}, f32[1,128]{1,0:T(1,128)}, f32[1,128]{1,0:T(1,128)}, bf16[480,256]{1,0:T(8,128)(2,1)}, bf16[480,256]{1,0:T...) custom-call(s32[5]{0:T(128)} %pad_add_fusion.info_ref, f32[256,1280]{1,0:T(8,128)} %get-tuple-element.209.dq_ref, ...), custom_call_target="tpu_custom_call" | custom-call | flops 1 | bytes 1 | tf_op jit(solution)/shard_map/heads_back/pallas_call | solution.py:503
  540.8 11.9 %heads_back.3 = (bf16[4,256,480]{2,1,0:T(8,128)(2,1)}, f32[1,128]{1,0:T(1,128)}, f32[1,128]{1,0:T(1,128)}, bf16[480,256]{1,0:T(8,128)(2,1)}, bf16[480,256]{1,0:T...) custom-call(s32[5]{0:T(128)} %pad_add_fusion.info_ref, f32[256,1280]{1,0:T(8,128)} %get-tuple-element.214.dq_ref, ...), custom_call_target="tpu_custom_call" | custom-call | flops 1 | bytes 1 | tf_op jit(solution)/shard_map/heads_back/pallas_call | solution.py:503
  552.7 13.5 %weight_grads.9 = bf16[4,3,512,256]{3,2,1,0:T(8,128)(2,1)} custom-call(s32[4]{0:T(128)} %copy-done.32, bf16[256,2048]{1,0:T(8,128)(2,1)} %get-tuple-element.154.refs_0_, bf16[256,2048]{1,0:T(8,128)(2,1)} %get-tuple-element.159.refs_1_, bf16[256,2048]{1,0:T(8,128)(2,1)} %collective-permute-done.7.refs_2_, bf16[256,2048]{1,0:T(8,128)(2,1)} %copy-done.3, ...), custom_call_target="tpu_custom_call" | custom-call | flops 1 | bytes 1 | tf_op jit(solution)/shard_map/weight_grads/pallas_call | solution.py:1068
  578.9 13.8 %project_back.1 = (bf16[512,2048]{1,0:T(8,128)(2,1)}, f32[1,2048]{1,0:T(1,128)}) custom-call(s32[5]{0:T(128)} %pad_add_fusion.info_ref, bf16[512,2048]{1,0:T(8,128)(2,1)} %bitcast.54, f32[512,2048]{1,0:T(8,128)} %get-tuple-element.231.mid_ref, f32[1,2048]{1,0:T(1,128)} %bitcast.77, bf16[4,256,480]{2,1,0:T(8,128)(2,1)} %get-tuple-element.223.refs_0_, ...), custom_call_target="tpu_custom_call" | custom-call | flops 1 | bytes 1 | tf_op jit(solution)/shard_map/project_back/pallas_call | solution.py:572
  600.5 7.0 %weight_grads.10 = bf16[4,1,480,256]{3,2,1,0:T(8,128)(2,1)} custom-call(s32[4]{0:T(128)} %get-tuple-element.233.order_ref, bf16[512,2048]{1,0:T(8,128)(2,1)} %get-tuple-element.165.refs_0_, bf16[512,2048]{1,0:T(8,128)(2,1)} %collective-permute-done.16.refs_1_, bf16[512,2048]{1,0:T(8,128)(2,1)} %collective-permute-done.15.refs_2_, ...), custom_call_target="tpu_custom_call" | custom-call | flops 1 | bytes 1 | tf_op jit(solution)/shard_map/weight_grads/pallas_call | solution.py:1068
  609.7 6.1 collective-permute-done.52.refs_1_
  626.9 9.5 %collective-permute-done.46.refs_12_ = bf16[4,1,480,256]{3,2,1,0:T(8,128)(2,1)S(1)} collective-permute-done((bf16[4,1,480,256]{3,2,1,0:T(8,128)(2,1)}, bf16[4,1,480,256]{3,2,1,0:T(8,128)(2,1)S(1)}, u32[]{:S(2)}, u32[]{:S(2)}) %collective-permute-start.46) | collective-permute-done | bytes 983072 | tf_op jit(solution)/shard_map/ppermute | solution.py:52
  637.4 7.4 %weight_grads.11 = (bf16[1,480,256]{2,1,0:T(8,128)(2,1)}, bf16[1,480,256]{2,1,0:T(8,128)(2,1)}, bf16[1,480,256]{2,1,0:T(8,128)(2,1)}, bf16[1,480,256]{2,1,0:T(8,128)(2,1)}) custom-call(s32[4]{0:T(128)} %get-tuple-element.249.order_ref, bf16[512,2048]{1,0:T(8,128)(2,1)} %get-tuple-element.165.refs_0_, bf16[512,2048]{1,0:T(8,128)(2,1)} %collective-permute-done.16.refs_1_, ...), custom_call_target="tpu_custom_call" | custom-call | flops 1 | bytes 1 | tf_op jit(solution)/shard_map/weight_grads/pallas_call | solution.py:1068
  660.1 6.6 finish_rows.1
  666.7 7.2 %collective-permute-done.49 = bf16[1,480,256]{2,1,0:T(8,128)(2,1)S(1)} collective-permute-done((bf16[1,480,256]{2,1,0:T(8,128)(2,1)}, bf16[1,480,256]{2,1,0:T(8,128)(2,1)S(1)}, u32[]{:S(2)}, u32[]{:S(2)}) %collective-permute-start.49) | collective-permute-done | bytes 245792 | tf_op jit(solution)/shard_map/ppermute | solution.py:52
  (261 shorter events, 134.2 us)
Async XLA Ops:
  7.2 61.8 %all-gather.9.cloned.1.call-start = ((), (), s32[]{:S(2)}) async-start(), calls=%async_computation.8 | async-start | bytes 1474560 | tf_op jit(solution)/shard_map/all_gather | solution.py:1170
  8.0 219.5 %all-gather.5.cloned.1.call-start = ((), (), s32[]{:S(2)}) async-start(), calls=%async_computation.3 | async-start | bytes 10616832 | tf_op jit(solution)/shard_map/all_gather | solution.py:1170
  67.6 236.2 %all-gather.7.cloned.1.call-start = ((), (), s32[]{:S(2)}) async-start(), calls=%async_computation.4 | async-start | bytes 7077888 | tf_op jit(solution)/shard_map/all_gather | solution.py:1170
  68.9 509.9 %reduce-scatter.4.cloned.1.call-start = ((), (), s32[]{:S(2)}) async-start(), calls=%async_computation.5 | async-start | bytes 5898240 | tf_op jit(solution)/shard_map/reduce_scatter | solution.py:1237
  69.0 32.0 %collective-permute-start = (bf16[8,320,256]{2,1,0:T(8,128)(2,1)}, bf16[8,320,256]{2,1,0:T(8,128)(2,1)}, u32[]{:S(2)}, u32[]{:S(2)}) collective-permute-start(bf16[8,320,256]{2,1,0:T(8,128)(2,1)} %bitcast.57), channel_id=1, source_target_pairs={{0,2},{1,3},{2,0},{3,1},{4,6},{5,7},{6,4},{7,5},{8,10},{9,11},{10,... | collective-permute-start | bytes 3932168 | tf_op jit(solution)/shard_map/ppermute | solution.py:52
  93.0 21.4 %collective-permute-start.3 = (bf16[512,640]{1,0:T(8,128)(2,1)}, bf16[512,640]{1,0:T(8,128)(2,1)S(1)}, u32[]{:S(2)}, u32[]{:S(2)}) collective-permute-start(bf16[512,640]{1,0:T(8,128)(2,1)} %get-tuple-element.148.refs_0_), channel_id=1, source_target_pairs={{0,2},{1,3},{2,0},{3,1},{4,6},{5,7},{6,4},{7,5},{8,10},{9,11},{10,... | collective-permute-start | bytes 1966088 | tf_op jit(solution)/shard_map/ppermute | solution.py:52
  94.4 20.0 %collective-permute-start.2 = (bf16[512,640]{1,0:T(8,128)(2,1)}, bf16[512,640]{1,0:T(8,128)(2,1)S(1)}, u32[]{:S(2)}, u32[]{:S(2)}) collective-permute-start(bf16[512,640]{1,0:T(8,128)(2,1)} %get-tuple-element.148.refs_0_), channel_id=1, source_target_pairs={{0,1},{1,0},{2,3},{3,2},{4,5},{5,4},{6,7},{7,6},{8,9},{9,8},{10,11... | collective-permute-start | bytes 1966088 | tf_op jit(solution)/shard_map/ppermute | solution.py:52
  94.5 21.3 %collective-permute-start.1 = (bf16[8,320,256]{2,1,0:T(8,128)(2,1)S(1)}, bf16[8,320,256]{2,1,0:T(8,128)(2,1)S(1)}, u32[]{:S(2)}, u32[]{:S(2)}) collective-permute-start(bf16[8,320,256]{2,1,0:T(8,128)(2,1)S(1)} %bitcast.61), channel_id=1, source_target_pairs={{0,1},{1,0},{2,3},{3,2},{4,5},{5,4},{6,7},{7,6},{8,9},{9,8},{10,11... | collective-permute-start | bytes 3932168 | tf_op jit(solution)/shard_map/ppermute | solution.py:52
  101.0 35.5 %collective-permute-start.5 = (bf16[8,320,256]{2,1,0:T(8,128)(2,1)}, bf16[8,320,256]{2,1,0:T(8,128)(2,1)}, u32[]{:S(2)}, u32[]{:S(2)}) collective-permute-start(bf16[8,320,256]{2,1,0:T(8,128)(2,1)} %collective-permute-done.refs_2_.refs_8_), channel_id=1, source_target_pairs={{0,1},{1,0},{2,3},{3,2},{4,5},{5,4},{6,7},{7,6},{8,9},{9,8},{10,11... | collective-permute-start | bytes 3932168 | tf_op jit(solution)/shard_map/ppermute | solution.py:52
  114.4 48.7 %collective-permute-start.8 = (bf16[512,2048]{1,0:T(8,128)(2,1)S(1)}, bf16[512,2048]{1,0:T(8,128)(2,1)}, u32[]{:S(2)}, u32[]{:S(2)}) collective-permute-start(bf16[512,2048]{1,0:T(8,128)(2,1)S(1)} %fusion.refs_8_.refs_4_), channel_id=1, source_target_pairs={{0,2},{1,3},{2,0},{3,1},{4,6},{5,7},{6,4},{7,5},{8,10},{9,11},{10,... | collective-permute-start | bytes 6291464 | tf_op jit(solution)/shard_map/ppermute | solution.py:52
  115.3 47.8 %collective-permute-start.9 = (bf16[512,2048]{1,0:T(8,128)(2,1)S(1)}, bf16[512,2048]{1,0:T(8,128)(2,1)}, u32[]{:S(2)}, u32[]{:S(2)}) collective-permute-start(bf16[512,2048]{1,0:T(8,128)(2,1)S(1)} %fusion.refs_8_.refs_4_), channel_id=1, source_target_pairs={{0,1},{1,0},{2,3},{3,2},{4,5},{5,4},{6,7},{7,6},{8,9},{9,8},{10,11... | collective-permute-start | bytes 6291464 | tf_op jit(solution)/shard_map/ppermute | solution.py:52
  145.6 38.6 %collective-permute-start.6 = (bf16[256,2048]{1,0:T(8,128)(2,1)}, bf16[256,2048]{1,0:T(8,128)(2,1)S(1)}, u32[]{:S(2)}, u32[]{:S(2)}) collective-permute-start(bf16[256,2048]{1,0:T(8,128)(2,1)} %get-tuple-element.154.refs_0_), channel_id=1, source_target_pairs={{0,2},{1,3},{2,0},{3,1},{4,6},{5,7},{6,4},{7,5},{8,10},{9,11},{10,... | collective-permute-start | bytes 3145736 | tf_op jit(solution)/shard_map/ppermute | solution.py:52
  145.6 38.5 %collective-permute-start.7 = (bf16[256,2048]{1,0:T(8,128)(2,1)}, bf16[256,2048]{1,0:T(8,128)(2,1)}, u32[]{:S(2)}, u32[]{:S(2)}) collective-permute-start(bf16[256,2048]{1,0:T(8,128)(2,1)} %get-tuple-element.154.refs_0_), channel_id=1, source_target_pairs={{0,1},{1,0},{2,3},{3,2},{4,5},{5,4},{6,7},{7,6},{8,9},{9,8},{10,11... | collective-permute-start | bytes 3145736 | tf_op jit(solution)/shard_map/ppermute | solution.py:52
  193.2 25.9 %collective-permute-start.11 = (bf16[256,2048]{1,0:T(8,128)(2,1)}, bf16[256,2048]{1,0:T(8,128)(2,1)}, u32[]{:S(2)}, u32[]{:S(2)}) collective-permute-start(bf16[256,2048]{1,0:T(8,128)(2,1)} %get-tuple-element.159.refs_1_), channel_id=1, source_target_pairs={{0,2},{1,3},{2,0},{3,1},{4,6},{5,7},{6,4},{7,5},{8,10},{9,11},{10,... | collective-permute-start | bytes 3145736 | tf_op jit(solution)/shard_map/ppermute | solution.py:52
  194.1 26.9 %collective-permute-start.14 = (bf16[512,2048]{1,0:T(8,128)(2,1)}, bf16[512,2048]{1,0:T(8,128)(2,1)S(1)}, u32[]{:S(2)}, u32[]{:S(2)}) collective-permute-start(bf16[512,2048]{1,0:T(8,128)(2,1)} %collective-permute-done.8.refs_10_.refs_4_), channel_id=1, source_target_pairs={{0,1},{1,0},{2,3},{3,2},{4,5},{5,4},{6,7},{7,6},{8,9},{9,8},{10,11... | collective-permute-start | bytes 6291464 | tf_op jit(solution)/shard_map/ppermute | solution.py:52
  219.1 84.5 %collective-permute-start.15 = (bf16[512,2048]{1,0:T(8,128)(2,1)}, bf16[512,2048]{1,0:T(8,128)(2,1)}, u32[]{:S(2)}, u32[]{:S(2)}) collective-permute-start(bf16[512,2048]{1,0:T(8,128)(2,1)} %get-tuple-element.165.refs_0_), channel_id=1, source_target_pairs={{0,2},{1,3},{2,0},{3,1},{4,6},{5,7},{6,4},{7,5},{8,10},{9,11},{10,... | collective-permute-start | bytes 6291464 | tf_op jit(solution)/shard_map/ppermute | solution.py:52
  219.9 83.7 %collective-permute-start.16 = (bf16[512,2048]{1,0:T(8,128)(2,1)}, bf16[512,2048]{1,0:T(8,128)(2,1)}, u32[]{:S(2)}, u32[]{:S(2)}) collective-permute-start(bf16[512,2048]{1,0:T(8,128)(2,1)} %get-tuple-element.165.refs_0_), channel_id=1, source_target_pairs={{0,1},{1,0},{2,3},{3,2},{4,5},{5,4},{6,7},{7,6},{8,9},{9,8},{10,11... | collective-permute-start | bytes 6291464 | tf_op jit(solution)/shard_map/ppermute | solution.py:52
  350.3 47.9 %collective-permute-start.18 = (bf16[512,2048]{1,0:T(8,128)(2,1)}, bf16[512,2048]{1,0:T(8,128)(2,1)S(1)}, u32[]{:S(2)}, u32[]{:S(2)}) collective-permute-start(bf16[512,2048]{1,0:T(8,128)(2,1)} %combine.12), channel_id=1, source_target_pairs={{0,2},{1,3},{2,0},{3,1},{4,6},{5,7},{6,4},{7,5},{8,10},{9,11},{10,... | collective-permute-start | bytes 6291464 | tf_op jit(solution)/shard_map/ppermute | solution.py:52
  351.8 107.8 %collective-permute-start.23 = (bf16[4,3,768,256]{3,2,1,0:T(8,128)(2,1)}, bf16[4,3,768,256]{3,2,1,0:T(8,128)(2,1)}, u32[]{:S(2)}, u32[]{:S(2)}) collective-permute-start(bf16[4,3,768,256]{3,2,1,0:T(8,128)(2,1)} %weight_grads.6), channel_id=1, source_target_pairs={{0,4},{4,0},{1,5},{5,1},{2,6},{6,2},{3,7},{7,3},{8,12},{12,8},{9,1... | collective-permute-start | bytes 14155784 | tf_op jit(solution)/shard_map/ppermute | solution.py:52
  477.5 173.1 %reduce-scatter.8.cloned.1.call-start = ((), (), s32[]{:S(2)}) async-start(), calls=%async_computation.7 | async-start | bytes 3932160 | tf_op jit(solution)/shard_map/reduce_scatter | solution.py:1237
  477.5 75.2 %collective-permute-start.32 = (bf16[4,3,512,256]{3,2,1,0:T(8,128)(2,1)}, bf16[4,3,512,256]{3,2,1,0:T(8,128)(2,1)}, u32[]{:S(2)}, u32[]{:S(2)}) collective-permute-start(bf16[4,3,512,256]{3,2,1,0:T(8,128)(2,1)} %weight_grads.7), channel_id=1, source_target_pairs={{0,4},{4,0},{1,5},{5,1},{2,6},{6,2},{3,7},{7,3},{8,12},{12,8},{9,1... | collective-permute-start | bytes 9437192 | tf_op jit(solution)/shard_map/ppermute | solution.py:52
  478.6 74.0 %collective-permute-start.31 = (bf16[8,320,256]{2,1,0:T(8,128)(2,1)}, bf16[8,320,256]{2,1,0:T(8,128)(2,1)S(1)}, u32[]{:S(2)}, u32[]{:S(2)}) collective-permute-start(bf16[8,320,256]{2,1,0:T(8,128)(2,1)} %combine.16), channel_id=1, source_target_pairs={{0,2},{1,3},{2,0},{3,1},{4,6},{5,7},{6,4},{7,5},{8,10},{9,11},{10,... | collective-permute-start | bytes 3932168 | tf_op jit(solution)/shard_map/ppermute | solution.py:52
  482.6 31.8 %collective-permute-start.25 = (bf16[256,640]{1,0:T(8,128)(2,1)}, bf16[256,640]{1,0:T(8,128)(2,1)S(1)}, u32[]{:S(2)}, u32[]{:S(2)}) collective-permute-start(bf16[256,640]{1,0:T(8,128)(2,1)} %get-tuple-element.216), channel_id=1, source_target_pairs={{0,1},{1,0},{2,3},{3,2},{4,5},{5,4},{6,7},{7,6},{8,9},{9,8},{10,11... | collective-permute-start | bytes 983048 | tf_op jit(solution)/shard_map/ppermute | solution.py:52
  566.3 92.1 %reduce-scatter.6.cloned.1.call-start = ((), (), s32[]{:S(2)}) async-start(), calls=%async_computation.6 | async-start | bytes 819200 | tf_op jit(solution)/shard_map/reduce_scatter | solution.py:1323
  575.0 20.6 %collective-permute-start.35 = (bf16[480,256]{1,0:T(8,128)(2,1)}, bf16[480,256]{1,0:T(8,128)(2,1)S(1)}, u32[]{:S(2)}, u32[]{:S(2)}) collective-permute-start(bf16[480,256]{1,0:T(8,128)(2,1)} %get-tuple-element.238), channel_id=1, source_target_pairs={{0,2},{1,3},{2,0},{3,1},{4,6},{5,7},{6,4},{7,5},{8,10},{9,11},{10,... | collective-permute-start | bytes 737288 | tf_op jit(solution)/shard_map/ppermute | solution.py:52
  576.5 19.8 %collective-permute-start.37 = (bf16[480,256]{1,0:T(8,128)(2,1)}, bf16[480,256]{1,0:T(8,128)(2,1)S(1)}, u32[]{:S(2)}, u32[]{:S(2)}) collective-permute-start(bf16[480,256]{1,0:T(8,128)(2,1)} %get-tuple-element.240), channel_id=1, source_target_pairs={{0,3},{1,2},{2,1},{3,0},{4,7},{5,6},{6,5},{7,4},{8,11},{9,10},{10,... | collective-permute-start | bytes 737288 | tf_op jit(solution)/shard_map/ppermute | solution.py:52
  576.6 21.3 %collective-permute-start.34 = (bf16[480,256]{1,0:T(8,128)(2,1)}, bf16[480,256]{1,0:T(8,128)(2,1)S(1)}, u32[]{:S(2)}, u32[]{:S(2)}) collective-permute-start(bf16[480,256]{1,0:T(8,128)(2,1)} %get-tuple-element.237), channel_id=1, source_target_pairs={{0,1},{1,0},{2,3},{3,2},{4,5},{5,4},{6,7},{7,6},{8,9},{9,8},{10,11... | collective-permute-start | bytes 737288 | tf_op jit(solution)/shard_map/ppermute | solution.py:52
  577.2 20.7 %collective-permute-start.36 = (bf16[480,256]{1,0:T(8,128)(2,1)}, bf16[480,256]{1,0:T(8,128)(2,1)S(1)}, u32[]{:S(2)}, u32[]{:S(2)}) collective-permute-start(bf16[480,256]{1,0:T(8,128)(2,1)} %get-tuple-element.239), channel_id=1, source_target_pairs={{0,2},{1,3},{2,0},{3,1},{4,6},{5,7},{6,4},{7,5},{8,10},{9,11},{10,... | collective-permute-start | bytes 737288 | tf_op jit(solution)/shard_map/ppermute | solution.py:52
  578.7 21.1 %collective-permute-start.38 = (bf16[480,256]{1,0:T(8,128)(2,1)}, bf16[480,256]{1,0:T(8,128)(2,1)S(1)}, u32[]{:S(2)}, u32[]{:S(2)}) collective-permute-start(bf16[480,256]{1,0:T(8,128)(2,1)} %get-tuple-element.241), channel_id=1, source_target_pairs={{0,3},{1,2},{2,1},{3,0},{4,7},{5,6},{6,5},{7,4},{8,11},{9,10},{10,... | collective-permute-start | bytes 737288 | tf_op jit(solution)/shard_map/ppermute | solution.py:52
  607.5 52.6 %collective-permute-start.42 = (bf16[512,2048]{1,0:T(8,128)(2,1)S(1)}, bf16[512,2048]{1,0:T(8,128)(2,1)}, u32[]{:S(2)}, u32[]{:S(2)}) collective-permute-start(bf16[512,2048]{1,0:T(8,128)(2,1)S(1)} %copy-done.9), channel_id=1, source_target_pairs={{0,2},{1,3},{2,0},{3,1},{4,6},{5,7},{6,4},{7,5},{8,10},{9,11},{10,... | collective-permute-start | bytes 6291464 | tf_op jit(solution)/shard_map/ppermute | solution.py:52
  608.3 28.1 %collective-permute-start.46 = (bf16[4,1,480,256]{3,2,1,0:T(8,128)(2,1)}, bf16[4,1,480,256]{3,2,1,0:T(8,128)(2,1)S(1)}, u32[]{:S(2)}, u32[]{:S(2)}) collective-permute-start(bf16[4,1,480,256]{3,2,1,0:T(8,128)(2,1)} %weight_grads.10), channel_id=1, source_target_pairs={{0,4},{4,0},{1,5},{5,1},{2,6},{6,2},{3,7},{7,3},{8,12},{12,8},{9,1... | collective-permute-start | bytes 2949128 | tf_op jit(solution)/shard_map/ppermute | solution.py:52
  653.3 20.5 %collective-permute-start.49 = (bf16[1,480,256]{2,1,0:T(8,128)(2,1)}, bf16[1,480,256]{2,1,0:T(8,128)(2,1)S(1)}, u32[]{:S(2)}, u32[]{:S(2)}) collective-permute-start(bf16[1,480,256]{2,1,0:T(8,128)(2,1)} %get-tuple-element.254), channel_id=1, source_target_pairs={{0,16},{8,24},{16,0},{24,8},{1,17},{9,25},{17,1},{25,9},{2,18},{10... | collective-permute-start | bytes 737288 | tf_op jit(solution)/shard_map/ppermute | solution.py:52
  (75 other events, 761.5 us)
Sparse Core Ops, SparseCore 0:
  10.2 54.6 all-gather.8
  67.8 136.5 all-gather.4
  206.6 97.2 all-gather.6
  477.6 83.3 reduce-scatter.3
  566.4 59.2 reduce-scatter.7
  627.8 22.7 reduce-scatter.5
